TPU v7x, 32 devices: a whole 2x2x4 slice. The times are simulated.
32 devices in a mesh: segment: 2 (over x), seq: 16 (over z, y, core).
Axes of the slice: x: 2, y: 2, z: 4, core: 2. Of those that a mesh axis runs over, the one named last changes fastest.
Arguments:
- queries: bfloat16 [2, 1024, 1536], P('segment', 'seq'), may hold values from -10 to 10
- key_value: bfloat16 [2, 2, 1024, 1536], P(None, 'segment', 'seq'), may hold values from -10 to 10
Outputs:
- handed: bfloat16 [2, 1024, 1536], P('segment', 'seq')
All inputs are finite; a program needn't handle non-finite values.
Results may differ from a plain program's by a relative error of at most 0.0065.
Values may be sent and summed in bfloat16 or wider, within the bound.
No kernel may reach another device: no remote copies, remote signals or barrier semaphores. Data moves between devices by JAX's collectives and lax.ppermute only.
A program may use at most 64 MiB of HBM per device.

v0:
```python
import jax
import jax.numpy as jnp
from jax import lax
from jax.sharding import PartitionSpec as P

HD = 128


def from_behind(value, axis, steps):
    count = lax.axis_size(axis)
    pairs = [(source, (source + steps) % count) for source in range(count)]
    return lax.ppermute(value, axis, pairs)


def attend(running, query_heads, kv_block):
    top_score, weight_sum, accumulated = running
    head_count = query_heads.shape[1]
    key_heads = kv_block[0].reshape(-1, head_count, HD)
    value_heads = kv_block[1].reshape(-1, head_count, HD)
    scores = jnp.einsum(
        "qhd,khd->qhk", query_heads, key_heads, preferred_element_type=jnp.float32
    ) * HD ** (-0.5)
    new_top = jnp.maximum(top_score, jnp.max(scores, axis=-1))
    factor = jnp.exp(top_score - new_top)
    weights = jnp.exp(scores - new_top[..., None])
    weight_sum = weight_sum * factor + jnp.sum(weights, axis=-1)
    rounded = weights.astype(jnp.bfloat16)
    accumulated = accumulated * factor[..., None] + jnp.einsum(
        "qhk,khd->qhd", rounded, value_heads, preferred_element_type=jnp.float32
    )
    return (new_top, weight_sum, accumulated)


def shards(queries, key_value):
    row_count = queries.shape[1]
    full_width = queries.shape[2]
    head_count = full_width // HD
    query_heads = queries.reshape(row_count, head_count, HD)
    holders = min(32, lax.axis_size("seq"))
    hop_distance = lax.axis_size("seq") // holders
    running = (
        jnp.full((row_count, head_count), -jnp.inf, jnp.float32),
        jnp.zeros((row_count, head_count), jnp.float32),
        jnp.zeros((row_count, head_count, HD), jnp.float32),
    )
    running = attend(running, query_heads, key_value)

    def one_hop(turn_index, loop_carry):
        current, kv_block = loop_carry
        kv_block = from_behind(kv_block, "seq", hop_distance)
        return (attend(current, query_heads, kv_block), kv_block)

    running, kv_block = lax.fori_loop(0, holders - 1, one_hop, (running, key_value))
    top_score, weight_sum, accumulated = running
    result = (
        (accumulated / weight_sum[..., None]).reshape(1, row_count, full_width).astype(jnp.bfloat16)
    )
    return from_behind(result, "segment", 1)


def solution(mesh):
    return jax.shard_map(
        shards,
        mesh=mesh,
        in_specs=(P("segment", "seq", None), P(None, "segment", "seq", None)),
        out_specs=P("segment", "seq", None),
        check_vma=False,
    )
```

profile of v0, /device:TPU:0, one launch (start us, length us, event | category | flops | bytes accessed | tf_op | source)
XLA Modules:
  0.0 177.1 jit_solution(18141472771233260422)
XLA Ops:
  0.0 1.0 copy.51
  1.0 0.1 reshape_squeeze.6
  1.2 0.8 copy-done
  2.2 0.2 fusion.20
  2.5 0.1 reshape_squeeze.7
  2.7 0.3 fusion.8
  3.0 167.2 %while.16 = (s32[]{:T(128)}, f32[64,12]{0,1:T(8,128)S(1)}, f32[64,12]{0,1:T(8,128)S(1)}, f32[64,12,128]{2,0,1:T(8,128)S(1)}, bf16[2,1,64,1536]{3,2,1,0:T(8,128)(...) while((s32[]{:T(128)}, f32[64,12]{0,1:T(8,128)S(1)}, f32[64,12]{0,1:T(8,128)S(1)}, ...), condition=%wide.region_5.0_spmd, body=%wide.region_2.0_spmd.sunk | while | flops 25658880 | bytes 5947509 | solution.py:53
  3.0 0.5 collective-permute-start
  3.5 10.5 %collective-permute-done = bf16[2,1,64,1536]{3,2,1,0:T(8,128)(2,1)S(1)} collective-permute-done((bf16[2,1,64,1536]{3,2,1,0:T(8,128)(2,1)S(1)}, bf16[2,1,64,1536]{3,2,1,0:T(8,128)(2,1)S(1)}, u32[]{:S(2)}, u32[]{:S(2)}) %collective-permute-start) | collective-permute-done | bytes 393248 | tf_op jit(solution)/shard_map/while/body/eval_jaxpr/ppermute | solution.py:12
  14.0 0.1 squeeze.8
  14.1 0.1 squeeze.9
  14.3 0.2 fusion.34
  14.7 0.3 fusion.36
  15.1 9.9 %collective-permute-done = bf16[2,1,64,1536]{3,2,1,0:T(8,128)(2,1)S(1)} collective-permute-done((bf16[2,1,64,1536]{3,2,1,0:T(8,128)(2,1)S(1)}, bf16[2,1,64,1536]{3,2,1,0:T(8,128)(2,1)S(1)}, u32[]{:S(2)}, u32[]{:S(2)}) %collective-permute-start) | collective-permute-done | bytes 393248 | tf_op jit(solution)/shard_map/while/body/eval_jaxpr/ppermute | solution.py:12
  25.1 0.1 squeeze.8
  25.2 0.1 squeeze.9
  25.4 0.2 fusion.34
  25.8 0.3 fusion.36
  26.2 9.9 %collective-permute-done = bf16[2,1,64,1536]{3,2,1,0:T(8,128)(2,1)S(1)} collective-permute-done((bf16[2,1,64,1536]{3,2,1,0:T(8,128)(2,1)S(1)}, bf16[2,1,64,1536]{3,2,1,0:T(8,128)(2,1)S(1)}, u32[]{:S(2)}, u32[]{:S(2)}) %collective-permute-start) | collective-permute-done | bytes 393248 | tf_op jit(solution)/shard_map/while/body/eval_jaxpr/ppermute | solution.py:12
  36.1 0.1 squeeze.8
  36.3 0.1 squeeze.9
  36.4 0.2 fusion.34
  36.8 0.3 fusion.36
  37.3 9.9 %collective-permute-done = bf16[2,1,64,1536]{3,2,1,0:T(8,128)(2,1)S(1)} collective-permute-done((bf16[2,1,64,1536]{3,2,1,0:T(8,128)(2,1)S(1)}, bf16[2,1,64,1536]{3,2,1,0:T(8,128)(2,1)S(1)}, u32[]{:S(2)}, u32[]{:S(2)}) %collective-permute-start) | collective-permute-done | bytes 393248 | tf_op jit(solution)/shard_map/while/body/eval_jaxpr/ppermute | solution.py:12
  47.2 0.1 squeeze.8
  47.5 0.2 fusion.34
  47.9 0.3 fusion.36
  48.4 9.9 %collective-permute-done = bf16[2,1,64,1536]{3,2,1,0:T(8,128)(2,1)S(1)} collective-permute-done((bf16[2,1,64,1536]{3,2,1,0:T(8,128)(2,1)S(1)}, bf16[2,1,64,1536]{3,2,1,0:T(8,128)(2,1)S(1)}, u32[]{:S(2)}, u32[]{:S(2)}) %collective-permute-start) | collective-permute-done | bytes 393248 | tf_op jit(solution)/shard_map/while/body/eval_jaxpr/ppermute | solution.py:12
  58.6 0.2 fusion.34
  59.0 0.3 fusion.36
  59.5 9.9 %collective-permute-done = bf16[2,1,64,1536]{3,2,1,0:T(8,128)(2,1)S(1)} collective-permute-done((bf16[2,1,64,1536]{3,2,1,0:T(8,128)(2,1)S(1)}, bf16[2,1,64,1536]{3,2,1,0:T(8,128)(2,1)S(1)}, u32[]{:S(2)}, u32[]{:S(2)}) %collective-permute-start) | collective-permute-done | bytes 393248 | tf_op jit(solution)/shard_map/while/body/eval_jaxpr/ppermute | solution.py:12
  69.7 0.2 fusion.34
  70.1 0.3 fusion.36
  70.5 9.9 %collective-permute-done = bf16[2,1,64,1536]{3,2,1,0:T(8,128)(2,1)S(1)} collective-permute-done((bf16[2,1,64,1536]{3,2,1,0:T(8,128)(2,1)S(1)}, bf16[2,1,64,1536]{3,2,1,0:T(8,128)(2,1)S(1)}, u32[]{:S(2)}, u32[]{:S(2)}) %collective-permute-start) | collective-permute-done | bytes 393248 | tf_op jit(solution)/shard_map/while/body/eval_jaxpr/ppermute | solution.py:12
  80.8 0.2 fusion.34
  81.2 0.3 fusion.36
  81.6 9.9 %collective-permute-done = bf16[2,1,64,1536]{3,2,1,0:T(8,128)(2,1)S(1)} collective-permute-done((bf16[2,1,64,1536]{3,2,1,0:T(8,128)(2,1)S(1)}, bf16[2,1,64,1536]{3,2,1,0:T(8,128)(2,1)S(1)}, u32[]{:S(2)}, u32[]{:S(2)}) %collective-permute-start) | collective-permute-done | bytes 393248 | tf_op jit(solution)/shard_map/while/body/eval_jaxpr/ppermute | solution.py:12
  91.9 0.2 fusion.34
  92.2 0.3 fusion.36
  92.7 9.9 %collective-permute-done = bf16[2,1,64,1536]{3,2,1,0:T(8,128)(2,1)S(1)} collective-permute-done((bf16[2,1,64,1536]{3,2,1,0:T(8,128)(2,1)S(1)}, bf16[2,1,64,1536]{3,2,1,0:T(8,128)(2,1)S(1)}, u32[]{:S(2)}, u32[]{:S(2)}) %collective-permute-start) | collective-permute-done | bytes 393248 | tf_op jit(solution)/shard_map/while/body/eval_jaxpr/ppermute | solution.py:12
  102.9 0.2 fusion.34
  103.3 0.3 fusion.36
  103.8 9.9 %collective-permute-done = bf16[2,1,64,1536]{3,2,1,0:T(8,128)(2,1)S(1)} collective-permute-done((bf16[2,1,64,1536]{3,2,1,0:T(8,128)(2,1)S(1)}, bf16[2,1,64,1536]{3,2,1,0:T(8,128)(2,1)S(1)}, u32[]{:S(2)}, u32[]{:S(2)}) %collective-permute-start) | collective-permute-done | bytes 393248 | tf_op jit(solution)/shard_map/while/body/eval_jaxpr/ppermute | solution.py:12
  114.0 0.2 fusion.34
  114.4 0.3 fusion.36
  114.9 9.9 %collective-permute-done = bf16[2,1,64,1536]{3,2,1,0:T(8,128)(2,1)S(1)} collective-permute-done((bf16[2,1,64,1536]{3,2,1,0:T(8,128)(2,1)S(1)}, bf16[2,1,64,1536]{3,2,1,0:T(8,128)(2,1)S(1)}, u32[]{:S(2)}, u32[]{:S(2)}) %collective-permute-start) | collective-permute-done | bytes 393248 | tf_op jit(solution)/shard_map/while/body/eval_jaxpr/ppermute | solution.py:12
  125.1 0.2 fusion.34
  125.5 0.3 fusion.36
  126.0 9.9 %collective-permute-done = bf16[2,1,64,1536]{3,2,1,0:T(8,128)(2,1)S(1)} collective-permute-done((bf16[2,1,64,1536]{3,2,1,0:T(8,128)(2,1)S(1)}, bf16[2,1,64,1536]{3,2,1,0:T(8,128)(2,1)S(1)}, u32[]{:S(2)}, u32[]{:S(2)}) %collective-permute-start) | collective-permute-done | bytes 393248 | tf_op jit(solution)/shard_map/while/body/eval_jaxpr/ppermute | solution.py:12
  136.2 0.2 fusion.34
  136.6 0.3 fusion.36
  137.0 9.9 %collective-permute-done = bf16[2,1,64,1536]{3,2,1,0:T(8,128)(2,1)S(1)} collective-permute-done((bf16[2,1,64,1536]{3,2,1,0:T(8,128)(2,1)S(1)}, bf16[2,1,64,1536]{3,2,1,0:T(8,128)(2,1)S(1)}, u32[]{:S(2)}, u32[]{:S(2)}) %collective-permute-start) | collective-permute-done | bytes 393248 | tf_op jit(solution)/shard_map/while/body/eval_jaxpr/ppermute | solution.py:12
  147.3 0.2 fusion.34
  147.7 0.3 fusion.36
  148.1 9.9 %collective-permute-done = bf16[2,1,64,1536]{3,2,1,0:T(8,128)(2,1)S(1)} collective-permute-done((bf16[2,1,64,1536]{3,2,1,0:T(8,128)(2,1)S(1)}, bf16[2,1,64,1536]{3,2,1,0:T(8,128)(2,1)S(1)}, u32[]{:S(2)}, u32[]{:S(2)}) %collective-permute-start) | collective-permute-done | bytes 393248 | tf_op jit(solution)/shard_map/while/body/eval_jaxpr/ppermute | solution.py:12
  158.4 0.2 fusion.34
  158.7 0.3 fusion.36
  159.2 9.9 %collective-permute-done = bf16[2,1,64,1536]{3,2,1,0:T(8,128)(2,1)S(1)} collective-permute-done((bf16[2,1,64,1536]{3,2,1,0:T(8,128)(2,1)S(1)}, bf16[2,1,64,1536]{3,2,1,0:T(8,128)(2,1)S(1)}, u32[]{:S(2)}, u32[]{:S(2)}) %collective-permute-start) | collective-permute-done | bytes 393248 | tf_op jit(solution)/shard_map/while/body/eval_jaxpr/ppermute | solution.py:12
  169.4 0.2 fusion.34
  169.8 0.3 fusion.36
  170.2 0.2 divide_convert_fusion
  170.7 2.0 %collective-permute-start.1 = (bf16[1,64,1536]{2,1,0:T(8,128)(2,1)S(1)}, bf16[1,64,1536]{2,1,0:T(8,128)(2,1)S(1)}, u32[]{:S(2)}, u32[]{:S(2)}) collective-permute-start(bf16[1,64,1536]{2,1,0:T(8,128)(2,1)S(1)} %convert_element_type.22), channel_id=1, source_target_pairs={{0,16},{16,0},{1,17},{17,1},{2,18},{18,2},{3,19},{19,3},{4,20},{20... | collective-permute-start | bytes 589832 | tf_op jit(solution)/shard_map/ppermute | solution.py:12
  172.7 3.7 %collective-permute-done.1 = bf16[1,64,1536]{2,1,0:T(8,128)(2,1)S(1)} collective-permute-done((bf16[1,64,1536]{2,1,0:T(8,128)(2,1)S(1)}, bf16[1,64,1536]{2,1,0:T(8,128)(2,1)S(1)}, u32[]{:S(2)}, u32[]{:S(2)}) %collective-permute-start.1) | collective-permute-done | bytes 196640 | tf_op jit(solution)/shard_map/ppermute | solution.py:12
  176.4 0.7 copy.53
  (135 shorter events, 7.2 us)
Async XLA Ops:
  1.0 0.9 copy-start
  3.0 11.0 %collective-permute-start = (bf16[2,1,64,1536]{3,2,1,0:T(8,128)(2,1)S(1)}, bf16[2,1,64,1536]{3,2,1,0:T(8,128)(2,1)S(1)}, u32[]{:S(2)}, u32[]{:S(2)}) collective-permute-start(bf16[2,1,64,1536]{3,2,1,0:T(8,128)(2,1)S(1)} %get-tuple-element.130), channel_id=1, source_target_pairs={{0,1},{1,2},{2,3},{3,4},{4,5},{5,6},{6,7},{7,8},{8,9},{9,10},{10,1... | collective-permute-start | bytes 1179656 | tf_op jit(solution)/shard_map/while/body/eval_jaxpr/ppermute | solution.py:12
  15.1 10.0 %collective-permute-start = (bf16[2,1,64,1536]{3,2,1,0:T(8,128)(2,1)S(1)}, bf16[2,1,64,1536]{3,2,1,0:T(8,128)(2,1)S(1)}, u32[]{:S(2)}, u32[]{:S(2)}) collective-permute-start(bf16[2,1,64,1536]{3,2,1,0:T(8,128)(2,1)S(1)} %get-tuple-element.130), channel_id=1, source_target_pairs={{0,1},{1,2},{2,3},{3,4},{4,5},{5,6},{6,7},{7,8},{8,9},{9,10},{10,1... | collective-permute-start | bytes 1179656 | tf_op jit(solution)/shard_map/while/body/eval_jaxpr/ppermute | solution.py:12
  26.2 10.0 %collective-permute-start = (bf16[2,1,64,1536]{3,2,1,0:T(8,128)(2,1)S(1)}, bf16[2,1,64,1536]{3,2,1,0:T(8,128)(2,1)S(1)}, u32[]{:S(2)}, u32[]{:S(2)}) collective-permute-start(bf16[2,1,64,1536]{3,2,1,0:T(8,128)(2,1)S(1)} %get-tuple-element.130), channel_id=1, source_target_pairs={{0,1},{1,2},{2,3},{3,4},{4,5},{5,6},{6,7},{7,8},{8,9},{9,10},{10,1... | collective-permute-start | bytes 1179656 | tf_op jit(solution)/shard_map/while/body/eval_jaxpr/ppermute | solution.py:12
  37.2 10.0 %collective-permute-start = (bf16[2,1,64,1536]{3,2,1,0:T(8,128)(2,1)S(1)}, bf16[2,1,64,1536]{3,2,1,0:T(8,128)(2,1)S(1)}, u32[]{:S(2)}, u32[]{:S(2)}) collective-permute-start(bf16[2,1,64,1536]{3,2,1,0:T(8,128)(2,1)S(1)} %get-tuple-element.130), channel_id=1, source_target_pairs={{0,1},{1,2},{2,3},{3,4},{4,5},{5,6},{6,7},{7,8},{8,9},{9,10},{10,1... | collective-permute-start | bytes 1179656 | tf_op jit(solution)/shard_map/while/body/eval_jaxpr/ppermute | solution.py:12
  48.3 10.0 %collective-permute-start = (bf16[2,1,64,1536]{3,2,1,0:T(8,128)(2,1)S(1)}, bf16[2,1,64,1536]{3,2,1,0:T(8,128)(2,1)S(1)}, u32[]{:S(2)}, u32[]{:S(2)}) collective-permute-start(bf16[2,1,64,1536]{3,2,1,0:T(8,128)(2,1)S(1)} %get-tuple-element.130), channel_id=1, source_target_pairs={{0,1},{1,2},{2,3},{3,4},{4,5},{5,6},{6,7},{7,8},{8,9},{9,10},{10,1... | collective-permute-start | bytes 1179656 | tf_op jit(solution)/shard_map/while/body/eval_jaxpr/ppermute | solution.py:12
  59.4 10.0 %collective-permute-start = (bf16[2,1,64,1536]{3,2,1,0:T(8,128)(2,1)S(1)}, bf16[2,1,64,1536]{3,2,1,0:T(8,128)(2,1)S(1)}, u32[]{:S(2)}, u32[]{:S(2)}) collective-permute-start(bf16[2,1,64,1536]{3,2,1,0:T(8,128)(2,1)S(1)} %get-tuple-element.130), channel_id=1, source_target_pairs={{0,1},{1,2},{2,3},{3,4},{4,5},{5,6},{6,7},{7,8},{8,9},{9,10},{10,1... | collective-permute-start | bytes 1179656 | tf_op jit(solution)/shard_map/while/body/eval_jaxpr/ppermute | solution.py:12
  70.5 10.0 %collective-permute-start = (bf16[2,1,64,1536]{3,2,1,0:T(8,128)(2,1)S(1)}, bf16[2,1,64,1536]{3,2,1,0:T(8,128)(2,1)S(1)}, u32[]{:S(2)}, u32[]{:S(2)}) collective-permute-start(bf16[2,1,64,1536]{3,2,1,0:T(8,128)(2,1)S(1)} %get-tuple-element.130), channel_id=1, source_target_pairs={{0,1},{1,2},{2,3},{3,4},{4,5},{5,6},{6,7},{7,8},{8,9},{9,10},{10,1... | collective-permute-start | bytes 1179656 | tf_op jit(solution)/shard_map/while/body/eval_jaxpr/ppermute | solution.py:12
  81.6 10.0 %collective-permute-start = (bf16[2,1,64,1536]{3,2,1,0:T(8,128)(2,1)S(1)}, bf16[2,1,64,1536]{3,2,1,0:T(8,128)(2,1)S(1)}, u32[]{:S(2)}, u32[]{:S(2)}) collective-permute-start(bf16[2,1,64,1536]{3,2,1,0:T(8,128)(2,1)S(1)} %get-tuple-element.130), channel_id=1, source_target_pairs={{0,1},{1,2},{2,3},{3,4},{4,5},{5,6},{6,7},{7,8},{8,9},{9,10},{10,1... | collective-permute-start | bytes 1179656 | tf_op jit(solution)/shard_map/while/body/eval_jaxpr/ppermute | solution.py:12
  92.6 10.0 %collective-permute-start = (bf16[2,1,64,1536]{3,2,1,0:T(8,128)(2,1)S(1)}, bf16[2,1,64,1536]{3,2,1,0:T(8,128)(2,1)S(1)}, u32[]{:S(2)}, u32[]{:S(2)}) collective-permute-start(bf16[2,1,64,1536]{3,2,1,0:T(8,128)(2,1)S(1)} %get-tuple-element.130), channel_id=1, source_target_pairs={{0,1},{1,2},{2,3},{3,4},{4,5},{5,6},{6,7},{7,8},{8,9},{9,10},{10,1... | collective-permute-start | bytes 1179656 | tf_op jit(solution)/shard_map/while/body/eval_jaxpr/ppermute | solution.py:12
  103.7 10.0 %collective-permute-start = (bf16[2,1,64,1536]{3,2,1,0:T(8,128)(2,1)S(1)}, bf16[2,1,64,1536]{3,2,1,0:T(8,128)(2,1)S(1)}, u32[]{:S(2)}, u32[]{:S(2)}) collective-permute-start(bf16[2,1,64,1536]{3,2,1,0:T(8,128)(2,1)S(1)} %get-tuple-element.130), channel_id=1, source_target_pairs={{0,1},{1,2},{2,3},{3,4},{4,5},{5,6},{6,7},{7,8},{8,9},{9,10},{10,1... | collective-permute-start | bytes 1179656 | tf_op jit(solution)/shard_map/while/body/eval_jaxpr/ppermute | solution.py:12
  114.8 10.0 %collective-permute-start = (bf16[2,1,64,1536]{3,2,1,0:T(8,128)(2,1)S(1)}, bf16[2,1,64,1536]{3,2,1,0:T(8,128)(2,1)S(1)}, u32[]{:S(2)}, u32[]{:S(2)}) collective-permute-start(bf16[2,1,64,1536]{3,2,1,0:T(8,128)(2,1)S(1)} %get-tuple-element.130), channel_id=1, source_target_pairs={{0,1},{1,2},{2,3},{3,4},{4,5},{5,6},{6,7},{7,8},{8,9},{9,10},{10,1... | collective-permute-start | bytes 1179656 | tf_op jit(solution)/shard_map/while/body/eval_jaxpr/ppermute | solution.py:12
  125.9 10.0 %collective-permute-start = (bf16[2,1,64,1536]{3,2,1,0:T(8,128)(2,1)S(1)}, bf16[2,1,64,1536]{3,2,1,0:T(8,128)(2,1)S(1)}, u32[]{:S(2)}, u32[]{:S(2)}) collective-permute-start(bf16[2,1,64,1536]{3,2,1,0:T(8,128)(2,1)S(1)} %get-tuple-element.130), channel_id=1, source_target_pairs={{0,1},{1,2},{2,3},{3,4},{4,5},{5,6},{6,7},{7,8},{8,9},{9,10},{10,1... | collective-permute-start | bytes 1179656 | tf_op jit(solution)/shard_map/while/body/eval_jaxpr/ppermute | solution.py:12
  137.0 10.0 %collective-permute-start = (bf16[2,1,64,1536]{3,2,1,0:T(8,128)(2,1)S(1)}, bf16[2,1,64,1536]{3,2,1,0:T(8,128)(2,1)S(1)}, u32[]{:S(2)}, u32[]{:S(2)}) collective-permute-start(bf16[2,1,64,1536]{3,2,1,0:T(8,128)(2,1)S(1)} %get-tuple-element.130), channel_id=1, source_target_pairs={{0,1},{1,2},{2,3},{3,4},{4,5},{5,6},{6,7},{7,8},{8,9},{9,10},{10,1... | collective-permute-start | bytes 1179656 | tf_op jit(solution)/shard_map/while/body/eval_jaxpr/ppermute | solution.py:12
  148.1 10.0 %collective-permute-start = (bf16[2,1,64,1536]{3,2,1,0:T(8,128)(2,1)S(1)}, bf16[2,1,64,1536]{3,2,1,0:T(8,128)(2,1)S(1)}, u32[]{:S(2)}, u32[]{:S(2)}) collective-permute-start(bf16[2,1,64,1536]{3,2,1,0:T(8,128)(2,1)S(1)} %get-tuple-element.130), channel_id=1, source_target_pairs={{0,1},{1,2},{2,3},{3,4},{4,5},{5,6},{6,7},{7,8},{8,9},{9,10},{10,1... | collective-permute-start | bytes 1179656 | tf_op jit(solution)/shard_map/while/body/eval_jaxpr/ppermute | solution.py:12
  159.1 10.0 %collective-permute-start = (bf16[2,1,64,1536]{3,2,1,0:T(8,128)(2,1)S(1)}, bf16[2,1,64,1536]{3,2,1,0:T(8,128)(2,1)S(1)}, u32[]{:S(2)}, u32[]{:S(2)}) collective-permute-start(bf16[2,1,64,1536]{3,2,1,0:T(8,128)(2,1)S(1)} %get-tuple-element.130), channel_id=1, source_target_pairs={{0,1},{1,2},{2,3},{3,4},{4,5},{5,6},{6,7},{7,8},{8,9},{9,10},{10,1... | collective-permute-start | bytes 1179656 | tf_op jit(solution)/shard_map/while/body/eval_jaxpr/ppermute | solution.py:12
  170.7 5.7 %collective-permute-start.1 = (bf16[1,64,1536]{2,1,0:T(8,128)(2,1)S(1)}, bf16[1,64,1536]{2,1,0:T(8,128)(2,1)S(1)}, u32[]{:S(2)}, u32[]{:S(2)}) collective-permute-start(bf16[1,64,1536]{2,1,0:T(8,128)(2,1)S(1)} %convert_element_type.22), channel_id=1, source_target_pairs={{0,16},{16,0},{1,17},{17,1},{2,18},{18,2},{3,19},{19,3},{4,20},{20... | collective-permute-start | bytes 589832 | tf_op jit(solution)/shard_map/ppermute | solution.py:12
where the time goes:
time: 177 us
  waiting for transfers between devices  153 us (86%)
  matrix products  9.37 us (5%)
  local copies, waits for them, and re-layouts  8.59 us (5%)
  starting transfers between devices  3.31 us (2%)
  other arithmetic  1.79 us (1%)
    ppermute x16, waiting for transfers between devices, from_behind(): return lax.ppermute(value, axis, pairs)  153 us
    dot_general x16, matrix products, attend(): jnp.einsum('qhk,khd->qhd', rounded, value_heads, preferred_element_type=j...  5.4 us
    dot_general x16, matrix products, attend(): jnp.einsum('qhd,khd->qhk', query_heads, key_heads, preferred_element_type...  3.97 us
  transfers between devices with their start and end apart: 16, of which 16 were waited for; matrix products, arithmetic and copies ran while one was open for 0% of the time, Pallas kernels for 0%

commit v1 on v0

v1 whole, which is shorter than its diff:
```python
import functools

import jax
import jax.numpy as jnp
from jax import lax
from jax.experimental import pallas as pl
from jax.experimental.pallas import tpu as pltpu
from jax.sharding import PartitionSpec as P

HD = 128
ANY = pl.BlockSpec(memory_space=pl.ANY)
VMEM = pl.BlockSpec(memory_space=pltpu.VMEM)


def group_count(heads, places):
    count = 1
    while heads % (2 * count) == 0 and places % (2 * count) == 0:
        count *= 2
    return count


def split_heads(queries, key_value, groups, inner):
    rows, full = queries.shape[1:]
    width = full // groups

    def kernel(q_ref, kv_ref, *rest):
        outs, sem = rest[:-1], rest[-1]
        mine = lax.axis_index("seq") // inner
        copies = []
        for which in range(3):
            source = q_ref.at[0] if which == 2 else kv_ref.at[which, 0]
            for step in range(groups):
                start = pl.multiple_of((mine ^ step) * width, 128)
                copies.append(
                    pltpu.make_async_copy(
                        source.at[:, pl.ds(start, width)],
                        outs[which * groups + step],
                        sem.at[which * groups + step],
                    )
                )
        for copy in copies:
            copy.start()
        for copy in copies:
            copy.wait()

    pieces = pl.pallas_call(
        kernel,
        out_shape=[jax.ShapeDtypeStruct((rows, width), queries.dtype)] * (3 * groups),
        in_specs=[ANY, ANY],
        out_specs=[VMEM] * (3 * groups),
        scratch_shapes=[pltpu.SemaphoreType.DMA((3 * groups,))],
        name="split_heads",
    )(queries, key_value)
    return pieces[:groups], pieces[groups : 2 * groups], pieces[2 * groups :]


def attend(query_pieces, key_blocks, value_blocks):
    groups = len(query_pieces)
    blocks = len(key_blocks)
    rows, width = query_pieces[0].shape
    contract = (((1,), (1,)), ((), ()))

    def kernel(*refs):
        q_refs = refs[:groups]
        k_refs = refs[groups : groups + blocks]
        v_refs = refs[groups + blocks : groups + 2 * blocks]
        out_refs = refs[groups + 2 * blocks :]
        for head in range(width // HD):
            cols = slice(head * HD, (head + 1) * HD)
            q = jnp.concatenate([ref[:, cols] for ref in q_refs], axis=0)
            scores = [
                lax.dot_general(
                    q, ref[:, cols], contract, preferred_element_type=jnp.float32
                )
                * HD ** (-0.5)
                for ref in k_refs
            ]
            top = functools.reduce(
                jnp.maximum, [jnp.max(s, axis=1, keepdims=True) for s in scores]
            )
            total = 0.0
            acc = 0.0
            for s, ref in zip(scores, v_refs):
                weights = jnp.exp(s - top)
                total = total + jnp.sum(weights, axis=1, keepdims=True)
                acc = acc + jnp.dot(
                    weights.astype(jnp.bfloat16),
                    ref[:, cols],
                    preferred_element_type=jnp.float32,
                )
            out = (acc / total).astype(jnp.bfloat16)
            for step, ref in enumerate(out_refs):
                ref[:, cols] = out[step * rows : (step + 1) * rows]

    return pl.pallas_call(
        kernel,
        out_shape=[jax.ShapeDtypeStruct((rows, width), jnp.bfloat16)] * groups,
        in_specs=[VMEM] * (groups + 2 * blocks),
        out_specs=[VMEM] * groups,
        name="attend",
    )(*query_pieces, *key_blocks, *value_blocks)


def join_heads(pieces, inner):
    groups = len(pieces)
    rows, width = pieces[0].shape

    def kernel(*refs):
        out_ref, sem = refs[groups:]
        mine = lax.axis_index("seq") // inner
        copies = [
            pltpu.make_async_copy(
                refs[step],
                out_ref.at[0, :, pl.ds(pl.multiple_of((mine ^ step) * width, 128), width)],
                sem.at[step],
            )
            for step in range(groups)
        ]
        for copy in copies:
            copy.start()
        for copy in copies:
            copy.wait()

    return pl.pallas_call(
        kernel,
        out_shape=jax.ShapeDtypeStruct((1, rows, groups * width), jnp.bfloat16),
        in_specs=[VMEM] * groups,
        out_specs=ANY,
        scratch_shapes=[pltpu.SemaphoreType.DMA((groups,))],
        name="join_heads",
    )(*pieces)


def shards(queries, key_value):
    places = lax.axis_size("seq")
    segments = lax.axis_size("segment")
    heads = queries.shape[2] // HD
    groups = group_count(heads, places)
    inner = places // groups

    def swap(value, bits):
        return lax.ppermute(value, "seq", [(i, i ^ bits) for i in range(places)])

    def exchange(pieces):
        far = [swap(pieces[s], s * inner) for s in range(groups - 1, 0, -1)]
        return [pieces[0]] + far[::-1]

    def gather(pieces):
        blocks = [jnp.concatenate(exchange(pieces), axis=0)]
        bits = inner // 2
        while bits:
            blocks = blocks + [swap(block, bits) for block in blocks]
            bits //= 2
        return blocks

    keys, values, query_pieces = split_heads(queries, key_value, groups, inner)
    key_blocks = gather(keys)
    value_blocks = gather(values)
    query_pieces = exchange(query_pieces)
    attended = attend(query_pieces, key_blocks, value_blocks)

    def hand(value, step):
        pairs = [
            (
                segment * places + i,
                ((segment + 1) % segments) * places + (i ^ (step * inner)),
            )
            for segment in range(segments)
            for i in range(places)
        ]
        return lax.ppermute(value, ("segment", "seq"), pairs)

    handed = [hand(attended[s], s) for s in range(groups - 1, -1, -1)][::-1]
    return join_heads(handed, inner)


def solution(mesh):
    return jax.shard_map(
        shards,
        mesh=mesh,
        in_specs=(P("segment", "seq", None), P(None, "segment", "seq", None)),
        out_specs=P("segment", "seq", None),
        check_vma=False,
    )
```

time: 177 us -> 62.4 us (0.35)
  waiting for transfers between devices: 153 us -> 26.9 us
  starting transfers between devices: 3.31 us -> 24.4 us
  matrix products: 9.37 us -> 0 us
  Pallas kernels: 0 us -> 7.34 us
  local copies, waits for them, and re-layouts: 8.59 us -> 3.14 us
  other arithmetic: 1.79 us -> 0 us
    ppermute x16 -> x19, waiting for transfers between devices: 153 us -> 26.9 us  [the longest x15 21.8 us: swap(): return lax.ppermute(value, 'seq', [(i, i ^ bits) for i in range(places)])]
    ppermute x16 -> x19, starting transfers between devices: 3.31 us -> 24.4 us  [the longest x15 17.7 us: swap(): return lax.ppermute(value, 'seq', [(i, i ^ bits) for i in range(places)])]
    dot_general x32 -> x0, matrix products: 9.37 us -> none  [the longest x16 5.4 us: attend(): jnp.einsum('qhk,khd->qhd', rounded, value_heads, preferred_element_type=j...]
    pallas_call x0 -> x3, Pallas kernels: none -> 7.34 us  [the longest x1 3.8 us: attend(): pl.pallas_call(kernel, out_shape=[jax.ShapeDtypeStruct((rows, width), jnp...]
    squeeze x30 -> x0, local copies, waits for them, and re-layouts: 4.5 us -> none  [the longest x15 2.25 us: attend(): key_heads = kv_block[0].reshape(-1, head_count, HD)]
  transfers between devices with their start and end apart: 16 -> 19, of which waited for: 16 -> 8; matrix products, arithmetic and copies ran while one was open for 0% -> 1% of each run, Pallas kernels for 0% -> 0%
where the time goes in v1:
time: 62.4 us; the launch traced here: 62.1 us
  waiting for transfers between devices  26.9 us (43%)
  starting transfers between devices  24.4 us (39%)
  Pallas kernels  7.34 us (12%)
  local copies, waits for them, and re-layouts  3.14 us (5%)
    ppermute x15, waiting for transfers between devices, swap(): return lax.ppermute(value, 'seq', [(i, i ^ bits) for i in range(places)])  21.8 us
    ppermute x15, starting transfers between devices, swap(): return lax.ppermute(value, 'seq', [(i, i ^ bits) for i in range(places)])  17.7 us
    ppermute x4, starting transfers between devices, hand(): return lax.ppermute(value, ('segment', 'seq'), pairs)  6.75 us
    ppermute x4, waiting for transfers between devices, hand(): return lax.ppermute(value, ('segment', 'seq'), pairs)  5.09 us
    pallas_call x1, Pallas kernels, attend(): pl.pallas_call(kernel, out_shape=[jax.ShapeDtypeStruct((rows, width), jnp...  3.8 us
    unnamed x46, local copies, waits for them, and re-layouts  3.12 us
    pallas_call x1, Pallas kernels, split_heads(): pl.pallas_call(kernel, out_shape=[jax.ShapeDtypeStruct((rows, width), que...  1.97 us
    pallas_call x1, Pallas kernels, join_heads(): pl.pallas_call(kernel, out_shape=jax.ShapeDtypeStruct((1, rows, groups *...  1.57 us
  transfers between devices with their start and end apart: 19, of which 8 were waited for; matrix products, arithmetic and copies ran while one was open for 1% of the time, Pallas kernels for 0%

profile of v1, /device:TPU:0, one launch (start us, length us, event | category | flops | bytes accessed | tf_op | source)
XLA Modules:
  0.0 62.1 jit_solution(10081572995696195786)
XLA Ops:
  0.0 2.0 %split_heads.1 = (bf16[64,384]{1,0:T(8,128)(2,1)}, bf16[64,384]{1,0:T(8,128)(2,1)}, bf16[64,384]{1,0:T(8,128)(2,1)}, bf16[64,384]{1,0:T(8,128)(2,1)}, bf16[64,38...) custom-call(bf16[1,64,1536]{2,1,0:T(8,128)(2,1)} %q_ref.1, ...), custom_call_target="tpu_custom_call" | custom-call | tf_op jit(solution)/shard_map/split_heads/pallas_call | solution.py:46
  2.0 3.1 %collective-permute-start.3 = (bf16[64,384]{1,0:T(8,128)(2,1)}, bf16[64,384]{1,0:T(8,128)(2,1)S(1)}, u32[]{:S(2)}, u32[]{:S(2)}) collective-permute-start(bf16[64,384]{1,0:T(8,128)(2,1)} %get-tuple-element.26), channel_id=1, source_target_pairs={{0,4},{1,5},{2,6},{3,7},{4,0},{5,1},{6,2},{7,3},{8,12},{9,13},{10,... | collective-permute-start | bytes 147464 | tf_op jit(solution)/shard_map/ppermute | solution.py:142
  5.1 2.6 %collective-permute-start.4 = (bf16[64,384]{1,0:T(8,128)(2,1)}, bf16[64,384]{1,0:T(8,128)(2,1)S(1)}, u32[]{:S(2)}, u32[]{:S(2)}) collective-permute-start(bf16[64,384]{1,0:T(8,128)(2,1)} %get-tuple-element.27), channel_id=1, source_target_pairs={{0,8},{1,9},{2,10},{3,11},{4,12},{5,13},{6,14},{7,15},{8,0},{9,1},... | collective-permute-start | bytes 147464 | tf_op jit(solution)/shard_map/ppermute | solution.py:142
  7.7 0.0 collective-permute-start.5
  7.7 0.9 %collective-permute-start.9 = (bf16[64,384]{1,0:T(8,128)(2,1)}, bf16[64,384]{1,0:T(8,128)(2,1)S(1)}, u32[]{:S(2)}, u32[]{:S(2)}) collective-permute-start(bf16[64,384]{1,0:T(8,128)(2,1)} %get-tuple-element.30), channel_id=1, source_target_pairs={{0,4},{1,5},{2,6},{3,7},{4,0},{5,1},{6,2},{7,3},{8,12},{9,13},{10,... | collective-permute-start | bytes 147464 | tf_op jit(solution)/shard_map/ppermute | solution.py:142
  8.6 3.5 %collective-permute-start.10 = (bf16[64,384]{1,0:T(8,128)(2,1)}, bf16[64,384]{1,0:T(8,128)(2,1)S(1)}, u32[]{:S(2)}, u32[]{:S(2)}) collective-permute-start(bf16[64,384]{1,0:T(8,128)(2,1)} %get-tuple-element.31), channel_id=1, source_target_pairs={{0,8},{1,9},{2,10},{3,11},{4,12},{5,13},{6,14},{7,15},{8,0},{9,1},... | collective-permute-start | bytes 147464 | tf_op jit(solution)/shard_map/ppermute | solution.py:142
  12.0 0.8 %constant_dynamic-update-slice_fusion.3 = bf16[256,384]{1,0:T(8,128)(2,1)S(1)} fusion(bf16[64,384]{1,0:T(8,128)(2,1)} %get-tuple-element.25), kind=kLoop, calls=%fused_computation.3 | loop fusion | bytes 98304
  12.9 0.0 copy-done.15
  12.9 0.0 collective-permute-done.9
  12.9 0.8 %copy-done.19 = bf16[64,384]{1,0:T(8,128)(2,1)S(1)} copy-done((bf16[64,384]{1,0:T(8,128)(2,1)S(1)}, bf16[64,384]{1,0:T(8,128)(2,1)}, u32[]{:S(2)}) %copy-start.19) | copy-done | bytes 49176
  13.7 2.2 %collective-permute-start.11 = (bf16[64,384]{1,0:T(8,128)(2,1)S(1)}, bf16[64,384]{1,0:T(8,128)(2,1)S(1)}, u32[]{:S(2)}, u32[]{:S(2)}) collective-permute-start(bf16[64,384]{1,0:T(8,128)(2,1)S(1)} %copy-done.19), channel_id=1, source_target_pairs={{0,12},{1,13},{2,14},{3,15},{4,8},{5,9},{6,10},{7,11},{8,4},{9,5},... | collective-permute-start | bytes 147464 | tf_op jit(solution)/shard_map/ppermute | solution.py:142
  15.9 0.0 collective-permute-done.10
  15.9 3.6 %collective-permute-done.11 = bf16[64,384]{1,0:T(8,128)(2,1)S(1)} collective-permute-done((bf16[64,384]{1,0:T(8,128)(2,1)S(1)}, bf16[64,384]{1,0:T(8,128)(2,1)S(1)}, u32[]{:S(2)}, u32[]{:S(2)}) %collective-permute-start.11) | collective-permute-done | bytes 49184 | tf_op jit(solution)/shard_map/ppermute | solution.py:142
  19.6 0.0 copy-start.1
  19.6 1.6 %collective-permute-start.12 = (bf16[256,384]{1,0:T(8,128)(2,1)S(1)}, bf16[256,384]{1,0:T(8,128)(2,1)S(1)}, u32[]{:S(2)}, u32[]{:S(2)}) collective-permute-start(bf16[256,384]{1,0:T(8,128)(2,1)S(1)} %constant_dynamic-update-slice_fusion.4.refs_8_), channel_id=1, source_target_pairs={{0,2},{1,3},{2,0},{3,1},{4,6},{5,7},{6,4},{7,5},{8,10},{9,11},{10,... | collective-permute-start | bytes 589832 | tf_op jit(solution)/shard_map/ppermute | solution.py:142
  21.2 0.0 collective-permute-done.3
  21.2 0.0 collective-permute-done.4
  21.2 0.0 copy-start.18
  21.2 0.0 copy-start.17
  21.2 0.0 copy-start.16
  21.2 0.0 collective-permute-done.5
  21.3 0.0 copy-start
  21.3 0.6 collective-permute-start.6
  21.8 0.0 collective-permute-start.13
  21.9 0.5 collective-permute-start.7
  22.4 3.5 %collective-permute-done.12.refs_9_ = bf16[256,384]{1,0:T(8,128)(2,1)S(1)} collective-permute-done((bf16[256,384]{1,0:T(8,128)(2,1)S(1)}, bf16[256,384]{1,0:T(8,128)(2,1)S(1)}, u32[]{:S(2)}, u32[]{:S(2)}) %collective-permute-start.12) | collective-permute-done | bytes 196640 | tf_op jit(solution)/shard_map/ppermute | solution.py:142
  25.9 0.0 collective-permute-start.14
  25.9 2.1 %collective-permute-done.6.refs_5_ = bf16[256,384]{1,0:T(8,128)(2,1)S(1)} collective-permute-done((bf16[256,384]{1,0:T(8,128)(2,1)S(1)}, bf16[256,384]{1,0:T(8,128)(2,1)S(1)}, u32[]{:S(2)}, u32[]{:S(2)}) %collective-permute-start.6) | collective-permute-done | bytes 196640 | tf_op jit(solution)/shard_map/ppermute | solution.py:142
  28.0 0.0 collective-permute-start.8
  28.0 0.0 copy-done.18
  28.0 0.1 collective-permute-start
  28.1 4.1 %collective-permute-done.refs_1_ = bf16[64,384]{1,0:T(8,128)(2,1)S(1)} collective-permute-done((bf16[64,384]{1,0:T(8,128)(2,1)S(1)}, bf16[64,384]{1,0:T(8,128)(2,1)S(1)}, u32[]{:S(2)}, u32[]{:S(2)}) %collective-permute-start) | collective-permute-done | bytes 49184 | tf_op jit(solution)/shard_map/ppermute | solution.py:142
  32.1 0.0 copy-done.17
  32.1 0.7 %collective-permute-start.1 = (bf16[64,384]{1,0:T(8,128)(2,1)S(1)}, bf16[64,384]{1,0:T(8,128)(2,1)S(1)}, u32[]{:S(2)}, u32[]{:S(2)}) collective-permute-start(bf16[64,384]{1,0:T(8,128)(2,1)S(1)} %copy-done.17), channel_id=1, source_target_pairs={{0,8},{1,9},{2,10},{3,11},{4,12},{5,13},{6,14},{7,15},{8,0},{9,1},... | collective-permute-start | bytes 147464 | tf_op jit(solution)/shard_map/ppermute | solution.py:142
  32.9 4.5 %collective-permute-done.1.refs_2_ = bf16[64,384]{1,0:T(8,128)(2,1)S(1)} collective-permute-done((bf16[64,384]{1,0:T(8,128)(2,1)S(1)}, bf16[64,384]{1,0:T(8,128)(2,1)S(1)}, u32[]{:S(2)}, u32[]{:S(2)}) %collective-permute-start.1) | collective-permute-done | bytes 49184 | tf_op jit(solution)/shard_map/ppermute | solution.py:142
  37.4 0.0 copy-done.16
  37.4 1.9 %collective-permute-start.2 = (bf16[64,384]{1,0:T(8,128)(2,1)S(1)}, bf16[64,384]{1,0:T(8,128)(2,1)S(1)}, u32[]{:S(2)}, u32[]{:S(2)}) collective-permute-start(bf16[64,384]{1,0:T(8,128)(2,1)S(1)} %copy-done.16), channel_id=1, source_target_pairs={{0,12},{1,13},{2,14},{3,15},{4,8},{5,9},{6,10},{7,11},{8,4},{9,5},... | collective-permute-start | bytes 147464 | tf_op jit(solution)/shard_map/ppermute | solution.py:142
  39.3 4.0 %collective-permute-done.2.refs_3_ = bf16[64,384]{1,0:T(8,128)(2,1)S(1)} collective-permute-done((bf16[64,384]{1,0:T(8,128)(2,1)S(1)}, bf16[64,384]{1,0:T(8,128)(2,1)S(1)}, u32[]{:S(2)}, u32[]{:S(2)}) %collective-permute-start.2) | collective-permute-done | bytes 49184 | tf_op jit(solution)/shard_map/ppermute | solution.py:142
  43.3 0.0 collective-permute-done.13.refs_10_
  43.3 0.0 collective-permute-done.7.refs_6_
  43.3 0.0 copy-start.5
  43.3 0.0 collective-permute-done.14.refs_11_
  43.3 0.0 copy-start.6
  43.3 0.0 collective-permute-done.8.refs_7_
  43.3 0.0 copy-start.7
  43.3 0.0 copy-done.1
  43.4 0.0 copy-done
  43.4 0.5 copy-done.10
  43.9 0.1 copy-done.4
  44.0 0.1 copy-done.5
  44.1 0.1 copy-done.6
  44.1 0.1 copy-done.7
  44.2 3.8 %attend.1 = (bf16[64,384]{1,0:T(8,128)(2,1)}, bf16[64,384]{1,0:T(8,128)(2,1)}, bf16[64,384]{1,0:T(8,128)(2,1)}, bf16[64,384]{1,0:T(8,128)(2,1)}) custom-call(bf16[64,384]{1,0:T(8,128)(2,1)} %get-tuple-element.21.refs_0_, bf16[64,384]{1,0:T(8,128)(2,1)} %copy-done.8, bf16[64,384]{1,0:T(8,128)(2,1)} %copy-done.9, bf16[64,384]{1,0:T(8,128)(2,1)} %copy-done.10, ...), custom_call_target="tpu_custom_call" | custom-call | tf_op jit(solution)/shard_map/attend/pallas_call | solution.py:95
  48.0 1.5 %collective-permute-start.15 = (bf16[64,384]{1,0:T(8,128)(2,1)}, bf16[64,384]{1,0:T(8,128)(2,1)S(1)}, u32[]{:S(2)}, u32[]{:S(2)}) collective-permute-start(bf16[64,384]{1,0:T(8,128)(2,1)} %get-tuple-element.33), channel_id=1, source_target_pairs={{0,16},{1,17},{2,18},{3,19},{4,20},{5,21},{6,22},{7,23},{8,24},{9,... | collective-permute-start | bytes 147464 | tf_op jit(solution)/shard_map/ppermute | solution.py:171
  49.5 0.0 collective-permute-start.16
  49.5 3.4 %collective-permute-start.17 = (bf16[64,384]{1,0:T(8,128)(2,1)}, bf16[64,384]{1,0:T(8,128)(2,1)S(1)}, u32[]{:S(2)}, u32[]{:S(2)}) collective-permute-start(bf16[64,384]{1,0:T(8,128)(2,1)} %get-tuple-element.35), channel_id=1, source_target_pairs={{0,24},{1,25},{2,26},{3,27},{4,28},{5,29},{6,30},{7,31},{8,16},{9,... | collective-permute-start | bytes 147464 | tf_op jit(solution)/shard_map/ppermute | solution.py:171
  52.9 1.9 %collective-permute-start.18 = (bf16[64,384]{1,0:T(8,128)(2,1)}, bf16[64,384]{1,0:T(8,128)(2,1)S(1)}, u32[]{:S(2)}, u32[]{:S(2)}) collective-permute-start(bf16[64,384]{1,0:T(8,128)(2,1)} %get-tuple-element.36), channel_id=1, source_target_pairs={{0,28},{1,29},{2,30},{3,31},{4,24},{5,25},{6,26},{7,27},{8,20},{9,... | collective-permute-start | bytes 147464 | tf_op jit(solution)/shard_map/ppermute | solution.py:171
  54.8 0.0 collective-permute-done.15.refs_0_
  54.8 0.0 collective-permute-done.16.refs_1_
  54.8 1.1 %collective-permute-done.17.refs_2_ = bf16[64,384]{1,0:T(8,128)(2,1)S(1)} collective-permute-done((bf16[64,384]{1,0:T(8,128)(2,1)}, bf16[64,384]{1,0:T(8,128)(2,1)S(1)}, u32[]{:S(2)}, u32[]{:S(2)}) %collective-permute-start.17) | collective-permute-done | bytes 49184 | tf_op jit(solution)/shard_map/ppermute | solution.py:171
  55.9 4.0 %collective-permute-done.18.refs_3_ = bf16[64,384]{1,0:T(8,128)(2,1)S(1)} collective-permute-done((bf16[64,384]{1,0:T(8,128)(2,1)}, bf16[64,384]{1,0:T(8,128)(2,1)S(1)}, u32[]{:S(2)}, u32[]{:S(2)}) %collective-permute-start.18) | collective-permute-done | bytes 49184 | tf_op jit(solution)/shard_map/ppermute | solution.py:171
  59.9 0.0 copy-start.14
  59.9 0.6 copy-done.14
  60.5 1.6 %join_heads.1 = bf16[1,64,1536]{2,1,0:T(8,128)(2,1)} custom-call(bf16[64,384]{1,0:T(8,128)(2,1)} %copy-done.11, bf16[64,384]{1,0:T(8,128)(2,1)} %copy-done.12, bf16[64,384]{1,0:T(8,128)(2,1)} %copy-done.13, bf16[64,384]{1,0:T(8,128)(2,1)} %copy-done.14), custom_call_target="tpu_custom_call" | custom-call | tf_op jit(solution)/shard_map/join_heads/pallas_call | solution.py:124
  (25 shorter events, 0.1 us)
Async XLA Ops:
  2.0 19.2 %collective-permute-start.3 = (bf16[64,384]{1,0:T(8,128)(2,1)}, bf16[64,384]{1,0:T(8,128)(2,1)S(1)}, u32[]{:S(2)}, u32[]{:S(2)}) collective-permute-start(bf16[64,384]{1,0:T(8,128)(2,1)} %get-tuple-element.26), channel_id=1, source_target_pairs={{0,4},{1,5},{2,6},{3,7},{4,0},{5,1},{6,2},{7,3},{8,12},{9,13},{10,... | collective-permute-start | bytes 147464 | tf_op jit(solution)/shard_map/ppermute | solution.py:142
  5.1 16.1 %collective-permute-start.4 = (bf16[64,384]{1,0:T(8,128)(2,1)}, bf16[64,384]{1,0:T(8,128)(2,1)S(1)}, u32[]{:S(2)}, u32[]{:S(2)}) collective-permute-start(bf16[64,384]{1,0:T(8,128)(2,1)} %get-tuple-element.27), channel_id=1, source_target_pairs={{0,8},{1,9},{2,10},{3,11},{4,12},{5,13},{6,14},{7,15},{8,0},{9,1},... | collective-permute-start | bytes 147464 | tf_op jit(solution)/shard_map/ppermute | solution.py:142
  7.7 13.6 %collective-permute-start.5 = (bf16[64,384]{1,0:T(8,128)(2,1)}, bf16[64,384]{1,0:T(8,128)(2,1)S(1)}, u32[]{:S(2)}, u32[]{:S(2)}) collective-permute-start(bf16[64,384]{1,0:T(8,128)(2,1)} %get-tuple-element.28), channel_id=1, source_target_pairs={{0,12},{1,13},{2,14},{3,15},{4,8},{5,9},{6,10},{7,11},{8,4},{9,5},... | collective-permute-start | bytes 147464 | tf_op jit(solution)/shard_map/ppermute | solution.py:142
  7.7 5.2 %collective-permute-start.9 = (bf16[64,384]{1,0:T(8,128)(2,1)}, bf16[64,384]{1,0:T(8,128)(2,1)S(1)}, u32[]{:S(2)}, u32[]{:S(2)}) collective-permute-start(bf16[64,384]{1,0:T(8,128)(2,1)} %get-tuple-element.30), channel_id=1, source_target_pairs={{0,4},{1,5},{2,6},{3,7},{4,0},{5,1},{6,2},{7,3},{8,12},{9,13},{10,... | collective-permute-start | bytes 147464 | tf_op jit(solution)/shard_map/ppermute | solution.py:142
  8.6 7.3 %collective-permute-start.10 = (bf16[64,384]{1,0:T(8,128)(2,1)}, bf16[64,384]{1,0:T(8,128)(2,1)S(1)}, u32[]{:S(2)}, u32[]{:S(2)}) collective-permute-start(bf16[64,384]{1,0:T(8,128)(2,1)} %get-tuple-element.31), channel_id=1, source_target_pairs={{0,8},{1,9},{2,10},{3,11},{4,12},{5,13},{6,14},{7,15},{8,0},{9,1},... | collective-permute-start | bytes 147464 | tf_op jit(solution)/shard_map/ppermute | solution.py:142
  12.0 0.8 %copy-start.15 = (bf16[64,384]{1,0:T(8,128)(2,1)S(1)}, bf16[64,384]{1,0:T(8,128)(2,1)}, u32[]{:S(2)}) copy-start(bf16[64,384]{1,0:T(8,128)(2,1)} %get-tuple-element.29) | copy-start | bytes 147460
  12.9 0.8 %copy-start.19 = (bf16[64,384]{1,0:T(8,128)(2,1)S(1)}, bf16[64,384]{1,0:T(8,128)(2,1)}, u32[]{:S(2)}) copy-start(bf16[64,384]{1,0:T(8,128)(2,1)} %get-tuple-element.32) | copy-start | bytes 147460
  13.7 5.9 %collective-permute-start.11 = (bf16[64,384]{1,0:T(8,128)(2,1)S(1)}, bf16[64,384]{1,0:T(8,128)(2,1)S(1)}, u32[]{:S(2)}, u32[]{:S(2)}) collective-permute-start(bf16[64,384]{1,0:T(8,128)(2,1)S(1)} %copy-done.19), channel_id=1, source_target_pairs={{0,12},{1,13},{2,14},{3,15},{4,8},{5,9},{6,10},{7,11},{8,4},{9,5},... | collective-permute-start | bytes 147464 | tf_op jit(solution)/shard_map/ppermute | solution.py:142
  19.6 23.8 %copy-start.1 = (bf16[256,384]{1,0:T(8,128)(2,1)}, bf16[256,384]{1,0:T(8,128)(2,1)S(1)}, u32[]{:S(2)}) copy-start(bf16[256,384]{1,0:T(8,128)(2,1)S(1)} %constant_dynamic-update-slice_fusion.4.refs_8_) | copy-start | bytes 589828
  19.6 6.3 %collective-permute-start.12 = (bf16[256,384]{1,0:T(8,128)(2,1)S(1)}, bf16[256,384]{1,0:T(8,128)(2,1)S(1)}, u32[]{:S(2)}, u32[]{:S(2)}) collective-permute-start(bf16[256,384]{1,0:T(8,128)(2,1)S(1)} %constant_dynamic-update-slice_fusion.4.refs_8_), channel_id=1, source_target_pairs={{0,2},{1,3},{2,0},{3,1},{4,6},{5,7},{6,4},{7,5},{8,10},{9,11},{10,... | collective-permute-start | bytes 589832 | tf_op jit(solution)/shard_map/ppermute | solution.py:142
  21.2 6.8 %copy-start.18 = (bf16[64,384]{1,0:T(8,128)(2,1)S(1)}, bf16[64,384]{1,0:T(8,128)(2,1)}, u32[]{:S(2)}) copy-start(bf16[64,384]{1,0:T(8,128)(2,1)} %get-tuple-element.22) | copy-start | bytes 147460
  21.2 10.9 %copy-start.17 = (bf16[64,384]{1,0:T(8,128)(2,1)S(1)}, bf16[64,384]{1,0:T(8,128)(2,1)}, u32[]{:S(2)}) copy-start(bf16[64,384]{1,0:T(8,128)(2,1)} %get-tuple-element.23) | copy-start | bytes 147460
  21.2 16.2 %copy-start.16 = (bf16[64,384]{1,0:T(8,128)(2,1)S(1)}, bf16[64,384]{1,0:T(8,128)(2,1)}, u32[]{:S(2)}) copy-start(bf16[64,384]{1,0:T(8,128)(2,1)} %get-tuple-element.24) | copy-start | bytes 147460
  21.3 22.1 %copy-start = (bf16[256,384]{1,0:T(8,128)(2,1)}, bf16[256,384]{1,0:T(8,128)(2,1)S(1)}, u32[]{:S(2)}) copy-start(bf16[256,384]{1,0:T(8,128)(2,1)S(1)} %constant_dynamic-update-slice_fusion.refs_4_) | copy-start | bytes 589828
  21.3 6.7 %collective-permute-start.6 = (bf16[256,384]{1,0:T(8,128)(2,1)S(1)}, bf16[256,384]{1,0:T(8,128)(2,1)S(1)}, u32[]{:S(2)}, u32[]{:S(2)}) collective-permute-start(bf16[256,384]{1,0:T(8,128)(2,1)S(1)} %constant_dynamic-update-slice_fusion.refs_4_), channel_id=1, source_target_pairs={{0,2},{1,3},{2,0},{3,1},{4,6},{5,7},{6,4},{7,5},{8,10},{9,11},{10,... | collective-permute-start | bytes 589832 | tf_op jit(solution)/shard_map/ppermute | solution.py:142
  21.8 21.4 %collective-permute-start.13 = (bf16[256,384]{1,0:T(8,128)(2,1)S(1)}, bf16[256,384]{1,0:T(8,128)(2,1)S(1)}, u32[]{:S(2)}, u32[]{:S(2)}) collective-permute-start(bf16[256,384]{1,0:T(8,128)(2,1)S(1)} %constant_dynamic-update-slice_fusion.4.refs_8_), channel_id=1, source_target_pairs={{0,1},{1,0},{2,3},{3,2},{4,5},{5,4},{6,7},{7,6},{8,9},{9,8},{10,11... | collective-permute-start | bytes 589832 | tf_op jit(solution)/shard_map/ppermute | solution.py:142
  21.9 21.4 %collective-permute-start.7 = (bf16[256,384]{1,0:T(8,128)(2,1)S(1)}, bf16[256,384]{1,0:T(8,128)(2,1)S(1)}, u32[]{:S(2)}, u32[]{:S(2)}) collective-permute-start(bf16[256,384]{1,0:T(8,128)(2,1)S(1)} %constant_dynamic-update-slice_fusion.refs_4_), channel_id=1, source_target_pairs={{0,1},{1,0},{2,3},{3,2},{4,5},{5,4},{6,7},{7,6},{8,9},{9,8},{10,11... | collective-permute-start | bytes 589832 | tf_op jit(solution)/shard_map/ppermute | solution.py:142
  25.9 17.5 %copy-start.2 = (bf16[256,384]{1,0:T(8,128)(2,1)}, bf16[256,384]{1,0:T(8,128)(2,1)S(1)}, u32[]{:S(2)}) copy-start(bf16[256,384]{1,0:T(8,128)(2,1)S(1)} %collective-permute-done.12.refs_9_) | copy-start | bytes 589828
  25.9 17.4 %collective-permute-start.14 = (bf16[256,384]{1,0:T(8,128)(2,1)S(1)}, bf16[256,384]{1,0:T(8,128)(2,1)S(1)}, u32[]{:S(2)}, u32[]{:S(2)}) collective-permute-start(bf16[256,384]{1,0:T(8,128)(2,1)S(1)} %collective-permute-done.12.refs_9_), channel_id=1, source_target_pairs={{0,1},{1,0},{2,3},{3,2},{4,5},{5,4},{6,7},{7,6},{8,9},{9,8},{10,11... | collective-permute-start | bytes 589832 | tf_op jit(solution)/shard_map/ppermute | solution.py:142
  28.0 15.4 %copy-start.3 = (bf16[256,384]{1,0:T(8,128)(2,1)}, bf16[256,384]{1,0:T(8,128)(2,1)S(1)}, u32[]{:S(2)}) copy-start(bf16[256,384]{1,0:T(8,128)(2,1)S(1)} %collective-permute-done.6.refs_5_) | copy-start | bytes 589828
  28.0 15.3 %collective-permute-start.8 = (bf16[256,384]{1,0:T(8,128)(2,1)S(1)}, bf16[256,384]{1,0:T(8,128)(2,1)S(1)}, u32[]{:S(2)}, u32[]{:S(2)}) collective-permute-start(bf16[256,384]{1,0:T(8,128)(2,1)S(1)} %collective-permute-done.6.refs_5_), channel_id=1, source_target_pairs={{0,1},{1,0},{2,3},{3,2},{4,5},{5,4},{6,7},{7,6},{8,9},{9,8},{10,11... | collective-permute-start | bytes 589832 | tf_op jit(solution)/shard_map/ppermute | solution.py:142
  28.0 4.2 %collective-permute-start = (bf16[64,384]{1,0:T(8,128)(2,1)S(1)}, bf16[64,384]{1,0:T(8,128)(2,1)S(1)}, u32[]{:S(2)}, u32[]{:S(2)}) collective-permute-start(bf16[64,384]{1,0:T(8,128)(2,1)S(1)} %copy-done.18), channel_id=1, source_target_pairs={{0,4},{1,5},{2,6},{3,7},{4,0},{5,1},{6,2},{7,3},{8,12},{9,13},{10,... | collective-permute-start | bytes 147464 | tf_op jit(solution)/shard_map/ppermute | solution.py:142
  32.1 11.2 %copy-start.8 = (bf16[64,384]{1,0:T(8,128)(2,1)}, bf16[64,384]{1,0:T(8,128)(2,1)S(1)}, u32[]{:S(2)}) copy-start(bf16[64,384]{1,0:T(8,128)(2,1)S(1)} %collective-permute-done.refs_1_) | copy-start | bytes 147460
  32.1 5.2 %collective-permute-start.1 = (bf16[64,384]{1,0:T(8,128)(2,1)S(1)}, bf16[64,384]{1,0:T(8,128)(2,1)S(1)}, u32[]{:S(2)}, u32[]{:S(2)}) collective-permute-start(bf16[64,384]{1,0:T(8,128)(2,1)S(1)} %copy-done.17), channel_id=1, source_target_pairs={{0,8},{1,9},{2,10},{3,11},{4,12},{5,13},{6,14},{7,15},{8,0},{9,1},... | collective-permute-start | bytes 147464 | tf_op jit(solution)/shard_map/ppermute | solution.py:142
  37.4 6.0 %copy-start.9 = (bf16[64,384]{1,0:T(8,128)(2,1)}, bf16[64,384]{1,0:T(8,128)(2,1)S(1)}, u32[]{:S(2)}) copy-start(bf16[64,384]{1,0:T(8,128)(2,1)S(1)} %collective-permute-done.1.refs_2_) | copy-start | bytes 147460
  37.4 5.9 %collective-permute-start.2 = (bf16[64,384]{1,0:T(8,128)(2,1)S(1)}, bf16[64,384]{1,0:T(8,128)(2,1)S(1)}, u32[]{:S(2)}, u32[]{:S(2)}) collective-permute-start(bf16[64,384]{1,0:T(8,128)(2,1)S(1)} %copy-done.16), channel_id=1, source_target_pairs={{0,12},{1,13},{2,14},{3,15},{4,8},{5,9},{6,10},{7,11},{8,4},{9,5},... | collective-permute-start | bytes 147464 | tf_op jit(solution)/shard_map/ppermute | solution.py:142
  43.3 0.6 copy-start.10
  43.3 0.7 %copy-start.4 = (bf16[256,384]{1,0:T(8,128)(2,1)}, bf16[256,384]{1,0:T(8,128)(2,1)S(1)}, u32[]{:S(2)}) copy-start(bf16[256,384]{1,0:T(8,128)(2,1)S(1)} %collective-permute-done.13.refs_10_) | copy-start | bytes 589828
  43.3 0.8 %copy-start.5 = (bf16[256,384]{1,0:T(8,128)(2,1)}, bf16[256,384]{1,0:T(8,128)(2,1)S(1)}, u32[]{:S(2)}) copy-start(bf16[256,384]{1,0:T(8,128)(2,1)S(1)} %collective-permute-done.7.refs_6_) | copy-start | bytes 589828
  43.3 0.8 %copy-start.6 = (bf16[256,384]{1,0:T(8,128)(2,1)}, bf16[256,384]{1,0:T(8,128)(2,1)S(1)}, u32[]{:S(2)}) copy-start(bf16[256,384]{1,0:T(8,128)(2,1)S(1)} %collective-permute-done.14.refs_11_) | copy-start | bytes 589828
  43.3 0.9 %copy-start.7 = (bf16[256,384]{1,0:T(8,128)(2,1)}, bf16[256,384]{1,0:T(8,128)(2,1)S(1)}, u32[]{:S(2)}) copy-start(bf16[256,384]{1,0:T(8,128)(2,1)S(1)} %collective-permute-done.8.refs_7_) | copy-start | bytes 589828
  48.0 6.8 %collective-permute-start.15 = (bf16[64,384]{1,0:T(8,128)(2,1)}, bf16[64,384]{1,0:T(8,128)(2,1)S(1)}, u32[]{:S(2)}, u32[]{:S(2)}) collective-permute-start(bf16[64,384]{1,0:T(8,128)(2,1)} %get-tuple-element.33), channel_id=1, source_target_pairs={{0,16},{1,17},{2,18},{3,19},{4,20},{5,21},{6,22},{7,23},{8,24},{9,... | collective-permute-start | bytes 147464 | tf_op jit(solution)/shard_map/ppermute | solution.py:171
  49.5 5.3 %collective-permute-start.16 = (bf16[64,384]{1,0:T(8,128)(2,1)}, bf16[64,384]{1,0:T(8,128)(2,1)S(1)}, u32[]{:S(2)}, u32[]{:S(2)}) collective-permute-start(bf16[64,384]{1,0:T(8,128)(2,1)} %get-tuple-element.34), channel_id=1, source_target_pairs={{0,20},{1,21},{2,22},{3,23},{4,16},{5,17},{6,18},{7,19},{8,28},{9,... | collective-permute-start | bytes 147464 | tf_op jit(solution)/shard_map/ppermute | solution.py:171
  49.5 6.4 %collective-permute-start.17 = (bf16[64,384]{1,0:T(8,128)(2,1)}, bf16[64,384]{1,0:T(8,128)(2,1)S(1)}, u32[]{:S(2)}, u32[]{:S(2)}) collective-permute-start(bf16[64,384]{1,0:T(8,128)(2,1)} %get-tuple-element.35), channel_id=1, source_target_pairs={{0,24},{1,25},{2,26},{3,27},{4,28},{5,29},{6,30},{7,31},{8,16},{9,... | collective-permute-start | bytes 147464 | tf_op jit(solution)/shard_map/ppermute | solution.py:171
  52.9 7.0 %collective-permute-start.18 = (bf16[64,384]{1,0:T(8,128)(2,1)}, bf16[64,384]{1,0:T(8,128)(2,1)S(1)}, u32[]{:S(2)}, u32[]{:S(2)}) collective-permute-start(bf16[64,384]{1,0:T(8,128)(2,1)} %get-tuple-element.36), channel_id=1, source_target_pairs={{0,28},{1,29},{2,30},{3,31},{4,24},{5,25},{6,26},{7,27},{8,20},{9,... | collective-permute-start | bytes 147464 | tf_op jit(solution)/shard_map/ppermute | solution.py:171
  54.8 5.1 %copy-start.11 = (bf16[64,384]{1,0:T(8,128)(2,1)}, bf16[64,384]{1,0:T(8,128)(2,1)S(1)}, u32[]{:S(2)}) copy-start(bf16[64,384]{1,0:T(8,128)(2,1)S(1)} %collective-permute-done.15.refs_0_) | copy-start | bytes 147460
  54.8 5.1 %copy-start.12 = (bf16[64,384]{1,0:T(8,128)(2,1)}, bf16[64,384]{1,0:T(8,128)(2,1)S(1)}, u32[]{:S(2)}) copy-start(bf16[64,384]{1,0:T(8,128)(2,1)S(1)} %collective-permute-done.16.refs_1_) | copy-start | bytes 147460
  55.9 4.0 %copy-start.13 = (bf16[64,384]{1,0:T(8,128)(2,1)}, bf16[64,384]{1,0:T(8,128)(2,1)S(1)}, u32[]{:S(2)}) copy-start(bf16[64,384]{1,0:T(8,128)(2,1)S(1)} %collective-permute-done.17.refs_2_) | copy-start | bytes 147460
  59.9 0.6 copy-start.14

commit v2 on v1

v2 whole, which is shorter than its diff:
```python
import jax
import jax.numpy as jnp
from jax import lax
from jax.experimental import pallas as pl
from jax.experimental.pallas import tpu as pltpu
from jax.sharding import PartitionSpec as P

HD = 128
HBM = pl.BlockSpec(memory_space=pltpu.HBM)
VMEM = pl.BlockSpec(memory_space=pltpu.VMEM)
PARAMS = pltpu.CompilerParams(vmem_limit_bytes=16 << 20)


def group_count(heads, places):
    count = 1
    while heads % (2 * count) == 0 and places % (2 * count) == 0:
        count *= 2
    return count


def run_copies(pairs, sem):
    copies = [
        pltpu.make_async_copy(source, target, sem.at[i])
        for i, (source, target) in enumerate(pairs)
    ]
    for copy in copies:
        copy.start()
    for copy in copies:
        copy.wait()


def group_columns(step, inner, width):
    mine = lax.axis_index("seq") // inner
    return pl.ds(pl.multiple_of((mine ^ step) * width, HD), width)


def split_heads(queries, key_value, groups, inner):
    rows, full = queries.shape[1:]
    width = full // groups

    def kernel(q_ref, kv_ref, *rest):
        first, second, sem = rest[:groups], rest[groups : 2 * groups], rest[-1]
        mine = lax.axis_index("seq") // inner
        pairs = []
        for step in range(groups):
            start = (mine ^ step) * width
            cols = pl.ds(pl.multiple_of(start, HD), width)
            pairs.append((kv_ref.at[0, 0, :, cols], first[step]))
            pairs.append((kv_ref.at[1, 0, :, cols], second[step].at[:, pl.ds(0, width)]))
            pairs.append((q_ref.at[0, :, cols], second[step].at[:, pl.ds(width, width)]))
        run_copies(pairs, sem)

    out = pl.pallas_call(
        kernel,
        out_shape=[jax.ShapeDtypeStruct((rows, width), queries.dtype)] * groups
        + [jax.ShapeDtypeStruct((rows, 2 * width), queries.dtype)] * groups,
        in_specs=[HBM, HBM],
        out_specs=[VMEM] * (2 * groups),
        scratch_shapes=[pltpu.SemaphoreType.DMA((3 * groups,))],
        name="split_heads",
        compiler_params=PARAMS,
    )(
        pltpu.with_memory_space_constraint(queries, pltpu.HBM),
        pltpu.with_memory_space_constraint(key_value, pltpu.HBM),
    )
    return out[:groups], out[groups:]


def weigh(query_pieces, key_blocks, width):
    groups, blocks = len(query_pieces), len(key_blocks)
    rows = query_pieces[0].shape[0]
    offset = query_pieces[0].shape[1] - width
    heads, keys = width // HD, sum(block.shape[0] for block in key_blocks)
    contract = (((1,), (1,)), ((), ()))

    def kernel(*refs):
        query_refs, key_refs = refs[:groups], refs[groups : groups + blocks]
        weights_ref, sums_ref = refs[groups + blocks :]
        for head in range(heads):
            cols = slice(head * HD, (head + 1) * HD)
            q_cols = slice(offset + head * HD, offset + (head + 1) * HD)
            q = jnp.concatenate([ref[:, q_cols] for ref in query_refs], axis=0)
            k = jnp.concatenate([ref[:, cols] for ref in key_refs], axis=0)
            scores = lax.dot_general(q, k, contract, preferred_element_type=jnp.float32)
            scores = scores * HD ** (-0.5)
            weights = jnp.exp(scores - jnp.max(scores, axis=1, keepdims=True))
            sums_ref[:, head : head + 1] = jnp.sum(weights, axis=1, keepdims=True)
            weights_ref[head] = weights.astype(jnp.bfloat16)

    return pl.pallas_call(
        kernel,
        out_shape=[
            jax.ShapeDtypeStruct((heads, groups * rows, keys), jnp.bfloat16),
            jax.ShapeDtypeStruct((groups * rows, HD), jnp.float32),
        ],
        in_specs=[VMEM] * (groups + blocks),
        out_specs=[VMEM] * 2,
        name="weigh",
        compiler_params=PARAMS,
    )(*query_pieces, *key_blocks)


def average(weights, sums, value_blocks, groups):
    heads, queries, keys = weights.shape
    rows = queries // groups
    blocks = len(value_blocks)

    def kernel(weights_ref, sums_ref, *refs):
        value_refs, out_refs = refs[:blocks], refs[blocks:]
        for head in range(heads):
            cols = slice(head * HD, (head + 1) * HD)
            v = jnp.concatenate([ref[:, cols] for ref in value_refs], axis=0)
            total = jnp.dot(weights_ref[head], v, preferred_element_type=jnp.float32)
            out = (total / sums_ref[:, head : head + 1]).astype(jnp.bfloat16)
            for step, ref in enumerate(out_refs):
                ref[:, cols] = out[step * rows : (step + 1) * rows]

    return pl.pallas_call(
        kernel,
        out_shape=[jax.ShapeDtypeStruct((rows, heads * HD), jnp.bfloat16)] * groups,
        in_specs=[VMEM] * (2 + blocks),
        out_specs=[VMEM] * groups,
        name="average",
        compiler_params=PARAMS,
    )(weights, sums, *value_blocks)


def join_heads(pieces, inner):
    groups = len(pieces)
    rows, width = pieces[0].shape

    def kernel(*refs):
        out_ref, sem = refs[groups:]
        run_copies(
            [
                (refs[step], out_ref.at[0, :, group_columns(step, inner, width)])
                for step in range(groups)
            ],
            sem,
        )

    return pl.pallas_call(
        kernel,
        out_shape=jax.ShapeDtypeStruct((1, rows, groups * width), jnp.bfloat16),
        in_specs=[VMEM] * groups,
        out_specs=pl.BlockSpec(memory_space=pl.ANY),
        scratch_shapes=[pltpu.SemaphoreType.DMA((groups,))],
        name="join_heads",
        compiler_params=PARAMS,
    )(*pieces)


def shards(queries, key_value):
    places = lax.axis_size("seq")
    segments = lax.axis_size("segment")
    rows = queries.shape[1]
    groups = group_count(queries.shape[2] // HD, places)
    inner = places // groups

    def swap(value, bits):
        return lax.ppermute(value, "seq", [(i, i ^ bits) for i in range(places)])

    def exchange(pieces):
        far = [swap(pieces[s], s * inner) for s in range(groups - 1, 0, -1)]
        return [pieces[0]] + far[::-1]

    def gather(block):
        blocks, bits = [block], inner // 2
        while bits:
            blocks = blocks + [swap(block, bits) for block in blocks]
            bits //= 2
        return blocks

    width = queries.shape[2] // groups
    first, second = split_heads(queries, key_value, groups, inner)
    first, second = exchange(first), exchange(second)
    key_blocks = gather(jnp.concatenate(first, axis=0))
    value_blocks = gather(jnp.concatenate([piece[:, :width] for piece in second], axis=0))
    weights, sums = weigh(second, key_blocks, width)
    attended = average(weights, sums, value_blocks, groups)

    def hand(value, step):
        pairs = [
            (
                segment * places + i,
                ((segment + 1) % segments) * places + (i ^ (step * inner)),
            )
            for segment in range(segments)
            for i in range(places)
        ]
        return lax.ppermute(value, ("segment", "seq"), pairs)

    handed = [hand(attended[s], s) for s in range(groups - 1, -1, -1)][::-1]
    return join_heads(handed, inner)


def solution(mesh):
    return jax.shard_map(
        shards,
        mesh=mesh,
        in_specs=(P("segment", "seq", None), P(None, "segment", "seq", None)),
        out_specs=P("segment", "seq", None),
        check_vma=False,
    )
```

time: 62.4 us -> 39.8 us (0.64)
  waiting for transfers between devices: 26.9 us -> 15.1 us
  Pallas kernels: 7.34 us -> 3.58 us
  starting transfers between devices: 24.4 us -> 20.7 us
  local copies, waits for them, and re-layouts: 3.14 us -> 0.07 us
    ppermute x15 -> x12, waiting for transfers between devices: 21.8 us -> 10 us  [swap(): return lax.ppermute(value, 'seq', [(i, i ^ bits) for i in range(places)])]
    ppermute x15 -> x12, starting transfers between devices: 17.7 us -> 13.8 us  [swap(): return lax.ppermute(value, 'seq', [(i, i ^ bits) for i in range(places)])]
    unnamed x46 -> x3, local copies, waits for them, and re-layouts: 3.12 us -> 0.03 us
    pallas_call x1 -> x2, Pallas kernels: 3.8 us -> 1.71 us  [the longest x1 1.15 us: weigh(): pl.pallas_call(kernel, out_shape=[jax.ShapeDtypeStruct((heads, groups * r...]
    pallas_call x1, Pallas kernels: 1.57 us -> 0.7 us  [join_heads(): pl.pallas_call(kernel, out_shape=jax.ShapeDtypeStruct((1, rows, groups *...]
    pallas_call x1, Pallas kernels: 1.97 us -> 1.17 us  [split_heads(): pl.pallas_call(kernel, out_shape=[jax.ShapeDtypeStruct((rows, width), que...]
  transfers between devices with their start and end apart: 19 -> 16, of which waited for: 8 -> 6; matrix products, arithmetic and copies ran while one was open for 1% -> 0% of each run, Pallas kernels for 0% -> 3%
where the time goes in v2:
time: 39.8 us; the launch traced here: 39.6 us
  starting transfers between devices  20.7 us (52%)
  waiting for transfers between devices  15.1 us (38%)
  Pallas kernels  3.58 us (9%)
    ppermute x12, starting transfers between devices, swap(): return lax.ppermute(value, 'seq', [(i, i ^ bits) for i in range(places)])  13.8 us
    ppermute x12, waiting for transfers between devices, swap(): return lax.ppermute(value, 'seq', [(i, i ^ bits) for i in range(places)])  10 us
    ppermute x4, starting transfers between devices, hand(): return lax.ppermute(value, ('segment', 'seq'), pairs)  6.9 us
    ppermute x4, waiting for transfers between devices, hand(): return lax.ppermute(value, ('segment', 'seq'), pairs)  5.06 us
    pallas_call x1, Pallas kernels, split_heads(): pl.pallas_call(kernel, out_shape=[jax.ShapeDtypeStruct((rows, width), que...  1.17 us
    pallas_call x1, Pallas kernels, weigh(): pl.pallas_call(kernel, out_shape=[jax.ShapeDtypeStruct((heads, groups * r...  1.15 us
  transfers between devices with their start and end apart: 16, of which 6 were waited for; matrix products, arithmetic and copies ran while one was open for 0% of the time, Pallas kernels for 3%

profile of v2, /device:TPU:0, one launch (start us, length us, event | category | flops | bytes accessed | tf_op | source)
XLA Modules:
  0.0 39.6 jit_solution(5403987478640145807)
XLA Ops:
  0.0 1.2 %split_heads.1 = (bf16[64,384]{1,0:T(8,128)(2,1)S(1)}, bf16[64,384]{1,0:T(8,128)(2,1)S(1)}, bf16[64,384]{1,0:T(8,128)(2,1)S(1)}, bf16[64,384]{1,0:T(8,128)(2,1)S...) custom-call(bf16[1,64,1536]{2,1,0:T(8,128)(2,1)} %q_ref.1, ...), custom_call_target="tpu_custom_call" | custom-call | tf_op jit(solution)/shard_map/split_heads/pallas_call | solution.py:53
  1.2 3.1 %collective-permute-start.3 = (bf16[64,384]{1,0:T(8,128)(2,1)S(1)}, bf16[64,384]{1,0:T(8,128)(2,1)S(1)}, u32[]{:S(2)}, u32[]{:S(2)}) collective-permute-start(bf16[64,384]{1,0:T(8,128)(2,1)S(1)} %get-tuple-element.24), channel_id=1, source_target_pairs={{0,4},{1,5},{2,6},{3,7},{4,0},{5,1},{6,2},{7,3},{8,12},{9,13},{10,... | collective-permute-start | bytes 147464 | tf_op jit(solution)/shard_map/ppermute | solution.py:161
  4.3 2.6 %collective-permute-start.4 = (bf16[64,384]{1,0:T(8,128)(2,1)S(1)}, bf16[64,384]{1,0:T(8,128)(2,1)S(1)}, u32[]{:S(2)}, u32[]{:S(2)}) collective-permute-start(bf16[64,384]{1,0:T(8,128)(2,1)S(1)} %get-tuple-element.25), channel_id=1, source_target_pairs={{0,8},{1,9},{2,10},{3,11},{4,12},{5,13},{6,14},{7,15},{8,0},{9,1},... | collective-permute-start | bytes 147464 | tf_op jit(solution)/shard_map/ppermute | solution.py:161
  6.9 0.0 collective-permute-start.5
  6.9 0.9 %collective-permute-start = (bf16[64,768]{1,0:T(8,128)(2,1)S(1)}, bf16[64,768]{1,0:T(8,128)(2,1)S(1)}, u32[]{:S(2)}, u32[]{:S(2)}) collective-permute-start(bf16[64,768]{1,0:T(8,128)(2,1)S(1)} %get-tuple-element.20), channel_id=1, source_target_pairs={{0,4},{1,5},{2,6},{3,7},{4,0},{5,1},{6,2},{7,3},{8,12},{9,13},{10,... | collective-permute-start | bytes 294920 | tf_op jit(solution)/shard_map/ppermute | solution.py:161
  7.8 3.5 %collective-permute-start.1 = (bf16[64,768]{1,0:T(8,128)(2,1)S(1)}, bf16[64,768]{1,0:T(8,128)(2,1)S(1)}, u32[]{:S(2)}, u32[]{:S(2)}) collective-permute-start(bf16[64,768]{1,0:T(8,128)(2,1)S(1)} %get-tuple-element.21), channel_id=1, source_target_pairs={{0,8},{1,9},{2,10},{3,11},{4,12},{5,13},{6,14},{7,15},{8,0},{9,1},... | collective-permute-start | bytes 294920 | tf_op jit(solution)/shard_map/ppermute | solution.py:161
  11.3 0.0 collective-permute-done.3
  11.3 0.1 collective-permute-start.2
  11.4 0.0 collective-permute-done.4
  11.4 2.0 %collective-permute-done.5 = bf16[64,384]{1,0:T(8,128)(2,1)S(1)} collective-permute-done((bf16[64,384]{1,0:T(8,128)(2,1)S(1)}, bf16[64,384]{1,0:T(8,128)(2,1)S(1)}, u32[]{:S(2)}, u32[]{:S(2)}) %collective-permute-start.5) | collective-permute-done | bytes 49184 | tf_op jit(solution)/shard_map/ppermute | solution.py:161
  13.4 1.6 %collective-permute-start.6 = (bf16[256,384]{1,0:T(8,128)(2,1)S(1)}, bf16[256,384]{1,0:T(8,128)(2,1)S(1)}, u32[]{:S(2)}, u32[]{:S(2)}) collective-permute-start(bf16[256,384]{1,0:T(8,128)(2,1)S(1)} %constant_dynamic-update-slice_fusion.refs_4_), channel_id=1, source_target_pairs={{0,2},{1,3},{2,0},{3,1},{4,6},{5,7},{6,4},{7,5},{8,10},{9,11},{10,... | collective-permute-start | bytes 589832 | tf_op jit(solution)/shard_map/ppermute | solution.py:161
  15.0 0.0 collective-permute-done.refs_1_
  15.0 4.1 %collective-permute-done.1.refs_2_ = bf16[64,768]{1,0:T(8,128)(2,1)S(1)} collective-permute-done((bf16[64,768]{1,0:T(8,128)(2,1)S(1)}, bf16[64,768]{1,0:T(8,128)(2,1)S(1)}, u32[]{:S(2)}, u32[]{:S(2)}) %collective-permute-start.1) | collective-permute-done | bytes 98336 | tf_op jit(solution)/shard_map/ppermute | solution.py:161
  19.1 0.0 collective-permute-done.2.refs_3_
  19.2 1.6 %collective-permute-start.9 = (bf16[256,384]{1,0:T(8,128)(2,1)S(1)}, bf16[256,384]{1,0:T(8,128)(2,1)S(1)}, u32[]{:S(2)}, u32[]{:S(2)}) collective-permute-start(bf16[256,384]{1,0:T(8,128)(2,1)S(1)} %pad_maximum_fusion.refs_0_), channel_id=1, source_target_pairs={{0,2},{1,3},{2,0},{3,1},{4,6},{5,7},{6,4},{7,5},{8,10},{9,11},{10,... | collective-permute-start | bytes 589832 | tf_op jit(solution)/shard_map/ppermute | solution.py:161
  20.8 0.0 collective-permute-start.7
  20.8 0.0 collective-permute-done.6.refs_5_
  20.8 0.5 %collective-permute-start.8 = (bf16[256,384]{1,0:T(8,128)(2,1)S(1)}, bf16[256,384]{1,0:T(8,128)(2,1)S(1)}, u32[]{:S(2)}, u32[]{:S(2)}) collective-permute-start(bf16[256,384]{1,0:T(8,128)(2,1)S(1)} %collective-permute-done.6.refs_5_), channel_id=1, source_target_pairs={{0,1},{1,0},{2,3},{3,2},{4,5},{5,4},{6,7},{7,6},{8,9},{9,8},{10,11... | collective-permute-start | bytes 589832 | tf_op jit(solution)/shard_map/ppermute | solution.py:161
  21.3 0.0 collective-permute-start.10
  21.3 3.6 %collective-permute-done.9.refs_1_ = bf16[256,384]{1,0:T(8,128)(2,1)S(1)} collective-permute-done((bf16[256,384]{1,0:T(8,128)(2,1)S(1)}, bf16[256,384]{1,0:T(8,128)(2,1)S(1)}, u32[]{:S(2)}, u32[]{:S(2)}) %collective-permute-start.9) | collective-permute-done | bytes 196640 | tf_op jit(solution)/shard_map/ppermute | solution.py:161
  24.9 0.0 collective-permute-start.11
  24.9 0.0 collective-permute-done.7.refs_6_
  24.9 0.0 collective-permute-done.8.refs_7_
  24.9 1.1 %weigh.1 = (bf16[3,256,1024]{2,1,0:T(8,128)(2,1)S(1)}, f32[256,128]{1,0:T(8,128)S(1)}) custom-call(bf16[64,768]{1,0:T(8,128)(2,1)S(1)} %get-tuple-element.19.refs_0_, bf16[64,768]{1,0:T(8,128)(2,1)S(1)} %collective-permute-done.refs_1_, bf16[64,768]{1,0:T(8,128)(2,1)S(1)} %collective-permute-done.1.refs_2_, ...), custom_call_target="tpu_custom_call" | custom-call | tf_op jit(solution)/shard_map/weigh/pallas_call | solution.py:90
  26.1 0.0 collective-permute-done.10.refs_2_
  26.1 0.3 collective-permute-done.11.refs_3_
  26.3 0.6 %average.1 = (bf16[64,384]{1,0:T(8,128)(2,1)S(1)}, bf16[64,384]{1,0:T(8,128)(2,1)S(1)}, bf16[64,384]{1,0:T(8,128)(2,1)S(1)}, bf16[64,384]{1,0:T(8,128)(2,1)S(1)}) custom-call(bf16[3,256,1024]{2,1,0:T(8,128)(2,1)S(1)} %get-tuple-element.27.weights_ref, f32[256,128]{1,0:T(8,128)S(1)} %get-tuple-element.28.sums_ref, ...), custom_call_target="tpu_custom_call" | custom-call | tf_op jit(solution)/shard_map/average/pallas_call | solution.py:118
  26.9 1.6 %collective-permute-start.12 = (bf16[64,384]{1,0:T(8,128)(2,1)S(1)}, bf16[64,384]{1,0:T(8,128)(2,1)S(1)}, u32[]{:S(2)}, u32[]{:S(2)}) collective-permute-start(bf16[64,384]{1,0:T(8,128)(2,1)S(1)} %get-tuple-element.29), channel_id=1, source_target_pairs={{0,16},{1,17},{2,18},{3,19},{4,20},{5,21},{6,22},{7,23},{8,24},{9,... | collective-permute-start | bytes 147464 | tf_op jit(solution)/shard_map/ppermute | solution.py:191
  28.5 2.0 %collective-permute-start.13 = (bf16[64,384]{1,0:T(8,128)(2,1)S(1)}, bf16[64,384]{1,0:T(8,128)(2,1)S(1)}, u32[]{:S(2)}, u32[]{:S(2)}) collective-permute-start(bf16[64,384]{1,0:T(8,128)(2,1)S(1)} %get-tuple-element.30), channel_id=1, source_target_pairs={{0,20},{1,21},{2,22},{3,23},{4,16},{5,17},{6,18},{7,19},{8,28},{9,... | collective-permute-start | bytes 147464 | tf_op jit(solution)/shard_map/ppermute | solution.py:191
  30.5 1.5 %collective-permute-start.14 = (bf16[64,384]{1,0:T(8,128)(2,1)S(1)}, bf16[64,384]{1,0:T(8,128)(2,1)S(1)}, u32[]{:S(2)}, u32[]{:S(2)}) collective-permute-start(bf16[64,384]{1,0:T(8,128)(2,1)S(1)} %get-tuple-element.31), channel_id=1, source_target_pairs={{0,24},{1,25},{2,26},{3,27},{4,28},{5,29},{6,30},{7,31},{8,16},{9,... | collective-permute-start | bytes 147464 | tf_op jit(solution)/shard_map/ppermute | solution.py:191
  32.0 1.8 %collective-permute-start.15 = (bf16[64,384]{1,0:T(8,128)(2,1)S(1)}, bf16[64,384]{1,0:T(8,128)(2,1)S(1)}, u32[]{:S(2)}, u32[]{:S(2)}) collective-permute-start(bf16[64,384]{1,0:T(8,128)(2,1)S(1)} %get-tuple-element.32), channel_id=1, source_target_pairs={{0,28},{1,29},{2,30},{3,31},{4,24},{5,25},{6,26},{7,27},{8,20},{9,... | collective-permute-start | bytes 147464 | tf_op jit(solution)/shard_map/ppermute | solution.py:191
  33.8 0.0 collective-permute-done.12.refs_0_
  33.8 0.0 collective-permute-done.13.refs_1_
  33.8 3.8 %collective-permute-done.14.refs_2_ = bf16[64,384]{1,0:T(8,128)(2,1)S(1)} collective-permute-done((bf16[64,384]{1,0:T(8,128)(2,1)S(1)}, bf16[64,384]{1,0:T(8,128)(2,1)S(1)}, u32[]{:S(2)}, u32[]{:S(2)}) %collective-permute-start.14) | collective-permute-done | bytes 49184 | tf_op jit(solution)/shard_map/ppermute | solution.py:191
  37.6 1.3 %collective-permute-done.15.refs_3_ = bf16[64,384]{1,0:T(8,128)(2,1)S(1)} collective-permute-done((bf16[64,384]{1,0:T(8,128)(2,1)S(1)}, bf16[64,384]{1,0:T(8,128)(2,1)S(1)}, u32[]{:S(2)}, u32[]{:S(2)}) %collective-permute-start.15) | collective-permute-done | bytes 49184 | tf_op jit(solution)/shard_map/ppermute | solution.py:191
  38.9 0.7 %join_heads.1 = bf16[1,64,1536]{2,1,0:T(8,128)(2,1)} custom-call(bf16[64,384]{1,0:T(8,128)(2,1)S(1)} %collective-permute-done.12.refs_0_, bf16[64,384]{1,0:T(8,128)(2,1)S(1)} %collective-permute-done.13.refs_1_, bf16[64,384]{1,0:T(8,128)(2,1)S(1)} %collective-permute-done.14.refs_2_, bf16[64,384]{1,0:T(8,128)(2,1)S(1)} %collective-permute-done.15.refs_3_), custom_call_target="tpu_custom_call" | custom-call | tf_op jit(solution)/shard_map/join_heads/pallas_call | solution.py:142
  (9 shorter events, 0.1 us)
Async XLA Ops:
  1.2 10.1 %collective-permute-start.3 = (bf16[64,384]{1,0:T(8,128)(2,1)S(1)}, bf16[64,384]{1,0:T(8,128)(2,1)S(1)}, u32[]{:S(2)}, u32[]{:S(2)}) collective-permute-start(bf16[64,384]{1,0:T(8,128)(2,1)S(1)} %get-tuple-element.24), channel_id=1, source_target_pairs={{0,4},{1,5},{2,6},{3,7},{4,0},{5,1},{6,2},{7,3},{8,12},{9,13},{10,... | collective-permute-start | bytes 147464 | tf_op jit(solution)/shard_map/ppermute | solution.py:161
  4.3 7.1 %collective-permute-start.4 = (bf16[64,384]{1,0:T(8,128)(2,1)S(1)}, bf16[64,384]{1,0:T(8,128)(2,1)S(1)}, u32[]{:S(2)}, u32[]{:S(2)}) collective-permute-start(bf16[64,384]{1,0:T(8,128)(2,1)S(1)} %get-tuple-element.25), channel_id=1, source_target_pairs={{0,8},{1,9},{2,10},{3,11},{4,12},{5,13},{6,14},{7,15},{8,0},{9,1},... | collective-permute-start | bytes 147464 | tf_op jit(solution)/shard_map/ppermute | solution.py:161
  6.9 6.6 %collective-permute-start.5 = (bf16[64,384]{1,0:T(8,128)(2,1)S(1)}, bf16[64,384]{1,0:T(8,128)(2,1)S(1)}, u32[]{:S(2)}, u32[]{:S(2)}) collective-permute-start(bf16[64,384]{1,0:T(8,128)(2,1)S(1)} %get-tuple-element.26), channel_id=1, source_target_pairs={{0,12},{1,13},{2,14},{3,15},{4,8},{5,9},{6,10},{7,11},{8,4},{9,5},... | collective-permute-start | bytes 147464 | tf_op jit(solution)/shard_map/ppermute | solution.py:161
  6.9 8.2 %collective-permute-start = (bf16[64,768]{1,0:T(8,128)(2,1)S(1)}, bf16[64,768]{1,0:T(8,128)(2,1)S(1)}, u32[]{:S(2)}, u32[]{:S(2)}) collective-permute-start(bf16[64,768]{1,0:T(8,128)(2,1)S(1)} %get-tuple-element.20), channel_id=1, source_target_pairs={{0,4},{1,5},{2,6},{3,7},{4,0},{5,1},{6,2},{7,3},{8,12},{9,13},{10,... | collective-permute-start | bytes 294920 | tf_op jit(solution)/shard_map/ppermute | solution.py:161
  7.8 11.4 %collective-permute-start.1 = (bf16[64,768]{1,0:T(8,128)(2,1)S(1)}, bf16[64,768]{1,0:T(8,128)(2,1)S(1)}, u32[]{:S(2)}, u32[]{:S(2)}) collective-permute-start(bf16[64,768]{1,0:T(8,128)(2,1)S(1)} %get-tuple-element.21), channel_id=1, source_target_pairs={{0,8},{1,9},{2,10},{3,11},{4,12},{5,13},{6,14},{7,15},{8,0},{9,1},... | collective-permute-start | bytes 294920 | tf_op jit(solution)/shard_map/ppermute | solution.py:161
  11.3 7.8 %collective-permute-start.2 = (bf16[64,768]{1,0:T(8,128)(2,1)S(1)}, bf16[64,768]{1,0:T(8,128)(2,1)S(1)}, u32[]{:S(2)}, u32[]{:S(2)}) collective-permute-start(bf16[64,768]{1,0:T(8,128)(2,1)S(1)} %get-tuple-element.22), channel_id=1, source_target_pairs={{0,12},{1,13},{2,14},{3,15},{4,8},{5,9},{6,10},{7,11},{8,4},{9,5},... | collective-permute-start | bytes 294920 | tf_op jit(solution)/shard_map/ppermute | solution.py:161
  13.4 7.3 %collective-permute-start.6 = (bf16[256,384]{1,0:T(8,128)(2,1)S(1)}, bf16[256,384]{1,0:T(8,128)(2,1)S(1)}, u32[]{:S(2)}, u32[]{:S(2)}) collective-permute-start(bf16[256,384]{1,0:T(8,128)(2,1)S(1)} %constant_dynamic-update-slice_fusion.refs_4_), channel_id=1, source_target_pairs={{0,2},{1,3},{2,0},{3,1},{4,6},{5,7},{6,4},{7,5},{8,10},{9,11},{10,... | collective-permute-start | bytes 589832 | tf_op jit(solution)/shard_map/ppermute | solution.py:161
  19.2 5.7 %collective-permute-start.9 = (bf16[256,384]{1,0:T(8,128)(2,1)S(1)}, bf16[256,384]{1,0:T(8,128)(2,1)S(1)}, u32[]{:S(2)}, u32[]{:S(2)}) collective-permute-start(bf16[256,384]{1,0:T(8,128)(2,1)S(1)} %pad_maximum_fusion.refs_0_), channel_id=1, source_target_pairs={{0,2},{1,3},{2,0},{3,1},{4,6},{5,7},{6,4},{7,5},{8,10},{9,11},{10,... | collective-permute-start | bytes 589832 | tf_op jit(solution)/shard_map/ppermute | solution.py:161
  20.8 4.2 %collective-permute-start.7 = (bf16[256,384]{1,0:T(8,128)(2,1)S(1)}, bf16[256,384]{1,0:T(8,128)(2,1)S(1)}, u32[]{:S(2)}, u32[]{:S(2)}) collective-permute-start(bf16[256,384]{1,0:T(8,128)(2,1)S(1)} %constant_dynamic-update-slice_fusion.refs_4_), channel_id=1, source_target_pairs={{0,1},{1,0},{2,3},{3,2},{4,5},{5,4},{6,7},{7,6},{8,9},{9,8},{10,11... | collective-permute-start | bytes 589832 | tf_op jit(solution)/shard_map/ppermute | solution.py:161
  20.8 4.2 %collective-permute-start.8 = (bf16[256,384]{1,0:T(8,128)(2,1)S(1)}, bf16[256,384]{1,0:T(8,128)(2,1)S(1)}, u32[]{:S(2)}, u32[]{:S(2)}) collective-permute-start(bf16[256,384]{1,0:T(8,128)(2,1)S(1)} %collective-permute-done.6.refs_5_), channel_id=1, source_target_pairs={{0,1},{1,0},{2,3},{3,2},{4,5},{5,4},{6,7},{7,6},{8,9},{9,8},{10,11... | collective-permute-start | bytes 589832 | tf_op jit(solution)/shard_map/ppermute | solution.py:161
  21.3 4.8 %collective-permute-start.10 = (bf16[256,384]{1,0:T(8,128)(2,1)S(1)}, bf16[256,384]{1,0:T(8,128)(2,1)S(1)}, u32[]{:S(2)}, u32[]{:S(2)}) collective-permute-start(bf16[256,384]{1,0:T(8,128)(2,1)S(1)} %pad_maximum_fusion.refs_0_), channel_id=1, source_target_pairs={{0,1},{1,0},{2,3},{3,2},{4,5},{5,4},{6,7},{7,6},{8,9},{9,8},{10,11... | collective-permute-start | bytes 589832 | tf_op jit(solution)/shard_map/ppermute | solution.py:161
  24.9 1.4 %collective-permute-start.11 = (bf16[256,384]{1,0:T(8,128)(2,1)S(1)}, bf16[256,384]{1,0:T(8,128)(2,1)S(1)}, u32[]{:S(2)}, u32[]{:S(2)}) collective-permute-start(bf16[256,384]{1,0:T(8,128)(2,1)S(1)} %collective-permute-done.9.refs_1_), channel_id=1, source_target_pairs={{0,1},{1,0},{2,3},{3,2},{4,5},{5,4},{6,7},{7,6},{8,9},{9,8},{10,11... | collective-permute-start | bytes 589832 | tf_op jit(solution)/shard_map/ppermute | solution.py:161
  26.9 6.9 %collective-permute-start.12 = (bf16[64,384]{1,0:T(8,128)(2,1)S(1)}, bf16[64,384]{1,0:T(8,128)(2,1)S(1)}, u32[]{:S(2)}, u32[]{:S(2)}) collective-permute-start(bf16[64,384]{1,0:T(8,128)(2,1)S(1)} %get-tuple-element.29), channel_id=1, source_target_pairs={{0,16},{1,17},{2,18},{3,19},{4,20},{5,21},{6,22},{7,23},{8,24},{9,... | collective-permute-start | bytes 147464 | tf_op jit(solution)/shard_map/ppermute | solution.py:191
  28.5 5.3 %collective-permute-start.13 = (bf16[64,384]{1,0:T(8,128)(2,1)S(1)}, bf16[64,384]{1,0:T(8,128)(2,1)S(1)}, u32[]{:S(2)}, u32[]{:S(2)}) collective-permute-start(bf16[64,384]{1,0:T(8,128)(2,1)S(1)} %get-tuple-element.30), channel_id=1, source_target_pairs={{0,20},{1,21},{2,22},{3,23},{4,16},{5,17},{6,18},{7,19},{8,28},{9,... | collective-permute-start | bytes 147464 | tf_op jit(solution)/shard_map/ppermute | solution.py:191
  30.5 7.1 %collective-permute-start.14 = (bf16[64,384]{1,0:T(8,128)(2,1)S(1)}, bf16[64,384]{1,0:T(8,128)(2,1)S(1)}, u32[]{:S(2)}, u32[]{:S(2)}) collective-permute-start(bf16[64,384]{1,0:T(8,128)(2,1)S(1)} %get-tuple-element.31), channel_id=1, source_target_pairs={{0,24},{1,25},{2,26},{3,27},{4,28},{5,29},{6,30},{7,31},{8,16},{9,... | collective-permute-start | bytes 147464 | tf_op jit(solution)/shard_map/ppermute | solution.py:191
  32.0 6.9 %collective-permute-start.15 = (bf16[64,384]{1,0:T(8,128)(2,1)S(1)}, bf16[64,384]{1,0:T(8,128)(2,1)S(1)}, u32[]{:S(2)}, u32[]{:S(2)}) collective-permute-start(bf16[64,384]{1,0:T(8,128)(2,1)S(1)} %get-tuple-element.32), channel_id=1, source_target_pairs={{0,28},{1,29},{2,30},{3,31},{4,24},{5,25},{6,26},{7,27},{8,20},{9,... | collective-permute-start | bytes 147464 | tf_op jit(solution)/shard_map/ppermute | solution.py:191

commit v3 on v2

--- a/solution.py
+++ b/solution.py
@@ -164,18 +164,33 @@
         far = [swap(pieces[s], s * inner) for s in range(groups - 1, 0, -1)]
         return [pieces[0]] + far[::-1]
 
-    def gather(block):
-        blocks, bits = [block], inner // 2
-        while bits:
+    def gather(parts):
+        blocks, bits = list(parts), inner // 2
+        while bits > 1:
             blocks = blocks + [swap(block, bits) for block in blocks]
             bits //= 2
         return blocks
 
+    def with_other_core(blocks):
+        return blocks + [swap(block, 1) for block in blocks] if inner > 1 else blocks
+
     width = queries.shape[2] // groups
     first, second = split_heads(queries, key_value, groups, inner)
     first, second = exchange(first), exchange(second)
-    key_blocks = gather(jnp.concatenate(first, axis=0))
-    value_blocks = gather(jnp.concatenate([piece[:, :width] for piece in second], axis=0))
+    key_blocks = with_other_core(
+        [jnp.concatenate(gather([jnp.concatenate(first, axis=0)]), axis=0)]
+    )
+    values = [piece[:, :width] for piece in second]
+    near, far = values[: groups // 2], values[groups // 2 :]
+    parts = [jnp.concatenate(some, axis=0) for some in (near, far) if some]
+    blocks = gather(parts)
+    count = len(parts)
+    value_blocks = with_other_core(
+        [
+            jnp.concatenate(blocks[i : i + count], axis=0)
+            for i in range(0, len(blocks), count)
+        ]
+    )
     weights, sums = weigh(second, key_blocks, width)
     attended = average(weights, sums, value_blocks, groups)
 
@@ -190,7 +205,7 @@
         ]
         return lax.ppermute(value, ("segment", "seq"), pairs)
 
-    handed = [hand(attended[s], s) for s in range(groups - 1, -1, -1)][::-1]
+    handed = [hand(attended[s], s) for s in range(groups)]
     return join_heads(handed, inner)
 
 

time: 39.8 us -> 38.7 us (0.972)
  waiting for transfers between devices: 15.1 us -> 13.2 us
  starting transfers between devices: 20.7 us -> 21.4 us
    ppermute x12, waiting for transfers between devices: 10 us -> 8.13 us  [swap(): return lax.ppermute(value, 'seq', [(i, i ^ bits) for i in range(places)])]
    ppermute x12, starting transfers between devices: 13.8 us -> 14.6 us  [swap(): return lax.ppermute(value, 'seq', [(i, i ^ bits) for i in range(places)])]
  transfers between devices with their start and end apart: 16 -> 16, of which waited for: 6 -> 6; matrix products, arithmetic and copies ran while one was open for 0% -> 1% of each run, Pallas kernels for 3% -> 3%
where the time goes in v3:
time: 38.7 us; the launch traced here: 38.5 us
  starting transfers between devices  21.4 us (55%)
  waiting for transfers between devices  13.2 us (34%)
  Pallas kernels  3.58 us (9%)
    ppermute x12, starting transfers between devices, swap(): return lax.ppermute(value, 'seq', [(i, i ^ bits) for i in range(places)])  14.6 us
    ppermute x12, waiting for transfers between devices, swap(): return lax.ppermute(value, 'seq', [(i, i ^ bits) for i in range(places)])  8.13 us
    ppermute x4, starting transfers between devices, hand(): return lax.ppermute(value, ('segment', 'seq'), pairs)  6.81 us
    ppermute x4, waiting for transfers between devices, hand(): return lax.ppermute(value, ('segment', 'seq'), pairs)  5.04 us
    pallas_call x1, Pallas kernels, split_heads(): pl.pallas_call(kernel, out_shape=[jax.ShapeDtypeStruct((rows, width), que...  1.17 us
    pallas_call x1, Pallas kernels, weigh(): pl.pallas_call(kernel, out_shape=[jax.ShapeDtypeStruct((heads, groups * r...  1.15 us
  transfers between devices with their start and end apart: 16, of which 6 were waited for; matrix products, arithmetic and copies ran while one was open for 1% of the time, Pallas kernels for 3%

profile of v3, /device:TPU:0, one launch (start us, length us, event | category | flops | bytes accessed | tf_op | source)
XLA Modules:
  0.0 38.5 jit_solution(629034432262114955)
XLA Ops:
  0.0 1.2 %split_heads.1 = (bf16[64,384]{1,0:T(8,128)(2,1)S(1)}, bf16[64,384]{1,0:T(8,128)(2,1)S(1)}, bf16[64,384]{1,0:T(8,128)(2,1)S(1)}, bf16[64,384]{1,0:T(8,128)(2,1)S...) custom-call(bf16[1,64,1536]{2,1,0:T(8,128)(2,1)} %q_ref.1, ...), custom_call_target="tpu_custom_call" | custom-call | tf_op jit(solution)/shard_map/split_heads/pallas_call | solution.py:53
  1.2 3.1 %collective-permute-start.3 = (bf16[64,384]{1,0:T(8,128)(2,1)S(1)}, bf16[64,384]{1,0:T(8,128)(2,1)S(1)}, u32[]{:S(2)}, u32[]{:S(2)}) collective-permute-start(bf16[64,384]{1,0:T(8,128)(2,1)S(1)} %get-tuple-element.24), channel_id=1, source_target_pairs={{0,4},{1,5},{2,6},{3,7},{4,0},{5,1},{6,2},{7,3},{8,12},{9,13},{10,... | collective-permute-start | bytes 147464 | tf_op jit(solution)/shard_map/ppermute | solution.py:161
  4.3 2.6 %collective-permute-start.4 = (bf16[64,384]{1,0:T(8,128)(2,1)S(1)}, bf16[64,384]{1,0:T(8,128)(2,1)S(1)}, u32[]{:S(2)}, u32[]{:S(2)}) collective-permute-start(bf16[64,384]{1,0:T(8,128)(2,1)S(1)} %get-tuple-element.25), channel_id=1, source_target_pairs={{0,8},{1,9},{2,10},{3,11},{4,12},{5,13},{6,14},{7,15},{8,0},{9,1},... | collective-permute-start | bytes 147464 | tf_op jit(solution)/shard_map/ppermute | solution.py:161
  6.9 0.0 collective-permute-start.5
  6.9 0.9 %collective-permute-start = (bf16[64,768]{1,0:T(8,128)(2,1)S(1)}, bf16[64,768]{1,0:T(8,128)(2,1)S(1)}, u32[]{:S(2)}, u32[]{:S(2)}) collective-permute-start(bf16[64,768]{1,0:T(8,128)(2,1)S(1)} %get-tuple-element.20), channel_id=1, source_target_pairs={{0,4},{1,5},{2,6},{3,7},{4,0},{5,1},{6,2},{7,3},{8,12},{9,13},{10,... | collective-permute-start | bytes 294920 | tf_op jit(solution)/shard_map/ppermute | solution.py:161
  7.8 3.5 %collective-permute-start.1 = (bf16[64,768]{1,0:T(8,128)(2,1)S(1)}, bf16[64,768]{1,0:T(8,128)(2,1)S(1)}, u32[]{:S(2)}, u32[]{:S(2)}) collective-permute-start(bf16[64,768]{1,0:T(8,128)(2,1)S(1)} %get-tuple-element.21), channel_id=1, source_target_pairs={{0,8},{1,9},{2,10},{3,11},{4,12},{5,13},{6,14},{7,15},{8,0},{9,1},... | collective-permute-start | bytes 294920 | tf_op jit(solution)/shard_map/ppermute | solution.py:161
  11.3 0.0 collective-permute-done.3
  11.3 0.1 collective-permute-start.2
  11.3 0.0 collective-permute-done.4
  11.4 2.1 %collective-permute-done.5 = bf16[64,384]{1,0:T(8,128)(2,1)S(1)} collective-permute-done((bf16[64,384]{1,0:T(8,128)(2,1)S(1)}, bf16[64,384]{1,0:T(8,128)(2,1)S(1)}, u32[]{:S(2)}, u32[]{:S(2)}) %collective-permute-start.5) | collective-permute-done | bytes 49184 | tf_op jit(solution)/shard_map/ppermute | solution.py:161
  13.5 1.6 %collective-permute-start.6 = (bf16[256,384]{1,0:T(8,128)(2,1)S(1)}, bf16[256,384]{1,0:T(8,128)(2,1)S(1)}, u32[]{:S(2)}, u32[]{:S(2)}) collective-permute-start(bf16[256,384]{1,0:T(8,128)(2,1)S(1)} %pad_maximum_fusion), channel_id=1, source_target_pairs={{0,2},{1,3},{2,0},{3,1},{4,6},{5,7},{6,4},{7,5},{8,10},{9,11},{10,... | collective-permute-start | bytes 589832 | tf_op jit(solution)/shard_map/ppermute | solution.py:161
  15.1 0.0 collective-permute-done.refs_1_
  15.1 0.6 %collective-permute-start.8 = (bf16[128,384]{1,0:T(8,128)(2,1)S(1)}, bf16[128,384]{1,0:T(8,128)(2,1)S(1)}, u32[]{:S(2)}, u32[]{:S(2)}) collective-permute-start(bf16[128,384]{1,0:T(8,128)(2,1)S(1)} %pad_maximum_fusion.2), channel_id=1, source_target_pairs={{0,2},{1,3},{2,0},{3,1},{4,6},{5,7},{6,4},{7,5},{8,10},{9,11},{10,... | collective-permute-start | bytes 294920 | tf_op jit(solution)/shard_map/ppermute | solution.py:161
  15.7 3.4 %collective-permute-done.1.refs_2_ = bf16[64,768]{1,0:T(8,128)(2,1)S(1)} collective-permute-done((bf16[64,768]{1,0:T(8,128)(2,1)S(1)}, bf16[64,768]{1,0:T(8,128)(2,1)S(1)}, u32[]{:S(2)}, u32[]{:S(2)}) %collective-permute-start.1) | collective-permute-done | bytes 98336 | tf_op jit(solution)/shard_map/ppermute | solution.py:161
  19.1 0.0 collective-permute-done.2.refs_3_
  19.2 1.6 %collective-permute-start.9 = (bf16[128,384]{1,0:T(8,128)(2,1)S(1)}, bf16[128,384]{1,0:T(8,128)(2,1)S(1)}, u32[]{:S(2)}, u32[]{:S(2)}) collective-permute-start(bf16[128,384]{1,0:T(8,128)(2,1)S(1)} %pad_maximum_fusion.3), channel_id=1, source_target_pairs={{0,2},{1,3},{2,0},{3,1},{4,6},{5,7},{6,4},{7,5},{8,10},{9,11},{10,... | collective-permute-start | bytes 294920 | tf_op jit(solution)/shard_map/ppermute | solution.py:161
  20.8 0.1 collective-permute-start.10
  20.8 0.0 collective-permute-done.6
  20.9 0.5 %collective-permute-start.7 = (bf16[512,384]{1,0:T(8,128)(2,1)S(1)}, bf16[512,384]{1,0:T(8,128)(2,1)S(1)}, u32[]{:S(2)}, u32[]{:S(2)}) collective-permute-start(bf16[512,384]{1,0:T(8,128)(2,1)S(1)} %constant_dynamic-update-slice_fusion.refs_4_), channel_id=1, source_target_pairs={{0,1},{1,0},{2,3},{3,2},{4,5},{5,4},{6,7},{7,6},{8,9},{9,8},{10,11... | collective-permute-start | bytes 1179656 | tf_op jit(solution)/shard_map/ppermute | solution.py:161
  21.4 0.0 collective-permute-done.8
  21.5 2.4 %collective-permute-done.9 = bf16[128,384]{1,0:T(8,128)(2,1)S(1)} collective-permute-done((bf16[128,384]{1,0:T(8,128)(2,1)S(1)}, bf16[128,384]{1,0:T(8,128)(2,1)S(1)}, u32[]{:S(2)}, u32[]{:S(2)}) %collective-permute-start.9) | collective-permute-done | bytes 98336 | tf_op jit(solution)/shard_map/ppermute | solution.py:161
  23.9 0.1 collective-permute-start.11
  23.9 0.0 collective-permute-done.7.refs_5_
  23.9 1.1 %weigh.1 = (bf16[3,256,1024]{2,1,0:T(8,128)(2,1)S(1)}, f32[256,128]{1,0:T(8,128)S(1)}) custom-call(bf16[64,768]{1,0:T(8,128)(2,1)S(1)} %get-tuple-element.19.refs_0_, bf16[64,768]{1,0:T(8,128)(2,1)S(1)} %collective-permute-done.refs_1_, bf16[64,768]{1,0:T(8,128)(2,1)S(1)} %collective-permute-done.1.refs_2_, ...), custom_call_target="tpu_custom_call" | custom-call | tf_op jit(solution)/shard_map/weigh/pallas_call | solution.py:90
  25.1 0.0 collective-permute-done.10.refs_2_
  25.1 0.3 collective-permute-done.11.refs_3_
  25.4 0.6 %average.1 = (bf16[64,384]{1,0:T(8,128)(2,1)S(1)}, bf16[64,384]{1,0:T(8,128)(2,1)S(1)}, bf16[64,384]{1,0:T(8,128)(2,1)S(1)}, bf16[64,384]{1,0:T(8,128)(2,1)S(1)}) custom-call(bf16[3,256,1024]{2,1,0:T(8,128)(2,1)S(1)} %get-tuple-element.27.weights_ref, f32[256,128]{1,0:T(8,128)S(1)} %get-tuple-element.28.sums_ref, ...), custom_call_target="tpu_custom_call" | custom-call | tf_op jit(solution)/shard_map/average/pallas_call | solution.py:118
  25.9 1.6 %collective-permute-start.12 = (bf16[64,384]{1,0:T(8,128)(2,1)S(1)}, bf16[64,384]{1,0:T(8,128)(2,1)S(1)}, u32[]{:S(2)}, u32[]{:S(2)}) collective-permute-start(bf16[64,384]{1,0:T(8,128)(2,1)S(1)} %get-tuple-element.29), channel_id=1, source_target_pairs={{0,16},{1,17},{2,18},{3,19},{4,20},{5,21},{6,22},{7,23},{8,24},{9,... | collective-permute-start | bytes 147464 | tf_op jit(solution)/shard_map/ppermute | solution.py:206
  27.5 1.7 %collective-permute-start.13 = (bf16[64,384]{1,0:T(8,128)(2,1)S(1)}, bf16[64,384]{1,0:T(8,128)(2,1)S(1)}, u32[]{:S(2)}, u32[]{:S(2)}) collective-permute-start(bf16[64,384]{1,0:T(8,128)(2,1)S(1)} %get-tuple-element.30), channel_id=1, source_target_pairs={{0,20},{1,21},{2,22},{3,23},{4,16},{5,17},{6,18},{7,19},{8,28},{9,... | collective-permute-start | bytes 147464 | tf_op jit(solution)/shard_map/ppermute | solution.py:206
  29.2 1.8 %collective-permute-start.14 = (bf16[64,384]{1,0:T(8,128)(2,1)S(1)}, bf16[64,384]{1,0:T(8,128)(2,1)S(1)}, u32[]{:S(2)}, u32[]{:S(2)}) collective-permute-start(bf16[64,384]{1,0:T(8,128)(2,1)S(1)} %get-tuple-element.31), channel_id=1, source_target_pairs={{0,24},{1,25},{2,26},{3,27},{4,28},{5,29},{6,30},{7,31},{8,16},{9,... | collective-permute-start | bytes 147464 | tf_op jit(solution)/shard_map/ppermute | solution.py:206
  31.0 1.7 %collective-permute-start.15 = (bf16[64,384]{1,0:T(8,128)(2,1)S(1)}, bf16[64,384]{1,0:T(8,128)(2,1)S(1)}, u32[]{:S(2)}, u32[]{:S(2)}) collective-permute-start(bf16[64,384]{1,0:T(8,128)(2,1)S(1)} %get-tuple-element.32), channel_id=1, source_target_pairs={{0,28},{1,29},{2,30},{3,31},{4,24},{5,25},{6,26},{7,27},{8,20},{9,... | collective-permute-start | bytes 147464 | tf_op jit(solution)/shard_map/ppermute | solution.py:206
  32.7 0.0 collective-permute-done.12.refs_0_
  32.8 0.0 collective-permute-done.13.refs_1_
  32.8 2.9 %collective-permute-done.14.refs_2_ = bf16[64,384]{1,0:T(8,128)(2,1)S(1)} collective-permute-done((bf16[64,384]{1,0:T(8,128)(2,1)S(1)}, bf16[64,384]{1,0:T(8,128)(2,1)S(1)}, u32[]{:S(2)}, u32[]{:S(2)}) %collective-permute-start.14) | collective-permute-done | bytes 49184 | tf_op jit(solution)/shard_map/ppermute | solution.py:206
  35.7 2.1 %collective-permute-done.15.refs_3_ = bf16[64,384]{1,0:T(8,128)(2,1)S(1)} collective-permute-done((bf16[64,384]{1,0:T(8,128)(2,1)S(1)}, bf16[64,384]{1,0:T(8,128)(2,1)S(1)}, u32[]{:S(2)}, u32[]{:S(2)}) %collective-permute-start.15) | collective-permute-done | bytes 49184 | tf_op jit(solution)/shard_map/ppermute | solution.py:206
  37.8 0.7 %join_heads.1 = bf16[1,64,1536]{2,1,0:T(8,128)(2,1)} custom-call(bf16[64,384]{1,0:T(8,128)(2,1)S(1)} %collective-permute-done.12.refs_0_, bf16[64,384]{1,0:T(8,128)(2,1)S(1)} %collective-permute-done.13.refs_1_, bf16[64,384]{1,0:T(8,128)(2,1)S(1)} %collective-permute-done.14.refs_2_, bf16[64,384]{1,0:T(8,128)(2,1)S(1)} %collective-permute-done.15.refs_3_), custom_call_target="tpu_custom_call" | custom-call | tf_op jit(solution)/shard_map/join_heads/pallas_call | solution.py:142
  (15 shorter events, 0.2 us)
Async XLA Ops:
  1.2 10.1 %collective-permute-start.3 = (bf16[64,384]{1,0:T(8,128)(2,1)S(1)}, bf16[64,384]{1,0:T(8,128)(2,1)S(1)}, u32[]{:S(2)}, u32[]{:S(2)}) collective-permute-start(bf16[64,384]{1,0:T(8,128)(2,1)S(1)} %get-tuple-element.24), channel_id=1, source_target_pairs={{0,4},{1,5},{2,6},{3,7},{4,0},{5,1},{6,2},{7,3},{8,12},{9,13},{10,... | collective-permute-start | bytes 147464 | tf_op jit(solution)/shard_map/ppermute | solution.py:161
  4.3 7.1 %collective-permute-start.4 = (bf16[64,384]{1,0:T(8,128)(2,1)S(1)}, bf16[64,384]{1,0:T(8,128)(2,1)S(1)}, u32[]{:S(2)}, u32[]{:S(2)}) collective-permute-start(bf16[64,384]{1,0:T(8,128)(2,1)S(1)} %get-tuple-element.25), channel_id=1, source_target_pairs={{0,8},{1,9},{2,10},{3,11},{4,12},{5,13},{6,14},{7,15},{8,0},{9,1},... | collective-permute-start | bytes 147464 | tf_op jit(solution)/shard_map/ppermute | solution.py:161
  6.9 6.6 %collective-permute-start.5 = (bf16[64,384]{1,0:T(8,128)(2,1)S(1)}, bf16[64,384]{1,0:T(8,128)(2,1)S(1)}, u32[]{:S(2)}, u32[]{:S(2)}) collective-permute-start(bf16[64,384]{1,0:T(8,128)(2,1)S(1)} %get-tuple-element.26), channel_id=1, source_target_pairs={{0,12},{1,13},{2,14},{3,15},{4,8},{5,9},{6,10},{7,11},{8,4},{9,5},... | collective-permute-start | bytes 147464 | tf_op jit(solution)/shard_map/ppermute | solution.py:161
  6.9 8.2 %collective-permute-start = (bf16[64,768]{1,0:T(8,128)(2,1)S(1)}, bf16[64,768]{1,0:T(8,128)(2,1)S(1)}, u32[]{:S(2)}, u32[]{:S(2)}) collective-permute-start(bf16[64,768]{1,0:T(8,128)(2,1)S(1)} %get-tuple-element.20), channel_id=1, source_target_pairs={{0,4},{1,5},{2,6},{3,7},{4,0},{5,1},{6,2},{7,3},{8,12},{9,13},{10,... | collective-permute-start | bytes 294920 | tf_op jit(solution)/shard_map/ppermute | solution.py:161
  7.8 11.4 %collective-permute-start.1 = (bf16[64,768]{1,0:T(8,128)(2,1)S(1)}, bf16[64,768]{1,0:T(8,128)(2,1)S(1)}, u32[]{:S(2)}, u32[]{:S(2)}) collective-permute-start(bf16[64,768]{1,0:T(8,128)(2,1)S(1)} %get-tuple-element.21), channel_id=1, source_target_pairs={{0,8},{1,9},{2,10},{3,11},{4,12},{5,13},{6,14},{7,15},{8,0},{9,1},... | collective-permute-start | bytes 294920 | tf_op jit(solution)/shard_map/ppermute | solution.py:161
  11.3 7.8 %collective-permute-start.2 = (bf16[64,768]{1,0:T(8,128)(2,1)S(1)}, bf16[64,768]{1,0:T(8,128)(2,1)S(1)}, u32[]{:S(2)}, u32[]{:S(2)}) collective-permute-start(bf16[64,768]{1,0:T(8,128)(2,1)S(1)} %get-tuple-element.22), channel_id=1, source_target_pairs={{0,12},{1,13},{2,14},{3,15},{4,8},{5,9},{6,10},{7,11},{8,4},{9,5},... | collective-permute-start | bytes 294920 | tf_op jit(solution)/shard_map/ppermute | solution.py:161
  13.5 7.4 %collective-permute-start.6 = (bf16[256,384]{1,0:T(8,128)(2,1)S(1)}, bf16[256,384]{1,0:T(8,128)(2,1)S(1)}, u32[]{:S(2)}, u32[]{:S(2)}) collective-permute-start(bf16[256,384]{1,0:T(8,128)(2,1)S(1)} %pad_maximum_fusion), channel_id=1, source_target_pairs={{0,2},{1,3},{2,0},{3,1},{4,6},{5,7},{6,4},{7,5},{8,10},{9,11},{10,... | collective-permute-start | bytes 589832 | tf_op jit(solution)/shard_map/ppermute | solution.py:161
  15.1 6.3 %collective-permute-start.8 = (bf16[128,384]{1,0:T(8,128)(2,1)S(1)}, bf16[128,384]{1,0:T(8,128)(2,1)S(1)}, u32[]{:S(2)}, u32[]{:S(2)}) collective-permute-start(bf16[128,384]{1,0:T(8,128)(2,1)S(1)} %pad_maximum_fusion.2), channel_id=1, source_target_pairs={{0,2},{1,3},{2,0},{3,1},{4,6},{5,7},{6,4},{7,5},{8,10},{9,11},{10,... | collective-permute-start | bytes 294920 | tf_op jit(solution)/shard_map/ppermute | solution.py:161
  19.2 4.7 %collective-permute-start.9 = (bf16[128,384]{1,0:T(8,128)(2,1)S(1)}, bf16[128,384]{1,0:T(8,128)(2,1)S(1)}, u32[]{:S(2)}, u32[]{:S(2)}) collective-permute-start(bf16[128,384]{1,0:T(8,128)(2,1)S(1)} %pad_maximum_fusion.3), channel_id=1, source_target_pairs={{0,2},{1,3},{2,0},{3,1},{4,6},{5,7},{6,4},{7,5},{8,10},{9,11},{10,... | collective-permute-start | bytes 294920 | tf_op jit(solution)/shard_map/ppermute | solution.py:161
  20.8 4.3 %collective-permute-start.10 = (bf16[256,384]{1,0:T(8,128)(2,1)S(1)}, bf16[256,384]{1,0:T(8,128)(2,1)S(1)}, u32[]{:S(2)}, u32[]{:S(2)}) collective-permute-start(bf16[256,384]{1,0:T(8,128)(2,1)S(1)} %pad_maximum_fusion.1.refs_0_), channel_id=1, source_target_pairs={{0,1},{1,0},{2,3},{3,2},{4,5},{5,4},{6,7},{7,6},{8,9},{9,8},{10,11... | collective-permute-start | bytes 589832 | tf_op jit(solution)/shard_map/ppermute | solution.py:161
  20.9 3.0 %collective-permute-start.7 = (bf16[512,384]{1,0:T(8,128)(2,1)S(1)}, bf16[512,384]{1,0:T(8,128)(2,1)S(1)}, u32[]{:S(2)}, u32[]{:S(2)}) collective-permute-start(bf16[512,384]{1,0:T(8,128)(2,1)S(1)} %constant_dynamic-update-slice_fusion.refs_4_), channel_id=1, source_target_pairs={{0,1},{1,0},{2,3},{3,2},{4,5},{5,4},{6,7},{7,6},{8,9},{9,8},{10,11... | collective-permute-start | bytes 1179656 | tf_op jit(solution)/shard_map/ppermute | solution.py:161
  23.9 1.5 %collective-permute-start.11 = (bf16[256,384]{1,0:T(8,128)(2,1)S(1)}, bf16[256,384]{1,0:T(8,128)(2,1)S(1)}, u32[]{:S(2)}, u32[]{:S(2)}) collective-permute-start(bf16[256,384]{1,0:T(8,128)(2,1)S(1)} %constant_dynamic-update-slice_fusion.5.refs_1_), channel_id=1, source_target_pairs={{0,1},{1,0},{2,3},{3,2},{4,5},{5,4},{6,7},{7,6},{8,9},{9,8},{10,11... | collective-permute-start | bytes 589832 | tf_op jit(solution)/shard_map/ppermute | solution.py:161
  25.9 6.8 %collective-permute-start.12 = (bf16[64,384]{1,0:T(8,128)(2,1)S(1)}, bf16[64,384]{1,0:T(8,128)(2,1)S(1)}, u32[]{:S(2)}, u32[]{:S(2)}) collective-permute-start(bf16[64,384]{1,0:T(8,128)(2,1)S(1)} %get-tuple-element.29), channel_id=1, source_target_pairs={{0,16},{1,17},{2,18},{3,19},{4,20},{5,21},{6,22},{7,23},{8,24},{9,... | collective-permute-start | bytes 147464 | tf_op jit(solution)/shard_map/ppermute | solution.py:206
  27.5 5.3 %collective-permute-start.13 = (bf16[64,384]{1,0:T(8,128)(2,1)S(1)}, bf16[64,384]{1,0:T(8,128)(2,1)S(1)}, u32[]{:S(2)}, u32[]{:S(2)}) collective-permute-start(bf16[64,384]{1,0:T(8,128)(2,1)S(1)} %get-tuple-element.30), channel_id=1, source_target_pairs={{0,20},{1,21},{2,22},{3,23},{4,16},{5,17},{6,18},{7,19},{8,28},{9,... | collective-permute-start | bytes 147464 | tf_op jit(solution)/shard_map/ppermute | solution.py:206
  29.2 6.5 %collective-permute-start.14 = (bf16[64,384]{1,0:T(8,128)(2,1)S(1)}, bf16[64,384]{1,0:T(8,128)(2,1)S(1)}, u32[]{:S(2)}, u32[]{:S(2)}) collective-permute-start(bf16[64,384]{1,0:T(8,128)(2,1)S(1)} %get-tuple-element.31), channel_id=1, source_target_pairs={{0,24},{1,25},{2,26},{3,27},{4,28},{5,29},{6,30},{7,31},{8,16},{9,... | collective-permute-start | bytes 147464 | tf_op jit(solution)/shard_map/ppermute | solution.py:206
  31.0 6.8 %collective-permute-start.15 = (bf16[64,384]{1,0:T(8,128)(2,1)S(1)}, bf16[64,384]{1,0:T(8,128)(2,1)S(1)}, u32[]{:S(2)}, u32[]{:S(2)}) collective-permute-start(bf16[64,384]{1,0:T(8,128)(2,1)S(1)} %get-tuple-element.32), channel_id=1, source_target_pairs={{0,28},{1,29},{2,30},{3,31},{4,24},{5,25},{6,26},{7,27},{8,20},{9,... | collective-permute-start | bytes 147464 | tf_op jit(solution)/shard_map/ppermute | solution.py:206

commit v4 on v3

--- a/solution.py
+++ b/solution.py
@@ -100,29 +100,30 @@
     )(*query_pieces, *key_blocks)
 
 
-def average(weights, sums, value_blocks, groups):
+def average(weights, sums, value_blocks, groups, first, last, after):
     heads, queries, keys = weights.shape
     rows = queries // groups
     blocks = len(value_blocks)
 
     def kernel(weights_ref, sums_ref, *refs):
-        value_refs, out_refs = refs[:blocks], refs[blocks:]
+        value_refs, out_refs = refs[:blocks], refs[blocks + len(after) :]
+        some = slice(first * rows, last * rows)
         for head in range(heads):
             cols = slice(head * HD, (head + 1) * HD)
             v = jnp.concatenate([ref[:, cols] for ref in value_refs], axis=0)
-            total = jnp.dot(weights_ref[head], v, preferred_element_type=jnp.float32)
-            out = (total / sums_ref[:, head : head + 1]).astype(jnp.bfloat16)
+            total = jnp.dot(weights_ref[head, some], v, preferred_element_type=jnp.float32)
+            out = (total / sums_ref[some, head : head + 1]).astype(jnp.bfloat16)
             for step, ref in enumerate(out_refs):
                 ref[:, cols] = out[step * rows : (step + 1) * rows]
 
     return pl.pallas_call(
         kernel,
-        out_shape=[jax.ShapeDtypeStruct((rows, heads * HD), jnp.bfloat16)] * groups,
-        in_specs=[VMEM] * (2 + blocks),
-        out_specs=[VMEM] * groups,
+        out_shape=[jax.ShapeDtypeStruct((rows, heads * HD), jnp.bfloat16)] * (last - first),
+        in_specs=[VMEM] * (2 + blocks) + [pl.BlockSpec(memory_space=pl.ANY)] * len(after),
+        out_specs=[VMEM] * (last - first),
         name="average",
         compiler_params=PARAMS,
-    )(weights, sums, *value_blocks)
+    )(weights, sums, *value_blocks, *after)
 
 
 def join_heads(pieces, inner):
@@ -192,7 +193,8 @@
         ]
     )
     weights, sums = weigh(second, key_blocks, width)
-    attended = average(weights, sums, value_blocks, groups)
+    own = average(weights, sums, value_blocks, groups, 0, 1, [])
+    attended = own + average(weights, sums, value_blocks, groups, 1, groups, own)
 
     def hand(value, step):
         pairs = [

time: 38.7 us -> 38 us (0.982)
  waiting for transfers between devices: 13.2 us -> 12.3 us
    ppermute x4, waiting for transfers between devices: 5.04 us -> 4.2 us  [hand(): return lax.ppermute(value, ('segment', 'seq'), pairs)]
  transfers between devices with their start and end apart: 16 -> 16, of which waited for: 6 -> 7; matrix products, arithmetic and copies ran while one was open for 1% -> 1% of each run, Pallas kernels for 3% -> 3%
where the time goes in v4:
time: 38 us; the launch traced here: 37.8 us
  starting transfers between devices  21.4 us (56%)
  waiting for transfers between devices  12.3 us (32%)
  Pallas kernels  3.74 us (10%)
    ppermute x12, starting transfers between devices, swap(): return lax.ppermute(value, 'seq', [(i, i ^ bits) for i in range(places)])  14.6 us
    ppermute x12, waiting for transfers between devices, swap(): return lax.ppermute(value, 'seq', [(i, i ^ bits) for i in range(places)])  8.13 us
    ppermute x4, starting transfers between devices, hand(): return lax.ppermute(value, ('segment', 'seq'), pairs)  6.81 us
    ppermute x4, waiting for transfers between devices, hand(): return lax.ppermute(value, ('segment', 'seq'), pairs)  4.2 us
    pallas_call x1, Pallas kernels, split_heads(): pl.pallas_call(kernel, out_shape=[jax.ShapeDtypeStruct((rows, width), que...  1.17 us
    pallas_call x1, Pallas kernels, weigh(): pl.pallas_call(kernel, out_shape=[jax.ShapeDtypeStruct((heads, groups * r...  1.15 us
  transfers between devices with their start and end apart: 16, of which 7 were waited for; matrix products, arithmetic and copies ran while one was open for 1% of the time, Pallas kernels for 3%

profile of v4, /device:TPU:0, one launch (start us, length us, event | category | flops | bytes accessed | tf_op | source)
XLA Modules:
  0.0 37.8 jit_solution(13467416119046536202)
XLA Ops:
  0.0 1.2 %split_heads.1 = (bf16[64,384]{1,0:T(8,128)(2,1)S(1)}, bf16[64,384]{1,0:T(8,128)(2,1)S(1)}, bf16[64,384]{1,0:T(8,128)(2,1)S(1)}, bf16[64,384]{1,0:T(8,128)(2,1)S...) custom-call(bf16[1,64,1536]{2,1,0:T(8,128)(2,1)} %q_ref.1, ...), custom_call_target="tpu_custom_call" | custom-call | tf_op jit(solution)/shard_map/split_heads/pallas_call | solution.py:53
  1.2 3.1 %collective-permute-start.3 = (bf16[64,384]{1,0:T(8,128)(2,1)S(1)}, bf16[64,384]{1,0:T(8,128)(2,1)S(1)}, u32[]{:S(2)}, u32[]{:S(2)}) collective-permute-start(bf16[64,384]{1,0:T(8,128)(2,1)S(1)} %get-tuple-element.23), channel_id=1, source_target_pairs={{0,4},{1,5},{2,6},{3,7},{4,0},{5,1},{6,2},{7,3},{8,12},{9,13},{10,... | collective-permute-start | bytes 147464 | tf_op jit(solution)/shard_map/ppermute | solution.py:162
  4.3 2.6 %collective-permute-start.4 = (bf16[64,384]{1,0:T(8,128)(2,1)S(1)}, bf16[64,384]{1,0:T(8,128)(2,1)S(1)}, u32[]{:S(2)}, u32[]{:S(2)}) collective-permute-start(bf16[64,384]{1,0:T(8,128)(2,1)S(1)} %get-tuple-element.24), channel_id=1, source_target_pairs={{0,8},{1,9},{2,10},{3,11},{4,12},{5,13},{6,14},{7,15},{8,0},{9,1},... | collective-permute-start | bytes 147464 | tf_op jit(solution)/shard_map/ppermute | solution.py:162
  6.9 0.0 collective-permute-start.5
  6.9 0.9 %collective-permute-start = (bf16[64,768]{1,0:T(8,128)(2,1)S(1)}, bf16[64,768]{1,0:T(8,128)(2,1)S(1)}, u32[]{:S(2)}, u32[]{:S(2)}) collective-permute-start(bf16[64,768]{1,0:T(8,128)(2,1)S(1)} %get-tuple-element.19), channel_id=1, source_target_pairs={{0,4},{1,5},{2,6},{3,7},{4,0},{5,1},{6,2},{7,3},{8,12},{9,13},{10,... | collective-permute-start | bytes 294920 | tf_op jit(solution)/shard_map/ppermute | solution.py:162
  7.8 3.5 %collective-permute-start.1 = (bf16[64,768]{1,0:T(8,128)(2,1)S(1)}, bf16[64,768]{1,0:T(8,128)(2,1)S(1)}, u32[]{:S(2)}, u32[]{:S(2)}) collective-permute-start(bf16[64,768]{1,0:T(8,128)(2,1)S(1)} %get-tuple-element.20), channel_id=1, source_target_pairs={{0,8},{1,9},{2,10},{3,11},{4,12},{5,13},{6,14},{7,15},{8,0},{9,1},... | collective-permute-start | bytes 294920 | tf_op jit(solution)/shard_map/ppermute | solution.py:162
  11.3 0.0 collective-permute-done.3
  11.3 0.1 collective-permute-start.2
  11.3 0.0 collective-permute-done.4
  11.4 2.1 %collective-permute-done.5 = bf16[64,384]{1,0:T(8,128)(2,1)S(1)} collective-permute-done((bf16[64,384]{1,0:T(8,128)(2,1)S(1)}, bf16[64,384]{1,0:T(8,128)(2,1)S(1)}, u32[]{:S(2)}, u32[]{:S(2)}) %collective-permute-start.5) | collective-permute-done | bytes 49184 | tf_op jit(solution)/shard_map/ppermute | solution.py:162
  13.5 1.6 %collective-permute-start.6 = (bf16[256,384]{1,0:T(8,128)(2,1)S(1)}, bf16[256,384]{1,0:T(8,128)(2,1)S(1)}, u32[]{:S(2)}, u32[]{:S(2)}) collective-permute-start(bf16[256,384]{1,0:T(8,128)(2,1)S(1)} %pad_maximum_fusion), channel_id=1, source_target_pairs={{0,2},{1,3},{2,0},{3,1},{4,6},{5,7},{6,4},{7,5},{8,10},{9,11},{10,... | collective-permute-start | bytes 589832 | tf_op jit(solution)/shard_map/ppermute | solution.py:162
  15.1 0.0 collective-permute-done.refs_1_
  15.1 0.6 %collective-permute-start.8 = (bf16[128,384]{1,0:T(8,128)(2,1)S(1)}, bf16[128,384]{1,0:T(8,128)(2,1)S(1)}, u32[]{:S(2)}, u32[]{:S(2)}) collective-permute-start(bf16[128,384]{1,0:T(8,128)(2,1)S(1)} %pad_maximum_fusion.2), channel_id=1, source_target_pairs={{0,2},{1,3},{2,0},{3,1},{4,6},{5,7},{6,4},{7,5},{8,10},{9,11},{10,... | collective-permute-start | bytes 294920 | tf_op jit(solution)/shard_map/ppermute | solution.py:162
  15.7 3.4 %collective-permute-done.1.refs_2_ = bf16[64,768]{1,0:T(8,128)(2,1)S(1)} collective-permute-done((bf16[64,768]{1,0:T(8,128)(2,1)S(1)}, bf16[64,768]{1,0:T(8,128)(2,1)S(1)}, u32[]{:S(2)}, u32[]{:S(2)}) %collective-permute-start.1) | collective-permute-done | bytes 98336 | tf_op jit(solution)/shard_map/ppermute | solution.py:162
  19.1 0.0 collective-permute-done.2.refs_3_
  19.2 1.6 %collective-permute-start.9 = (bf16[128,384]{1,0:T(8,128)(2,1)S(1)}, bf16[128,384]{1,0:T(8,128)(2,1)S(1)}, u32[]{:S(2)}, u32[]{:S(2)}) collective-permute-start(bf16[128,384]{1,0:T(8,128)(2,1)S(1)} %pad_maximum_fusion.3), channel_id=1, source_target_pairs={{0,2},{1,3},{2,0},{3,1},{4,6},{5,7},{6,4},{7,5},{8,10},{9,11},{10,... | collective-permute-start | bytes 294920 | tf_op jit(solution)/shard_map/ppermute | solution.py:162
  20.8 0.1 collective-permute-start.10
  20.8 0.0 collective-permute-done.6
  20.9 0.5 %collective-permute-start.7 = (bf16[512,384]{1,0:T(8,128)(2,1)S(1)}, bf16[512,384]{1,0:T(8,128)(2,1)S(1)}, u32[]{:S(2)}, u32[]{:S(2)}) collective-permute-start(bf16[512,384]{1,0:T(8,128)(2,1)S(1)} %constant_dynamic-update-slice_fusion.refs_4_), channel_id=1, source_target_pairs={{0,1},{1,0},{2,3},{3,2},{4,5},{5,4},{6,7},{7,6},{8,9},{9,8},{10,11... | collective-permute-start | bytes 1179656 | tf_op jit(solution)/shard_map/ppermute | solution.py:162
  21.4 0.0 collective-permute-done.8
  21.5 2.4 %collective-permute-done.9 = bf16[128,384]{1,0:T(8,128)(2,1)S(1)} collective-permute-done((bf16[128,384]{1,0:T(8,128)(2,1)S(1)}, bf16[128,384]{1,0:T(8,128)(2,1)S(1)}, u32[]{:S(2)}, u32[]{:S(2)}) %collective-permute-start.9) | collective-permute-done | bytes 98336 | tf_op jit(solution)/shard_map/ppermute | solution.py:162
  23.9 0.1 collective-permute-start.11
  23.9 0.0 collective-permute-done.7.refs_5_
  23.9 1.1 %weigh.1 = (bf16[3,256,1024]{2,1,0:T(8,128)(2,1)S(1)}, f32[256,128]{1,0:T(8,128)S(1)}) custom-call(bf16[64,768]{1,0:T(8,128)(2,1)S(1)} %get-tuple-element.18.refs_0_, bf16[64,768]{1,0:T(8,128)(2,1)S(1)} %collective-permute-done.refs_1_, bf16[64,768]{1,0:T(8,128)(2,1)S(1)} %collective-permute-done.1.refs_2_, ...), custom_call_target="tpu_custom_call" | custom-call | tf_op jit(solution)/shard_map/weigh/pallas_call | solution.py:90
  25.1 0.0 collective-permute-done.10.refs_2_
  25.1 0.3 collective-permute-done.11.refs_3_
  25.4 0.3 average.2.refs_4_
  25.6 0.5 %average.3 = (bf16[64,384]{1,0:T(8,128)(2,1)S(1)}, bf16[64,384]{1,0:T(8,128)(2,1)S(1)}, bf16[64,384]{1,0:T(8,128)(2,1)S(1)}) custom-call(bf16[3,256,1024]{2,1,0:T(8,128)(2,1)S(1)} %get-tuple-element.26.weights_ref, f32[256,128]{1,0:T(8,128)S(1)} %get-tuple-element.27.sums_ref, bf16[256,384]{1,0:T(8,128)(2,1)S(1)} %pad_maximum_fusion.1.refs_0_, ...), custom_call_target="tpu_custom_call" | custom-call | tf_op jit(solution)/shard_map/average/pallas_call | solution.py:119
  26.1 2.7 %collective-permute-start.13 = (bf16[64,384]{1,0:T(8,128)(2,1)S(1)}, bf16[64,384]{1,0:T(8,128)(2,1)S(1)}, u32[]{:S(2)}, u32[]{:S(2)}) collective-permute-start(bf16[64,384]{1,0:T(8,128)(2,1)S(1)} %get-tuple-element.28), channel_id=1, source_target_pairs={{0,20},{1,21},{2,22},{3,23},{4,16},{5,17},{6,18},{7,19},{8,28},{9,... | collective-permute-start | bytes 147464 | tf_op jit(solution)/shard_map/ppermute | solution.py:208
  28.8 0.8 %collective-permute-start.14 = (bf16[64,384]{1,0:T(8,128)(2,1)S(1)}, bf16[64,384]{1,0:T(8,128)(2,1)S(1)}, u32[]{:S(2)}, u32[]{:S(2)}) collective-permute-start(bf16[64,384]{1,0:T(8,128)(2,1)S(1)} %get-tuple-element.29), channel_id=1, source_target_pairs={{0,24},{1,25},{2,26},{3,27},{4,28},{5,29},{6,30},{7,31},{8,16},{9,... | collective-permute-start | bytes 147464 | tf_op jit(solution)/shard_map/ppermute | solution.py:208
  29.7 2.7 %collective-permute-start.15 = (bf16[64,384]{1,0:T(8,128)(2,1)S(1)}, bf16[64,384]{1,0:T(8,128)(2,1)S(1)}, u32[]{:S(2)}, u32[]{:S(2)}) collective-permute-start(bf16[64,384]{1,0:T(8,128)(2,1)S(1)} %get-tuple-element.30), channel_id=1, source_target_pairs={{0,28},{1,29},{2,30},{3,31},{4,24},{5,25},{6,26},{7,27},{8,20},{9,... | collective-permute-start | bytes 147464 | tf_op jit(solution)/shard_map/ppermute | solution.py:208
  32.4 0.5 %collective-permute-start.12 = (bf16[64,384]{1,0:T(8,128)(2,1)S(1)}, bf16[64,384]{1,0:T(8,128)(2,1)S(1)}, u32[]{:S(2)}, u32[]{:S(2)}) collective-permute-start(bf16[64,384]{1,0:T(8,128)(2,1)S(1)} %average.2.refs_4_), channel_id=1, source_target_pairs={{0,16},{1,17},{2,18},{3,19},{4,20},{5,21},{6,22},{7,23},{8,24},{9,... | collective-permute-start | bytes 147464 | tf_op jit(solution)/shard_map/ppermute | solution.py:208
  32.9 0.0 collective-permute-done.13.refs_1_
  32.9 3.1 %collective-permute-done.14.refs_2_ = bf16[64,384]{1,0:T(8,128)(2,1)S(1)} collective-permute-done((bf16[64,384]{1,0:T(8,128)(2,1)S(1)}, bf16[64,384]{1,0:T(8,128)(2,1)S(1)}, u32[]{:S(2)}, u32[]{:S(2)}) %collective-permute-start.14) | collective-permute-done | bytes 49184 | tf_op jit(solution)/shard_map/ppermute | solution.py:208
  36.0 0.6 %collective-permute-done.15.refs_3_ = bf16[64,384]{1,0:T(8,128)(2,1)S(1)} collective-permute-done((bf16[64,384]{1,0:T(8,128)(2,1)S(1)}, bf16[64,384]{1,0:T(8,128)(2,1)S(1)}, u32[]{:S(2)}, u32[]{:S(2)}) %collective-permute-start.15) | collective-permute-done | bytes 49184 | tf_op jit(solution)/shard_map/ppermute | solution.py:208
  36.6 0.5 %collective-permute-done.12.refs_0_ = bf16[64,384]{1,0:T(8,128)(2,1)S(1)} collective-permute-done((bf16[64,384]{1,0:T(8,128)(2,1)S(1)}, bf16[64,384]{1,0:T(8,128)(2,1)S(1)}, u32[]{:S(2)}, u32[]{:S(2)}) %collective-permute-start.12) | collective-permute-done | bytes 49184 | tf_op jit(solution)/shard_map/ppermute | solution.py:208
  37.1 0.7 %join_heads.1 = bf16[1,64,1536]{2,1,0:T(8,128)(2,1)} custom-call(bf16[64,384]{1,0:T(8,128)(2,1)S(1)} %collective-permute-done.12.refs_0_, bf16[64,384]{1,0:T(8,128)(2,1)S(1)} %collective-permute-done.13.refs_1_, bf16[64,384]{1,0:T(8,128)(2,1)S(1)} %collective-permute-done.14.refs_2_, bf16[64,384]{1,0:T(8,128)(2,1)S(1)} %collective-permute-done.15.refs_3_), custom_call_target="tpu_custom_call" | custom-call | tf_op jit(solution)/shard_map/join_heads/pallas_call | solution.py:143
  (15 shorter events, 0.2 us)
Async XLA Ops:
  1.2 10.1 %collective-permute-start.3 = (bf16[64,384]{1,0:T(8,128)(2,1)S(1)}, bf16[64,384]{1,0:T(8,128)(2,1)S(1)}, u32[]{:S(2)}, u32[]{:S(2)}) collective-permute-start(bf16[64,384]{1,0:T(8,128)(2,1)S(1)} %get-tuple-element.23), channel_id=1, source_target_pairs={{0,4},{1,5},{2,6},{3,7},{4,0},{5,1},{6,2},{7,3},{8,12},{9,13},{10,... | collective-permute-start | bytes 147464 | tf_op jit(solution)/shard_map/ppermute | solution.py:162
  4.3 7.1 %collective-permute-start.4 = (bf16[64,384]{1,0:T(8,128)(2,1)S(1)}, bf16[64,384]{1,0:T(8,128)(2,1)S(1)}, u32[]{:S(2)}, u32[]{:S(2)}) collective-permute-start(bf16[64,384]{1,0:T(8,128)(2,1)S(1)} %get-tuple-element.24), channel_id=1, source_target_pairs={{0,8},{1,9},{2,10},{3,11},{4,12},{5,13},{6,14},{7,15},{8,0},{9,1},... | collective-permute-start | bytes 147464 | tf_op jit(solution)/shard_map/ppermute | solution.py:162
  6.9 6.6 %collective-permute-start.5 = (bf16[64,384]{1,0:T(8,128)(2,1)S(1)}, bf16[64,384]{1,0:T(8,128)(2,1)S(1)}, u32[]{:S(2)}, u32[]{:S(2)}) collective-permute-start(bf16[64,384]{1,0:T(8,128)(2,1)S(1)} %get-tuple-element.25), channel_id=1, source_target_pairs={{0,12},{1,13},{2,14},{3,15},{4,8},{5,9},{6,10},{7,11},{8,4},{9,5},... | collective-permute-start | bytes 147464 | tf_op jit(solution)/shard_map/ppermute | solution.py:162
  6.9 8.2 %collective-permute-start = (bf16[64,768]{1,0:T(8,128)(2,1)S(1)}, bf16[64,768]{1,0:T(8,128)(2,1)S(1)}, u32[]{:S(2)}, u32[]{:S(2)}) collective-permute-start(bf16[64,768]{1,0:T(8,128)(2,1)S(1)} %get-tuple-element.19), channel_id=1, source_target_pairs={{0,4},{1,5},{2,6},{3,7},{4,0},{5,1},{6,2},{7,3},{8,12},{9,13},{10,... | collective-permute-start | bytes 294920 | tf_op jit(solution)/shard_map/ppermute | solution.py:162
  7.8 11.4 %collective-permute-start.1 = (bf16[64,768]{1,0:T(8,128)(2,1)S(1)}, bf16[64,768]{1,0:T(8,128)(2,1)S(1)}, u32[]{:S(2)}, u32[]{:S(2)}) collective-permute-start(bf16[64,768]{1,0:T(8,128)(2,1)S(1)} %get-tuple-element.20), channel_id=1, source_target_pairs={{0,8},{1,9},{2,10},{3,11},{4,12},{5,13},{6,14},{7,15},{8,0},{9,1},... | collective-permute-start | bytes 294920 | tf_op jit(solution)/shard_map/ppermute | solution.py:162
  11.3 7.8 %collective-permute-start.2 = (bf16[64,768]{1,0:T(8,128)(2,1)S(1)}, bf16[64,768]{1,0:T(8,128)(2,1)S(1)}, u32[]{:S(2)}, u32[]{:S(2)}) collective-permute-start(bf16[64,768]{1,0:T(8,128)(2,1)S(1)} %get-tuple-element.21), channel_id=1, source_target_pairs={{0,12},{1,13},{2,14},{3,15},{4,8},{5,9},{6,10},{7,11},{8,4},{9,5},... | collective-permute-start | bytes 294920 | tf_op jit(solution)/shard_map/ppermute | solution.py:162
  13.5 7.4 %collective-permute-start.6 = (bf16[256,384]{1,0:T(8,128)(2,1)S(1)}, bf16[256,384]{1,0:T(8,128)(2,1)S(1)}, u32[]{:S(2)}, u32[]{:S(2)}) collective-permute-start(bf16[256,384]{1,0:T(8,128)(2,1)S(1)} %pad_maximum_fusion), channel_id=1, source_target_pairs={{0,2},{1,3},{2,0},{3,1},{4,6},{5,7},{6,4},{7,5},{8,10},{9,11},{10,... | collective-permute-start | bytes 589832 | tf_op jit(solution)/shard_map/ppermute | solution.py:162
  15.1 6.3 %collective-permute-start.8 = (bf16[128,384]{1,0:T(8,128)(2,1)S(1)}, bf16[128,384]{1,0:T(8,128)(2,1)S(1)}, u32[]{:S(2)}, u32[]{:S(2)}) collective-permute-start(bf16[128,384]{1,0:T(8,128)(2,1)S(1)} %pad_maximum_fusion.2), channel_id=1, source_target_pairs={{0,2},{1,3},{2,0},{3,1},{4,6},{5,7},{6,4},{7,5},{8,10},{9,11},{10,... | collective-permute-start | bytes 294920 | tf_op jit(solution)/shard_map/ppermute | solution.py:162
  19.2 4.7 %collective-permute-start.9 = (bf16[128,384]{1,0:T(8,128)(2,1)S(1)}, bf16[128,384]{1,0:T(8,128)(2,1)S(1)}, u32[]{:S(2)}, u32[]{:S(2)}) collective-permute-start(bf16[128,384]{1,0:T(8,128)(2,1)S(1)} %pad_maximum_fusion.3), channel_id=1, source_target_pairs={{0,2},{1,3},{2,0},{3,1},{4,6},{5,7},{6,4},{7,5},{8,10},{9,11},{10,... | collective-permute-start | bytes 294920 | tf_op jit(solution)/shard_map/ppermute | solution.py:162
  20.8 4.3 %collective-permute-start.10 = (bf16[256,384]{1,0:T(8,128)(2,1)S(1)}, bf16[256,384]{1,0:T(8,128)(2,1)S(1)}, u32[]{:S(2)}, u32[]{:S(2)}) collective-permute-start(bf16[256,384]{1,0:T(8,128)(2,1)S(1)} %pad_maximum_fusion.1.refs_0_), channel_id=1, source_target_pairs={{0,1},{1,0},{2,3},{3,2},{4,5},{5,4},{6,7},{7,6},{8,9},{9,8},{10,11... | collective-permute-start | bytes 589832 | tf_op jit(solution)/shard_map/ppermute | solution.py:162
  20.9 3.0 %collective-permute-start.7 = (bf16[512,384]{1,0:T(8,128)(2,1)S(1)}, bf16[512,384]{1,0:T(8,128)(2,1)S(1)}, u32[]{:S(2)}, u32[]{:S(2)}) collective-permute-start(bf16[512,384]{1,0:T(8,128)(2,1)S(1)} %constant_dynamic-update-slice_fusion.refs_4_), channel_id=1, source_target_pairs={{0,1},{1,0},{2,3},{3,2},{4,5},{5,4},{6,7},{7,6},{8,9},{9,8},{10,11... | collective-permute-start | bytes 1179656 | tf_op jit(solution)/shard_map/ppermute | solution.py:162
  23.9 1.5 %collective-permute-start.11 = (bf16[256,384]{1,0:T(8,128)(2,1)S(1)}, bf16[256,384]{1,0:T(8,128)(2,1)S(1)}, u32[]{:S(2)}, u32[]{:S(2)}) collective-permute-start(bf16[256,384]{1,0:T(8,128)(2,1)S(1)} %constant_dynamic-update-slice_fusion.5.refs_1_), channel_id=1, source_target_pairs={{0,1},{1,0},{2,3},{3,2},{4,5},{5,4},{6,7},{7,6},{8,9},{9,8},{10,11... | collective-permute-start | bytes 589832 | tf_op jit(solution)/shard_map/ppermute | solution.py:162
  26.1 6.8 %collective-permute-start.13 = (bf16[64,384]{1,0:T(8,128)(2,1)S(1)}, bf16[64,384]{1,0:T(8,128)(2,1)S(1)}, u32[]{:S(2)}, u32[]{:S(2)}) collective-permute-start(bf16[64,384]{1,0:T(8,128)(2,1)S(1)} %get-tuple-element.28), channel_id=1, source_target_pairs={{0,20},{1,21},{2,22},{3,23},{4,16},{5,17},{6,18},{7,19},{8,28},{9,... | collective-permute-start | bytes 147464 | tf_op jit(solution)/shard_map/ppermute | solution.py:208
  28.8 7.2 %collective-permute-start.14 = (bf16[64,384]{1,0:T(8,128)(2,1)S(1)}, bf16[64,384]{1,0:T(8,128)(2,1)S(1)}, u32[]{:S(2)}, u32[]{:S(2)}) collective-permute-start(bf16[64,384]{1,0:T(8,128)(2,1)S(1)} %get-tuple-element.29), channel_id=1, source_target_pairs={{0,24},{1,25},{2,26},{3,27},{4,28},{5,29},{6,30},{7,31},{8,16},{9,... | collective-permute-start | bytes 147464 | tf_op jit(solution)/shard_map/ppermute | solution.py:208
  29.7 6.9 %collective-permute-start.15 = (bf16[64,384]{1,0:T(8,128)(2,1)S(1)}, bf16[64,384]{1,0:T(8,128)(2,1)S(1)}, u32[]{:S(2)}, u32[]{:S(2)}) collective-permute-start(bf16[64,384]{1,0:T(8,128)(2,1)S(1)} %get-tuple-element.30), channel_id=1, source_target_pairs={{0,28},{1,29},{2,30},{3,31},{4,24},{5,25},{6,26},{7,27},{8,20},{9,... | collective-permute-start | bytes 147464 | tf_op jit(solution)/shard_map/ppermute | solution.py:208
  32.4 4.7 %collective-permute-start.12 = (bf16[64,384]{1,0:T(8,128)(2,1)S(1)}, bf16[64,384]{1,0:T(8,128)(2,1)S(1)}, u32[]{:S(2)}, u32[]{:S(2)}) collective-permute-start(bf16[64,384]{1,0:T(8,128)(2,1)S(1)} %average.2.refs_4_), channel_id=1, source_target_pairs={{0,16},{1,17},{2,18},{3,19},{4,20},{5,21},{6,22},{7,23},{8,24},{9,... | collective-permute-start | bytes 147464 | tf_op jit(solution)/shard_map/ppermute | solution.py:208

commit v5 on v4

--- a/solution.py
+++ b/solution.py
@@ -6,6 +6,7 @@
 from jax.sharding import PartitionSpec as P
 
 HD = 128
+LOG2_E = 1.4426950408889634
 HBM = pl.BlockSpec(memory_space=pltpu.HBM)
 VMEM = pl.BlockSpec(memory_space=pltpu.VMEM)
 PARAMS = pltpu.CompilerParams(vmem_limit_bytes=16 << 20)
@@ -82,8 +83,8 @@
             q = jnp.concatenate([ref[:, q_cols] for ref in query_refs], axis=0)
             k = jnp.concatenate([ref[:, cols] for ref in key_refs], axis=0)
             scores = lax.dot_general(q, k, contract, preferred_element_type=jnp.float32)
-            scores = scores * HD ** (-0.5)
-            weights = jnp.exp(scores - jnp.max(scores, axis=1, keepdims=True))
+            scores = scores * (HD ** (-0.5) * LOG2_E)
+            weights = jnp.exp2(scores - jnp.max(scores, axis=1, keepdims=True))
             sums_ref[:, head : head + 1] = jnp.sum(weights, axis=1, keepdims=True)
             weights_ref[head] = weights.astype(jnp.bfloat16)
 
@@ -178,12 +179,15 @@
     width = queries.shape[2] // groups
     first, second = split_heads(queries, key_value, groups, inner)
     first, second = exchange(first), exchange(second)
+
+    def near_and_far(pieces):
+        halves = (pieces[: groups // 2], pieces[groups // 2 :])
+        return [jnp.concatenate(some, axis=0) for some in halves if some]
+
     key_blocks = with_other_core(
-        [jnp.concatenate(gather([jnp.concatenate(first, axis=0)]), axis=0)]
-    )
-    values = [piece[:, :width] for piece in second]
-    near, far = values[: groups // 2], values[groups // 2 :]
-    parts = [jnp.concatenate(some, axis=0) for some in (near, far) if some]
+        [jnp.concatenate(gather(near_and_far(first)), axis=0)]
+    )
+    parts = near_and_far([piece[:, :width] for piece in second])
     blocks = gather(parts)
     count = len(parts)
     value_blocks = with_other_core(

time: 38 us -> 37.9 us (level)
  starting transfers between devices: 21.4 us -> 23.2 us
  waiting for transfers between devices: 12.3 us -> 10.6 us
    ppermute x12 -> x13, starting transfers between devices: 14.6 us -> 16.4 us  [swap(): return lax.ppermute(value, 'seq', [(i, i ^ bits) for i in range(places)])]
    ppermute x12 -> x13, waiting for transfers between devices: 8.13 us -> 6.44 us  [swap(): return lax.ppermute(value, 'seq', [(i, i ^ bits) for i in range(places)])]
  transfers between devices with their start and end apart: 16 -> 17, of which waited for: 7 -> 7; matrix products, arithmetic and copies ran while one was open for 1% -> 1% of each run, Pallas kernels for 3% -> 3%
where the time goes in v5:
time: 37.9 us; the launch traced here: 37.7 us
  starting transfers between devices  23.2 us (61%)
  waiting for transfers between devices  10.6 us (28%)
  Pallas kernels  3.62 us (10%)
    ppermute x13, starting transfers between devices, swap(): return lax.ppermute(value, 'seq', [(i, i ^ bits) for i in range(places)])  16.4 us
    ppermute x4, starting transfers between devices, hand(): return lax.ppermute(value, ('segment', 'seq'), pairs)  6.81 us
    ppermute x13, waiting for transfers between devices, swap(): return lax.ppermute(value, 'seq', [(i, i ^ bits) for i in range(places)])  6.44 us
    ppermute x4, waiting for transfers between devices, hand(): return lax.ppermute(value, ('segment', 'seq'), pairs)  4.13 us
    pallas_call x1, Pallas kernels, split_heads(): pl.pallas_call(kernel, out_shape=[jax.ShapeDtypeStruct((rows, width), que...  1.17 us
    pallas_call x1, Pallas kernels, weigh(): pl.pallas_call(kernel, out_shape=[jax.ShapeDtypeStruct((heads, groups * r...  1.03 us
  transfers between devices with their start and end apart: 17, of which 7 were waited for; matrix products, arithmetic and copies ran while one was open for 1% of the time, Pallas kernels for 3%

profile of v5, /device:TPU:0, one launch (start us, length us, event | category | flops | bytes accessed | tf_op | source)
XLA Modules:
  0.0 37.7 jit_solution(5106917919791164321)
XLA Ops:
  0.0 1.2 %split_heads.1 = (bf16[64,384]{1,0:T(8,128)(2,1)S(1)}, bf16[64,384]{1,0:T(8,128)(2,1)S(1)}, bf16[64,384]{1,0:T(8,128)(2,1)S(1)}, bf16[64,384]{1,0:T(8,128)(2,1)S...) custom-call(bf16[1,64,1536]{2,1,0:T(8,128)(2,1)} %q_ref.1, ...), custom_call_target="tpu_custom_call" | custom-call | tf_op jit(solution)/shard_map/split_heads/pallas_call | solution.py:54
  1.2 3.1 %collective-permute-start.3 = (bf16[64,384]{1,0:T(8,128)(2,1)S(1)}, bf16[64,384]{1,0:T(8,128)(2,1)S(1)}, u32[]{:S(2)}, u32[]{:S(2)}) collective-permute-start(bf16[64,384]{1,0:T(8,128)(2,1)S(1)} %get-tuple-element.23), channel_id=1, source_target_pairs={{0,4},{1,5},{2,6},{3,7},{4,0},{5,1},{6,2},{7,3},{8,12},{9,13},{10,... | collective-permute-start | bytes 147464 | tf_op jit(solution)/shard_map/ppermute | solution.py:163
  4.3 2.6 %collective-permute-start.4 = (bf16[64,384]{1,0:T(8,128)(2,1)S(1)}, bf16[64,384]{1,0:T(8,128)(2,1)S(1)}, u32[]{:S(2)}, u32[]{:S(2)}) collective-permute-start(bf16[64,384]{1,0:T(8,128)(2,1)S(1)} %get-tuple-element.24), channel_id=1, source_target_pairs={{0,8},{1,9},{2,10},{3,11},{4,12},{5,13},{6,14},{7,15},{8,0},{9,1},... | collective-permute-start | bytes 147464 | tf_op jit(solution)/shard_map/ppermute | solution.py:163
  6.9 0.0 collective-permute-start.5
  6.9 0.9 %collective-permute-start = (bf16[64,768]{1,0:T(8,128)(2,1)S(1)}, bf16[64,768]{1,0:T(8,128)(2,1)S(1)}, u32[]{:S(2)}, u32[]{:S(2)}) collective-permute-start(bf16[64,768]{1,0:T(8,128)(2,1)S(1)} %get-tuple-element.19), channel_id=1, source_target_pairs={{0,4},{1,5},{2,6},{3,7},{4,0},{5,1},{6,2},{7,3},{8,12},{9,13},{10,... | collective-permute-start | bytes 294920 | tf_op jit(solution)/shard_map/ppermute | solution.py:163
  7.8 3.5 %collective-permute-start.1 = (bf16[64,768]{1,0:T(8,128)(2,1)S(1)}, bf16[64,768]{1,0:T(8,128)(2,1)S(1)}, u32[]{:S(2)}, u32[]{:S(2)}) collective-permute-start(bf16[64,768]{1,0:T(8,128)(2,1)S(1)} %get-tuple-element.20), channel_id=1, source_target_pairs={{0,8},{1,9},{2,10},{3,11},{4,12},{5,13},{6,14},{7,15},{8,0},{9,1},... | collective-permute-start | bytes 294920 | tf_op jit(solution)/shard_map/ppermute | solution.py:163
  11.3 0.0 collective-permute-done.3
  11.3 0.1 collective-permute-start.2
  11.4 0.0 collective-permute-done.4
  11.4 1.8 %collective-permute-start.6 = (bf16[128,384]{1,0:T(8,128)(2,1)S(1)}, bf16[128,384]{1,0:T(8,128)(2,1)S(1)}, u32[]{:S(2)}, u32[]{:S(2)}) collective-permute-start(bf16[128,384]{1,0:T(8,128)(2,1)S(1)} %pad_maximum_fusion.1), channel_id=1, source_target_pairs={{0,2},{1,3},{2,0},{3,1},{4,6},{5,7},{6,4},{7,5},{8,10},{9,11},{10,... | collective-permute-start | bytes 294920 | tf_op jit(solution)/shard_map/ppermute | solution.py:163
  13.2 0.3 collective-permute-done.5
  13.5 1.6 %collective-permute-start.7 = (bf16[128,384]{1,0:T(8,128)(2,1)S(1)}, bf16[128,384]{1,0:T(8,128)(2,1)S(1)}, u32[]{:S(2)}, u32[]{:S(2)}) collective-permute-start(bf16[128,384]{1,0:T(8,128)(2,1)S(1)} %pad_maximum_fusion.2), channel_id=1, source_target_pairs={{0,2},{1,3},{2,0},{3,1},{4,6},{5,7},{6,4},{7,5},{8,10},{9,11},{10,... | collective-permute-start | bytes 294920 | tf_op jit(solution)/shard_map/ppermute | solution.py:163
  15.1 0.0 collective-permute-done.refs_1_
  15.1 0.6 %collective-permute-start.9 = (bf16[128,384]{1,0:T(8,128)(2,1)S(1)}, bf16[128,384]{1,0:T(8,128)(2,1)S(1)}, u32[]{:S(2)}, u32[]{:S(2)}) collective-permute-start(bf16[128,384]{1,0:T(8,128)(2,1)S(1)} %pad_maximum_fusion.3), channel_id=1, source_target_pairs={{0,2},{1,3},{2,0},{3,1},{4,6},{5,7},{6,4},{7,5},{8,10},{9,11},{10,... | collective-permute-start | bytes 294920 | tf_op jit(solution)/shard_map/ppermute | solution.py:163
  15.7 3.4 %collective-permute-done.1.refs_2_ = bf16[64,768]{1,0:T(8,128)(2,1)S(1)} collective-permute-done((bf16[64,768]{1,0:T(8,128)(2,1)S(1)}, bf16[64,768]{1,0:T(8,128)(2,1)S(1)}, u32[]{:S(2)}, u32[]{:S(2)}) %collective-permute-start.1) | collective-permute-done | bytes 98336 | tf_op jit(solution)/shard_map/ppermute | solution.py:163
  19.1 0.0 collective-permute-done.2.refs_3_
  19.2 1.6 %collective-permute-start.10 = (bf16[128,384]{1,0:T(8,128)(2,1)S(1)}, bf16[128,384]{1,0:T(8,128)(2,1)S(1)}, u32[]{:S(2)}, u32[]{:S(2)}) collective-permute-start(bf16[128,384]{1,0:T(8,128)(2,1)S(1)} %pad_maximum_fusion.4), channel_id=1, source_target_pairs={{0,2},{1,3},{2,0},{3,1},{4,6},{5,7},{6,4},{7,5},{8,10},{9,11},{10,... | collective-permute-start | bytes 294920 | tf_op jit(solution)/shard_map/ppermute | solution.py:163
  20.8 0.1 collective-permute-start.11
  20.8 0.0 collective-permute-done.6
  20.9 0.0 collective-permute-done.7
  20.9 0.5 %collective-permute-start.8 = (bf16[512,384]{1,0:T(8,128)(2,1)S(1)}, bf16[512,384]{1,0:T(8,128)(2,1)S(1)}, u32[]{:S(2)}, u32[]{:S(2)}) collective-permute-start(bf16[512,384]{1,0:T(8,128)(2,1)S(1)} %constant_dynamic-update-slice_fusion.refs_4_), channel_id=1, source_target_pairs={{0,1},{1,0},{2,3},{3,2},{4,5},{5,4},{6,7},{7,6},{8,9},{9,8},{10,11... | collective-permute-start | bytes 1179656 | tf_op jit(solution)/shard_map/ppermute | solution.py:163
  21.5 0.0 collective-permute-done.9
  21.5 2.4 %collective-permute-done.10 = bf16[128,384]{1,0:T(8,128)(2,1)S(1)} collective-permute-done((bf16[128,384]{1,0:T(8,128)(2,1)S(1)}, bf16[128,384]{1,0:T(8,128)(2,1)S(1)}, u32[]{:S(2)}, u32[]{:S(2)}) %collective-permute-start.10) | collective-permute-done | bytes 98336 | tf_op jit(solution)/shard_map/ppermute | solution.py:163
  23.9 0.1 collective-permute-start.12
  23.9 0.0 collective-permute-done.8.refs_5_
  23.9 1.0 %weigh.1 = (bf16[3,256,1024]{2,1,0:T(8,128)(2,1)S(1)}, f32[256,128]{1,0:T(8,128)S(1)}) custom-call(bf16[64,768]{1,0:T(8,128)(2,1)S(1)} %get-tuple-element.18.refs_0_, bf16[64,768]{1,0:T(8,128)(2,1)S(1)} %collective-permute-done.refs_1_, bf16[64,768]{1,0:T(8,128)(2,1)S(1)} %collective-permute-done.1.refs_2_, ...), custom_call_target="tpu_custom_call" | custom-call | tf_op jit(solution)/shard_map/weigh/pallas_call | solution.py:91
  25.0 0.0 collective-permute-done.11.refs_2_
  25.0 0.4 %collective-permute-done.12.refs_3_ = bf16[256,384]{1,0:T(8,128)(2,1)S(1)} collective-permute-done((bf16[256,384]{1,0:T(8,128)(2,1)S(1)}, bf16[256,384]{1,0:T(8,128)(2,1)S(1)}, u32[]{:S(2)}, u32[]{:S(2)}) %collective-permute-start.12) | collective-permute-done | bytes 196640 | tf_op jit(solution)/shard_map/ppermute | solution.py:163
  25.4 0.3 average.2.refs_4_
  25.6 0.5 %average.3 = (bf16[64,384]{1,0:T(8,128)(2,1)S(1)}, bf16[64,384]{1,0:T(8,128)(2,1)S(1)}, bf16[64,384]{1,0:T(8,128)(2,1)S(1)}) custom-call(bf16[3,256,1024]{2,1,0:T(8,128)(2,1)S(1)} %get-tuple-element.26.weights_ref, f32[256,128]{1,0:T(8,128)S(1)} %get-tuple-element.27.sums_ref, bf16[256,384]{1,0:T(8,128)(2,1)S(1)} %pad_maximum_fusion.refs_0_, ...), custom_call_target="tpu_custom_call" | custom-call | tf_op jit(solution)/shard_map/average/pallas_call | solution.py:120
  26.1 2.7 %collective-permute-start.14 = (bf16[64,384]{1,0:T(8,128)(2,1)S(1)}, bf16[64,384]{1,0:T(8,128)(2,1)S(1)}, u32[]{:S(2)}, u32[]{:S(2)}) collective-permute-start(bf16[64,384]{1,0:T(8,128)(2,1)S(1)} %get-tuple-element.28), channel_id=1, source_target_pairs={{0,20},{1,21},{2,22},{3,23},{4,16},{5,17},{6,18},{7,19},{8,28},{9,... | collective-permute-start | bytes 147464 | tf_op jit(solution)/shard_map/ppermute | solution.py:212
  28.8 0.8 %collective-permute-start.15 = (bf16[64,384]{1,0:T(8,128)(2,1)S(1)}, bf16[64,384]{1,0:T(8,128)(2,1)S(1)}, u32[]{:S(2)}, u32[]{:S(2)}) collective-permute-start(bf16[64,384]{1,0:T(8,128)(2,1)S(1)} %get-tuple-element.29), channel_id=1, source_target_pairs={{0,24},{1,25},{2,26},{3,27},{4,28},{5,29},{6,30},{7,31},{8,16},{9,... | collective-permute-start | bytes 147464 | tf_op jit(solution)/shard_map/ppermute | solution.py:212
  29.7 2.7 %collective-permute-start.16 = (bf16[64,384]{1,0:T(8,128)(2,1)S(1)}, bf16[64,384]{1,0:T(8,128)(2,1)S(1)}, u32[]{:S(2)}, u32[]{:S(2)}) collective-permute-start(bf16[64,384]{1,0:T(8,128)(2,1)S(1)} %get-tuple-element.30), channel_id=1, source_target_pairs={{0,28},{1,29},{2,30},{3,31},{4,24},{5,25},{6,26},{7,27},{8,20},{9,... | collective-permute-start | bytes 147464 | tf_op jit(solution)/shard_map/ppermute | solution.py:212
  32.4 0.5 %collective-permute-start.13 = (bf16[64,384]{1,0:T(8,128)(2,1)S(1)}, bf16[64,384]{1,0:T(8,128)(2,1)S(1)}, u32[]{:S(2)}, u32[]{:S(2)}) collective-permute-start(bf16[64,384]{1,0:T(8,128)(2,1)S(1)} %average.2.refs_4_), channel_id=1, source_target_pairs={{0,16},{1,17},{2,18},{3,19},{4,20},{5,21},{6,22},{7,23},{8,24},{9,... | collective-permute-start | bytes 147464 | tf_op jit(solution)/shard_map/ppermute | solution.py:212
  32.9 0.0 collective-permute-done.14.refs_1_
  32.9 3.1 %collective-permute-done.15.refs_2_ = bf16[64,384]{1,0:T(8,128)(2,1)S(1)} collective-permute-done((bf16[64,384]{1,0:T(8,128)(2,1)S(1)}, bf16[64,384]{1,0:T(8,128)(2,1)S(1)}, u32[]{:S(2)}, u32[]{:S(2)}) %collective-permute-start.15) | collective-permute-done | bytes 49184 | tf_op jit(solution)/shard_map/ppermute | solution.py:212
  36.0 0.6 %collective-permute-done.16.refs_3_ = bf16[64,384]{1,0:T(8,128)(2,1)S(1)} collective-permute-done((bf16[64,384]{1,0:T(8,128)(2,1)S(1)}, bf16[64,384]{1,0:T(8,128)(2,1)S(1)}, u32[]{:S(2)}, u32[]{:S(2)}) %collective-permute-start.16) | collective-permute-done | bytes 49184 | tf_op jit(solution)/shard_map/ppermute | solution.py:212
  36.6 0.4 %collective-permute-done.13.refs_0_ = bf16[64,384]{1,0:T(8,128)(2,1)S(1)} collective-permute-done((bf16[64,384]{1,0:T(8,128)(2,1)S(1)}, bf16[64,384]{1,0:T(8,128)(2,1)S(1)}, u32[]{:S(2)}, u32[]{:S(2)}) %collective-permute-start.13) | collective-permute-done | bytes 49184 | tf_op jit(solution)/shard_map/ppermute | solution.py:212
  37.0 0.7 %join_heads.1 = bf16[1,64,1536]{2,1,0:T(8,128)(2,1)} custom-call(bf16[64,384]{1,0:T(8,128)(2,1)S(1)} %collective-permute-done.13.refs_0_, bf16[64,384]{1,0:T(8,128)(2,1)S(1)} %collective-permute-done.14.refs_1_, bf16[64,384]{1,0:T(8,128)(2,1)S(1)} %collective-permute-done.15.refs_2_, bf16[64,384]{1,0:T(8,128)(2,1)S(1)} %collective-permute-done.16.refs_3_), custom_call_target="tpu_custom_call" | custom-call | tf_op jit(solution)/shard_map/join_heads/pallas_call | solution.py:144
  (17 shorter events, 0.2 us)
Async XLA Ops:
  1.2 10.1 %collective-permute-start.3 = (bf16[64,384]{1,0:T(8,128)(2,1)S(1)}, bf16[64,384]{1,0:T(8,128)(2,1)S(1)}, u32[]{:S(2)}, u32[]{:S(2)}) collective-permute-start(bf16[64,384]{1,0:T(8,128)(2,1)S(1)} %get-tuple-element.23), channel_id=1, source_target_pairs={{0,4},{1,5},{2,6},{3,7},{4,0},{5,1},{6,2},{7,3},{8,12},{9,13},{10,... | collective-permute-start | bytes 147464 | tf_op jit(solution)/shard_map/ppermute | solution.py:163
  4.3 7.1 %collective-permute-start.4 = (bf16[64,384]{1,0:T(8,128)(2,1)S(1)}, bf16[64,384]{1,0:T(8,128)(2,1)S(1)}, u32[]{:S(2)}, u32[]{:S(2)}) collective-permute-start(bf16[64,384]{1,0:T(8,128)(2,1)S(1)} %get-tuple-element.24), channel_id=1, source_target_pairs={{0,8},{1,9},{2,10},{3,11},{4,12},{5,13},{6,14},{7,15},{8,0},{9,1},... | collective-permute-start | bytes 147464 | tf_op jit(solution)/shard_map/ppermute | solution.py:163
  6.9 6.6 %collective-permute-start.5 = (bf16[64,384]{1,0:T(8,128)(2,1)S(1)}, bf16[64,384]{1,0:T(8,128)(2,1)S(1)}, u32[]{:S(2)}, u32[]{:S(2)}) collective-permute-start(bf16[64,384]{1,0:T(8,128)(2,1)S(1)} %get-tuple-element.25), channel_id=1, source_target_pairs={{0,12},{1,13},{2,14},{3,15},{4,8},{5,9},{6,10},{7,11},{8,4},{9,5},... | collective-permute-start | bytes 147464 | tf_op jit(solution)/shard_map/ppermute | solution.py:163
  6.9 8.2 %collective-permute-start = (bf16[64,768]{1,0:T(8,128)(2,1)S(1)}, bf16[64,768]{1,0:T(8,128)(2,1)S(1)}, u32[]{:S(2)}, u32[]{:S(2)}) collective-permute-start(bf16[64,768]{1,0:T(8,128)(2,1)S(1)} %get-tuple-element.19), channel_id=1, source_target_pairs={{0,4},{1,5},{2,6},{3,7},{4,0},{5,1},{6,2},{7,3},{8,12},{9,13},{10,... | collective-permute-start | bytes 294920 | tf_op jit(solution)/shard_map/ppermute | solution.py:163
  7.8 11.4 %collective-permute-start.1 = (bf16[64,768]{1,0:T(8,128)(2,1)S(1)}, bf16[64,768]{1,0:T(8,128)(2,1)S(1)}, u32[]{:S(2)}, u32[]{:S(2)}) collective-permute-start(bf16[64,768]{1,0:T(8,128)(2,1)S(1)} %get-tuple-element.20), channel_id=1, source_target_pairs={{0,8},{1,9},{2,10},{3,11},{4,12},{5,13},{6,14},{7,15},{8,0},{9,1},... | collective-permute-start | bytes 294920 | tf_op jit(solution)/shard_map/ppermute | solution.py:163
  11.3 7.8 %collective-permute-start.2 = (bf16[64,768]{1,0:T(8,128)(2,1)S(1)}, bf16[64,768]{1,0:T(8,128)(2,1)S(1)}, u32[]{:S(2)}, u32[]{:S(2)}) collective-permute-start(bf16[64,768]{1,0:T(8,128)(2,1)S(1)} %get-tuple-element.21), channel_id=1, source_target_pairs={{0,12},{1,13},{2,14},{3,15},{4,8},{5,9},{6,10},{7,11},{8,4},{9,5},... | collective-permute-start | bytes 294920 | tf_op jit(solution)/shard_map/ppermute | solution.py:163
  11.4 9.5 %collective-permute-start.6 = (bf16[128,384]{1,0:T(8,128)(2,1)S(1)}, bf16[128,384]{1,0:T(8,128)(2,1)S(1)}, u32[]{:S(2)}, u32[]{:S(2)}) collective-permute-start(bf16[128,384]{1,0:T(8,128)(2,1)S(1)} %pad_maximum_fusion.1), channel_id=1, source_target_pairs={{0,2},{1,3},{2,0},{3,1},{4,6},{5,7},{6,4},{7,5},{8,10},{9,11},{10,... | collective-permute-start | bytes 294920 | tf_op jit(solution)/shard_map/ppermute | solution.py:163
  13.5 7.4 %collective-permute-start.7 = (bf16[128,384]{1,0:T(8,128)(2,1)S(1)}, bf16[128,384]{1,0:T(8,128)(2,1)S(1)}, u32[]{:S(2)}, u32[]{:S(2)}) collective-permute-start(bf16[128,384]{1,0:T(8,128)(2,1)S(1)} %pad_maximum_fusion.2), channel_id=1, source_target_pairs={{0,2},{1,3},{2,0},{3,1},{4,6},{5,7},{6,4},{7,5},{8,10},{9,11},{10,... | collective-permute-start | bytes 294920 | tf_op jit(solution)/shard_map/ppermute | solution.py:163
  15.1 6.3 %collective-permute-start.9 = (bf16[128,384]{1,0:T(8,128)(2,1)S(1)}, bf16[128,384]{1,0:T(8,128)(2,1)S(1)}, u32[]{:S(2)}, u32[]{:S(2)}) collective-permute-start(bf16[128,384]{1,0:T(8,128)(2,1)S(1)} %pad_maximum_fusion.3), channel_id=1, source_target_pairs={{0,2},{1,3},{2,0},{3,1},{4,6},{5,7},{6,4},{7,5},{8,10},{9,11},{10,... | collective-permute-start | bytes 294920 | tf_op jit(solution)/shard_map/ppermute | solution.py:163
  19.2 4.7 %collective-permute-start.10 = (bf16[128,384]{1,0:T(8,128)(2,1)S(1)}, bf16[128,384]{1,0:T(8,128)(2,1)S(1)}, u32[]{:S(2)}, u32[]{:S(2)}) collective-permute-start(bf16[128,384]{1,0:T(8,128)(2,1)S(1)} %pad_maximum_fusion.4), channel_id=1, source_target_pairs={{0,2},{1,3},{2,0},{3,1},{4,6},{5,7},{6,4},{7,5},{8,10},{9,11},{10,... | collective-permute-start | bytes 294920 | tf_op jit(solution)/shard_map/ppermute | solution.py:163
  20.8 4.2 %collective-permute-start.11 = (bf16[256,384]{1,0:T(8,128)(2,1)S(1)}, bf16[256,384]{1,0:T(8,128)(2,1)S(1)}, u32[]{:S(2)}, u32[]{:S(2)}) collective-permute-start(bf16[256,384]{1,0:T(8,128)(2,1)S(1)} %pad_maximum_fusion.refs_0_), channel_id=1, source_target_pairs={{0,1},{1,0},{2,3},{3,2},{4,5},{5,4},{6,7},{7,6},{8,9},{9,8},{10,11... | collective-permute-start | bytes 589832 | tf_op jit(solution)/shard_map/ppermute | solution.py:163
  20.9 3.0 %collective-permute-start.8 = (bf16[512,384]{1,0:T(8,128)(2,1)S(1)}, bf16[512,384]{1,0:T(8,128)(2,1)S(1)}, u32[]{:S(2)}, u32[]{:S(2)}) collective-permute-start(bf16[512,384]{1,0:T(8,128)(2,1)S(1)} %constant_dynamic-update-slice_fusion.refs_4_), channel_id=1, source_target_pairs={{0,1},{1,0},{2,3},{3,2},{4,5},{5,4},{6,7},{7,6},{8,9},{9,8},{10,11... | collective-permute-start | bytes 1179656 | tf_op jit(solution)/shard_map/ppermute | solution.py:163
  23.9 1.5 %collective-permute-start.12 = (bf16[256,384]{1,0:T(8,128)(2,1)S(1)}, bf16[256,384]{1,0:T(8,128)(2,1)S(1)}, u32[]{:S(2)}, u32[]{:S(2)}) collective-permute-start(bf16[256,384]{1,0:T(8,128)(2,1)S(1)} %constant_dynamic-update-slice_fusion.6.refs_1_), channel_id=1, source_target_pairs={{0,1},{1,0},{2,3},{3,2},{4,5},{5,4},{6,7},{7,6},{8,9},{9,8},{10,11... | collective-permute-start | bytes 589832 | tf_op jit(solution)/shard_map/ppermute | solution.py:163
  26.1 6.8 %collective-permute-start.14 = (bf16[64,384]{1,0:T(8,128)(2,1)S(1)}, bf16[64,384]{1,0:T(8,128)(2,1)S(1)}, u32[]{:S(2)}, u32[]{:S(2)}) collective-permute-start(bf16[64,384]{1,0:T(8,128)(2,1)S(1)} %get-tuple-element.28), channel_id=1, source_target_pairs={{0,20},{1,21},{2,22},{3,23},{4,16},{5,17},{6,18},{7,19},{8,28},{9,... | collective-permute-start | bytes 147464 | tf_op jit(solution)/shard_map/ppermute | solution.py:212
  28.8 7.2 %collective-permute-start.15 = (bf16[64,384]{1,0:T(8,128)(2,1)S(1)}, bf16[64,384]{1,0:T(8,128)(2,1)S(1)}, u32[]{:S(2)}, u32[]{:S(2)}) collective-permute-start(bf16[64,384]{1,0:T(8,128)(2,1)S(1)} %get-tuple-element.29), channel_id=1, source_target_pairs={{0,24},{1,25},{2,26},{3,27},{4,28},{5,29},{6,30},{7,31},{8,16},{9,... | collective-permute-start | bytes 147464 | tf_op jit(solution)/shard_map/ppermute | solution.py:212
  29.7 6.9 %collective-permute-start.16 = (bf16[64,384]{1,0:T(8,128)(2,1)S(1)}, bf16[64,384]{1,0:T(8,128)(2,1)S(1)}, u32[]{:S(2)}, u32[]{:S(2)}) collective-permute-start(bf16[64,384]{1,0:T(8,128)(2,1)S(1)} %get-tuple-element.30), channel_id=1, source_target_pairs={{0,28},{1,29},{2,30},{3,31},{4,24},{5,25},{6,26},{7,27},{8,20},{9,... | collective-permute-start | bytes 147464 | tf_op jit(solution)/shard_map/ppermute | solution.py:212
  32.4 4.7 %collective-permute-start.13 = (bf16[64,384]{1,0:T(8,128)(2,1)S(1)}, bf16[64,384]{1,0:T(8,128)(2,1)S(1)}, u32[]{:S(2)}, u32[]{:S(2)}) collective-permute-start(bf16[64,384]{1,0:T(8,128)(2,1)S(1)} %average.2.refs_4_), channel_id=1, source_target_pairs={{0,16},{1,17},{2,18},{3,19},{4,20},{5,21},{6,22},{7,23},{8,24},{9,... | collective-permute-start | bytes 147464 | tf_op jit(solution)/shard_map/ppermute | solution.py:212

commit v6 on v5

--- a/solution.py
+++ b/solution.py
@@ -198,7 +198,9 @@
     )
     weights, sums = weigh(second, key_blocks, width)
     own = average(weights, sums, value_blocks, groups, 0, 1, [])
-    attended = own + average(weights, sums, value_blocks, groups, 1, groups, own)
+    near_by = average(weights, sums, value_blocks, groups, 1, groups // 2, own)
+    rest = average(weights, sums, value_blocks, groups, groups // 2, groups, near_by)
+    attended = own + near_by + rest
 
     def hand(value, step):
         pairs = [

time: 37.9 us -> 37.9 us (level)
    pallas_call x2 -> x3, Pallas kernels: 0.73 us -> 0.88 us  [average(): pl.pallas_call(kernel, out_shape=[jax.ShapeDtypeStruct((rows, heads * HD)...]
where the time goes in v6:
time: 37.9 us; the launch traced here: 37.7 us
  starting transfers between devices  22.9 us (60%)
  waiting for transfers between devices  10.6 us (28%)
  Pallas kernels  3.78 us (10%)
    ppermute x13, starting transfers between devices, swap(): return lax.ppermute(value, 'seq', [(i, i ^ bits) for i in range(places)])  16.4 us
    ppermute x4, starting transfers between devices, hand(): return lax.ppermute(value, ('segment', 'seq'), pairs)  6.56 us
    ppermute x13, waiting for transfers between devices, swap(): return lax.ppermute(value, 'seq', [(i, i ^ bits) for i in range(places)])  6.44 us
    ppermute x4, waiting for transfers between devices, hand(): return lax.ppermute(value, ('segment', 'seq'), pairs)  4.21 us
    pallas_call x1, Pallas kernels, split_heads(): pl.pallas_call(kernel, out_shape=[jax.ShapeDtypeStruct((rows, width), que...  1.17 us
    pallas_call x1, Pallas kernels, weigh(): pl.pallas_call(kernel, out_shape=[jax.ShapeDtypeStruct((heads, groups * r...  1.03 us
    pallas_call x3, Pallas kernels, average(): pl.pallas_call(kernel, out_shape=[jax.ShapeDtypeStruct((rows, heads * HD)...  0.88 us
  transfers between devices with their start and end apart: 17, of which 7 were waited for; matrix products, arithmetic and copies ran while one was open for 1% of the time, Pallas kernels for 3%

profile of v6, /device:TPU:0, one launch (start us, length us, event | category | flops | bytes accessed | tf_op | source)
XLA Modules:
  0.0 37.7 jit_solution(16902004198421496385)
XLA Ops:
  0.0 1.2 %split_heads.1 = (bf16[64,384]{1,0:T(8,128)(2,1)S(1)}, bf16[64,384]{1,0:T(8,128)(2,1)S(1)}, bf16[64,384]{1,0:T(8,128)(2,1)S(1)}, bf16[64,384]{1,0:T(8,128)(2,1)S...) custom-call(bf16[1,64,1536]{2,1,0:T(8,128)(2,1)} %q_ref.1, ...), custom_call_target="tpu_custom_call" | custom-call | tf_op jit(solution)/shard_map/split_heads/pallas_call | solution.py:54
  1.2 3.1 %collective-permute-start.3 = (bf16[64,384]{1,0:T(8,128)(2,1)S(1)}, bf16[64,384]{1,0:T(8,128)(2,1)S(1)}, u32[]{:S(2)}, u32[]{:S(2)}) collective-permute-start(bf16[64,384]{1,0:T(8,128)(2,1)S(1)} %get-tuple-element.22), channel_id=1, source_target_pairs={{0,4},{1,5},{2,6},{3,7},{4,0},{5,1},{6,2},{7,3},{8,12},{9,13},{10,... | collective-permute-start | bytes 147464 | tf_op jit(solution)/shard_map/ppermute | solution.py:163
  4.3 2.6 %collective-permute-start.4 = (bf16[64,384]{1,0:T(8,128)(2,1)S(1)}, bf16[64,384]{1,0:T(8,128)(2,1)S(1)}, u32[]{:S(2)}, u32[]{:S(2)}) collective-permute-start(bf16[64,384]{1,0:T(8,128)(2,1)S(1)} %get-tuple-element.23), channel_id=1, source_target_pairs={{0,8},{1,9},{2,10},{3,11},{4,12},{5,13},{6,14},{7,15},{8,0},{9,1},... | collective-permute-start | bytes 147464 | tf_op jit(solution)/shard_map/ppermute | solution.py:163
  6.9 0.0 collective-permute-start.5
  6.9 0.9 %collective-permute-start = (bf16[64,768]{1,0:T(8,128)(2,1)S(1)}, bf16[64,768]{1,0:T(8,128)(2,1)S(1)}, u32[]{:S(2)}, u32[]{:S(2)}) collective-permute-start(bf16[64,768]{1,0:T(8,128)(2,1)S(1)} %get-tuple-element.18), channel_id=1, source_target_pairs={{0,4},{1,5},{2,6},{3,7},{4,0},{5,1},{6,2},{7,3},{8,12},{9,13},{10,... | collective-permute-start | bytes 294920 | tf_op jit(solution)/shard_map/ppermute | solution.py:163
  7.8 3.5 %collective-permute-start.1 = (bf16[64,768]{1,0:T(8,128)(2,1)S(1)}, bf16[64,768]{1,0:T(8,128)(2,1)S(1)}, u32[]{:S(2)}, u32[]{:S(2)}) collective-permute-start(bf16[64,768]{1,0:T(8,128)(2,1)S(1)} %get-tuple-element.19), channel_id=1, source_target_pairs={{0,8},{1,9},{2,10},{3,11},{4,12},{5,13},{6,14},{7,15},{8,0},{9,1},... | collective-permute-start | bytes 294920 | tf_op jit(solution)/shard_map/ppermute | solution.py:163
  11.3 0.0 collective-permute-done.3
  11.3 0.1 collective-permute-start.2
  11.4 0.0 collective-permute-done.4
  11.4 1.8 %collective-permute-start.6 = (bf16[128,384]{1,0:T(8,128)(2,1)S(1)}, bf16[128,384]{1,0:T(8,128)(2,1)S(1)}, u32[]{:S(2)}, u32[]{:S(2)}) collective-permute-start(bf16[128,384]{1,0:T(8,128)(2,1)S(1)} %pad_maximum_fusion.1), channel_id=1, source_target_pairs={{0,2},{1,3},{2,0},{3,1},{4,6},{5,7},{6,4},{7,5},{8,10},{9,11},{10,... | collective-permute-start | bytes 294920 | tf_op jit(solution)/shard_map/ppermute | solution.py:163
  13.2 0.3 collective-permute-done.5
  13.5 1.6 %collective-permute-start.7 = (bf16[128,384]{1,0:T(8,128)(2,1)S(1)}, bf16[128,384]{1,0:T(8,128)(2,1)S(1)}, u32[]{:S(2)}, u32[]{:S(2)}) collective-permute-start(bf16[128,384]{1,0:T(8,128)(2,1)S(1)} %pad_maximum_fusion.2), channel_id=1, source_target_pairs={{0,2},{1,3},{2,0},{3,1},{4,6},{5,7},{6,4},{7,5},{8,10},{9,11},{10,... | collective-permute-start | bytes 294920 | tf_op jit(solution)/shard_map/ppermute | solution.py:163
  15.1 0.0 collective-permute-done.refs_1_
  15.1 0.6 %collective-permute-start.9 = (bf16[128,384]{1,0:T(8,128)(2,1)S(1)}, bf16[128,384]{1,0:T(8,128)(2,1)S(1)}, u32[]{:S(2)}, u32[]{:S(2)}) collective-permute-start(bf16[128,384]{1,0:T(8,128)(2,1)S(1)} %pad_maximum_fusion.3), channel_id=1, source_target_pairs={{0,2},{1,3},{2,0},{3,1},{4,6},{5,7},{6,4},{7,5},{8,10},{9,11},{10,... | collective-permute-start | bytes 294920 | tf_op jit(solution)/shard_map/ppermute | solution.py:163
  15.7 3.4 %collective-permute-done.1.refs_2_ = bf16[64,768]{1,0:T(8,128)(2,1)S(1)} collective-permute-done((bf16[64,768]{1,0:T(8,128)(2,1)S(1)}, bf16[64,768]{1,0:T(8,128)(2,1)S(1)}, u32[]{:S(2)}, u32[]{:S(2)}) %collective-permute-start.1) | collective-permute-done | bytes 98336 | tf_op jit(solution)/shard_map/ppermute | solution.py:163
  19.1 0.0 collective-permute-done.2.refs_3_
  19.2 1.6 %collective-permute-start.10 = (bf16[128,384]{1,0:T(8,128)(2,1)S(1)}, bf16[128,384]{1,0:T(8,128)(2,1)S(1)}, u32[]{:S(2)}, u32[]{:S(2)}) collective-permute-start(bf16[128,384]{1,0:T(8,128)(2,1)S(1)} %pad_maximum_fusion.4), channel_id=1, source_target_pairs={{0,2},{1,3},{2,0},{3,1},{4,6},{5,7},{6,4},{7,5},{8,10},{9,11},{10,... | collective-permute-start | bytes 294920 | tf_op jit(solution)/shard_map/ppermute | solution.py:163
  20.8 0.1 collective-permute-start.11
  20.8 0.0 collective-permute-done.6
  20.9 0.0 collective-permute-done.7
  20.9 0.5 %collective-permute-start.8 = (bf16[512,384]{1,0:T(8,128)(2,1)S(1)}, bf16[512,384]{1,0:T(8,128)(2,1)S(1)}, u32[]{:S(2)}, u32[]{:S(2)}) collective-permute-start(bf16[512,384]{1,0:T(8,128)(2,1)S(1)} %constant_dynamic-update-slice_fusion.refs_4_), channel_id=1, source_target_pairs={{0,1},{1,0},{2,3},{3,2},{4,5},{5,4},{6,7},{7,6},{8,9},{9,8},{10,11... | collective-permute-start | bytes 1179656 | tf_op jit(solution)/shard_map/ppermute | solution.py:163
  21.5 0.0 collective-permute-done.9
  21.5 2.4 %collective-permute-done.10 = bf16[128,384]{1,0:T(8,128)(2,1)S(1)} collective-permute-done((bf16[128,384]{1,0:T(8,128)(2,1)S(1)}, bf16[128,384]{1,0:T(8,128)(2,1)S(1)}, u32[]{:S(2)}, u32[]{:S(2)}) %collective-permute-start.10) | collective-permute-done | bytes 98336 | tf_op jit(solution)/shard_map/ppermute | solution.py:163
  23.9 0.1 collective-permute-start.12
  23.9 0.0 collective-permute-done.8.refs_5_
  23.9 1.0 %weigh.1 = (bf16[3,256,1024]{2,1,0:T(8,128)(2,1)S(1)}, f32[256,128]{1,0:T(8,128)S(1)}) custom-call(bf16[64,768]{1,0:T(8,128)(2,1)S(1)} %get-tuple-element.17.refs_0_, bf16[64,768]{1,0:T(8,128)(2,1)S(1)} %collective-permute-done.refs_1_, bf16[64,768]{1,0:T(8,128)(2,1)S(1)} %collective-permute-done.1.refs_2_, ...), custom_call_target="tpu_custom_call" | custom-call | tf_op jit(solution)/shard_map/weigh/pallas_call | solution.py:91
  25.0 0.0 collective-permute-done.11.refs_2_
  25.0 0.4 %collective-permute-done.12.refs_3_ = bf16[256,384]{1,0:T(8,128)(2,1)S(1)} collective-permute-done((bf16[256,384]{1,0:T(8,128)(2,1)S(1)}, bf16[256,384]{1,0:T(8,128)(2,1)S(1)}, u32[]{:S(2)}, u32[]{:S(2)}) %collective-permute-start.12) | collective-permute-done | bytes 196640 | tf_op jit(solution)/shard_map/ppermute | solution.py:163
  25.4 0.3 average.3.refs_4_
  25.6 0.3 average.4.refs_4_
  25.9 0.4 average.5
  26.3 3.4 %collective-permute-start.15 = (bf16[64,384]{1,0:T(8,128)(2,1)S(1)}, bf16[64,384]{1,0:T(8,128)(2,1)S(1)}, u32[]{:S(2)}, u32[]{:S(2)}) collective-permute-start(bf16[64,384]{1,0:T(8,128)(2,1)S(1)} %get-tuple-element.27), channel_id=1, source_target_pairs={{0,24},{1,25},{2,26},{3,27},{4,28},{5,29},{6,30},{7,31},{8,16},{9,... | collective-permute-start | bytes 147464 | tf_op jit(solution)/shard_map/ppermute | solution.py:214
  29.7 1.7 %collective-permute-start.16 = (bf16[64,384]{1,0:T(8,128)(2,1)S(1)}, bf16[64,384]{1,0:T(8,128)(2,1)S(1)}, u32[]{:S(2)}, u32[]{:S(2)}) collective-permute-start(bf16[64,384]{1,0:T(8,128)(2,1)S(1)} %get-tuple-element.28), channel_id=1, source_target_pairs={{0,28},{1,29},{2,30},{3,31},{4,24},{5,25},{6,26},{7,27},{8,20},{9,... | collective-permute-start | bytes 147464 | tf_op jit(solution)/shard_map/ppermute | solution.py:214
  31.3 0.3 collective-permute-start.14
  31.6 1.2 %collective-permute-start.13 = (bf16[64,384]{1,0:T(8,128)(2,1)S(1)}, bf16[64,384]{1,0:T(8,128)(2,1)S(1)}, u32[]{:S(2)}, u32[]{:S(2)}) collective-permute-start(bf16[64,384]{1,0:T(8,128)(2,1)S(1)} %average.3.refs_4_), channel_id=1, source_target_pairs={{0,16},{1,17},{2,18},{3,19},{4,20},{5,21},{6,22},{7,23},{8,24},{9,... | collective-permute-start | bytes 147464 | tf_op jit(solution)/shard_map/ppermute | solution.py:214
  32.8 0.0 collective-permute-done.15.refs_2_
  32.8 3.8 %collective-permute-done.16.refs_3_ = bf16[64,384]{1,0:T(8,128)(2,1)S(1)} collective-permute-done((bf16[64,384]{1,0:T(8,128)(2,1)S(1)}, bf16[64,384]{1,0:T(8,128)(2,1)S(1)}, u32[]{:S(2)}, u32[]{:S(2)}) %collective-permute-start.16) | collective-permute-done | bytes 49184 | tf_op jit(solution)/shard_map/ppermute | solution.py:214
  36.6 0.3 collective-permute-done.14.refs_1_
  36.9 0.1 collective-permute-done.13.refs_0_
  37.0 0.7 %join_heads.1 = bf16[1,64,1536]{2,1,0:T(8,128)(2,1)} custom-call(bf16[64,384]{1,0:T(8,128)(2,1)S(1)} %collective-permute-done.13.refs_0_, bf16[64,384]{1,0:T(8,128)(2,1)S(1)} %collective-permute-done.14.refs_1_, bf16[64,384]{1,0:T(8,128)(2,1)S(1)} %collective-permute-done.15.refs_2_, bf16[64,384]{1,0:T(8,128)(2,1)S(1)} %collective-permute-done.16.refs_3_), custom_call_target="tpu_custom_call" | custom-call | tf_op jit(solution)/shard_map/join_heads/pallas_call | solution.py:144
  (17 shorter events, 0.2 us)
Async XLA Ops:
  1.2 10.1 %collective-permute-start.3 = (bf16[64,384]{1,0:T(8,128)(2,1)S(1)}, bf16[64,384]{1,0:T(8,128)(2,1)S(1)}, u32[]{:S(2)}, u32[]{:S(2)}) collective-permute-start(bf16[64,384]{1,0:T(8,128)(2,1)S(1)} %get-tuple-element.22), channel_id=1, source_target_pairs={{0,4},{1,5},{2,6},{3,7},{4,0},{5,1},{6,2},{7,3},{8,12},{9,13},{10,... | collective-permute-start | bytes 147464 | tf_op jit(solution)/shard_map/ppermute | solution.py:163
  4.3 7.1 %collective-permute-start.4 = (bf16[64,384]{1,0:T(8,128)(2,1)S(1)}, bf16[64,384]{1,0:T(8,128)(2,1)S(1)}, u32[]{:S(2)}, u32[]{:S(2)}) collective-permute-start(bf16[64,384]{1,0:T(8,128)(2,1)S(1)} %get-tuple-element.23), channel_id=1, source_target_pairs={{0,8},{1,9},{2,10},{3,11},{4,12},{5,13},{6,14},{7,15},{8,0},{9,1},... | collective-permute-start | bytes 147464 | tf_op jit(solution)/shard_map/ppermute | solution.py:163
  6.9 6.6 %collective-permute-start.5 = (bf16[64,384]{1,0:T(8,128)(2,1)S(1)}, bf16[64,384]{1,0:T(8,128)(2,1)S(1)}, u32[]{:S(2)}, u32[]{:S(2)}) collective-permute-start(bf16[64,384]{1,0:T(8,128)(2,1)S(1)} %get-tuple-element.24), channel_id=1, source_target_pairs={{0,12},{1,13},{2,14},{3,15},{4,8},{5,9},{6,10},{7,11},{8,4},{9,5},... | collective-permute-start | bytes 147464 | tf_op jit(solution)/shard_map/ppermute | solution.py:163
  6.9 8.2 %collective-permute-start = (bf16[64,768]{1,0:T(8,128)(2,1)S(1)}, bf16[64,768]{1,0:T(8,128)(2,1)S(1)}, u32[]{:S(2)}, u32[]{:S(2)}) collective-permute-start(bf16[64,768]{1,0:T(8,128)(2,1)S(1)} %get-tuple-element.18), channel_id=1, source_target_pairs={{0,4},{1,5},{2,6},{3,7},{4,0},{5,1},{6,2},{7,3},{8,12},{9,13},{10,... | collective-permute-start | bytes 294920 | tf_op jit(solution)/shard_map/ppermute | solution.py:163
  7.8 11.4 %collective-permute-start.1 = (bf16[64,768]{1,0:T(8,128)(2,1)S(1)}, bf16[64,768]{1,0:T(8,128)(2,1)S(1)}, u32[]{:S(2)}, u32[]{:S(2)}) collective-permute-start(bf16[64,768]{1,0:T(8,128)(2,1)S(1)} %get-tuple-element.19), channel_id=1, source_target_pairs={{0,8},{1,9},{2,10},{3,11},{4,12},{5,13},{6,14},{7,15},{8,0},{9,1},... | collective-permute-start | bytes 294920 | tf_op jit(solution)/shard_map/ppermute | solution.py:163
  11.3 7.8 %collective-permute-start.2 = (bf16[64,768]{1,0:T(8,128)(2,1)S(1)}, bf16[64,768]{1,0:T(8,128)(2,1)S(1)}, u32[]{:S(2)}, u32[]{:S(2)}) collective-permute-start(bf16[64,768]{1,0:T(8,128)(2,1)S(1)} %get-tuple-element.20), channel_id=1, source_target_pairs={{0,12},{1,13},{2,14},{3,15},{4,8},{5,9},{6,10},{7,11},{8,4},{9,5},... | collective-permute-start | bytes 294920 | tf_op jit(solution)/shard_map/ppermute | solution.py:163
  11.4 9.5 %collective-permute-start.6 = (bf16[128,384]{1,0:T(8,128)(2,1)S(1)}, bf16[128,384]{1,0:T(8,128)(2,1)S(1)}, u32[]{:S(2)}, u32[]{:S(2)}) collective-permute-start(bf16[128,384]{1,0:T(8,128)(2,1)S(1)} %pad_maximum_fusion.1), channel_id=1, source_target_pairs={{0,2},{1,3},{2,0},{3,1},{4,6},{5,7},{6,4},{7,5},{8,10},{9,11},{10,... | collective-permute-start | bytes 294920 | tf_op jit(solution)/shard_map/ppermute | solution.py:163
  13.5 7.4 %collective-permute-start.7 = (bf16[128,384]{1,0:T(8,128)(2,1)S(1)}, bf16[128,384]{1,0:T(8,128)(2,1)S(1)}, u32[]{:S(2)}, u32[]{:S(2)}) collective-permute-start(bf16[128,384]{1,0:T(8,128)(2,1)S(1)} %pad_maximum_fusion.2), channel_id=1, source_target_pairs={{0,2},{1,3},{2,0},{3,1},{4,6},{5,7},{6,4},{7,5},{8,10},{9,11},{10,... | collective-permute-start | bytes 294920 | tf_op jit(solution)/shard_map/ppermute | solution.py:163
  15.1 6.3 %collective-permute-start.9 = (bf16[128,384]{1,0:T(8,128)(2,1)S(1)}, bf16[128,384]{1,0:T(8,128)(2,1)S(1)}, u32[]{:S(2)}, u32[]{:S(2)}) collective-permute-start(bf16[128,384]{1,0:T(8,128)(2,1)S(1)} %pad_maximum_fusion.3), channel_id=1, source_target_pairs={{0,2},{1,3},{2,0},{3,1},{4,6},{5,7},{6,4},{7,5},{8,10},{9,11},{10,... | collective-permute-start | bytes 294920 | tf_op jit(solution)/shard_map/ppermute | solution.py:163
  19.2 4.7 %collective-permute-start.10 = (bf16[128,384]{1,0:T(8,128)(2,1)S(1)}, bf16[128,384]{1,0:T(8,128)(2,1)S(1)}, u32[]{:S(2)}, u32[]{:S(2)}) collective-permute-start(bf16[128,384]{1,0:T(8,128)(2,1)S(1)} %pad_maximum_fusion.4), channel_id=1, source_target_pairs={{0,2},{1,3},{2,0},{3,1},{4,6},{5,7},{6,4},{7,5},{8,10},{9,11},{10,... | collective-permute-start | bytes 294920 | tf_op jit(solution)/shard_map/ppermute | solution.py:163
  20.8 4.2 %collective-permute-start.11 = (bf16[256,384]{1,0:T(8,128)(2,1)S(1)}, bf16[256,384]{1,0:T(8,128)(2,1)S(1)}, u32[]{:S(2)}, u32[]{:S(2)}) collective-permute-start(bf16[256,384]{1,0:T(8,128)(2,1)S(1)} %pad_maximum_fusion.refs_0_), channel_id=1, source_target_pairs={{0,1},{1,0},{2,3},{3,2},{4,5},{5,4},{6,7},{7,6},{8,9},{9,8},{10,11... | collective-permute-start | bytes 589832 | tf_op jit(solution)/shard_map/ppermute | solution.py:163
  20.9 3.0 %collective-permute-start.8 = (bf16[512,384]{1,0:T(8,128)(2,1)S(1)}, bf16[512,384]{1,0:T(8,128)(2,1)S(1)}, u32[]{:S(2)}, u32[]{:S(2)}) collective-permute-start(bf16[512,384]{1,0:T(8,128)(2,1)S(1)} %constant_dynamic-update-slice_fusion.refs_4_), channel_id=1, source_target_pairs={{0,1},{1,0},{2,3},{3,2},{4,5},{5,4},{6,7},{7,6},{8,9},{9,8},{10,11... | collective-permute-start | bytes 1179656 | tf_op jit(solution)/shard_map/ppermute | solution.py:163
  23.9 1.5 %collective-permute-start.12 = (bf16[256,384]{1,0:T(8,128)(2,1)S(1)}, bf16[256,384]{1,0:T(8,128)(2,1)S(1)}, u32[]{:S(2)}, u32[]{:S(2)}) collective-permute-start(bf16[256,384]{1,0:T(8,128)(2,1)S(1)} %constant_dynamic-update-slice_fusion.6.refs_1_), channel_id=1, source_target_pairs={{0,1},{1,0},{2,3},{3,2},{4,5},{5,4},{6,7},{7,6},{8,9},{9,8},{10,11... | collective-permute-start | bytes 589832 | tf_op jit(solution)/shard_map/ppermute | solution.py:163
  26.3 6.6 %collective-permute-start.15 = (bf16[64,384]{1,0:T(8,128)(2,1)S(1)}, bf16[64,384]{1,0:T(8,128)(2,1)S(1)}, u32[]{:S(2)}, u32[]{:S(2)}) collective-permute-start(bf16[64,384]{1,0:T(8,128)(2,1)S(1)} %get-tuple-element.27), channel_id=1, source_target_pairs={{0,24},{1,25},{2,26},{3,27},{4,28},{5,29},{6,30},{7,31},{8,16},{9,... | collective-permute-start | bytes 147464 | tf_op jit(solution)/shard_map/ppermute | solution.py:214
  29.7 6.9 %collective-permute-start.16 = (bf16[64,384]{1,0:T(8,128)(2,1)S(1)}, bf16[64,384]{1,0:T(8,128)(2,1)S(1)}, u32[]{:S(2)}, u32[]{:S(2)}) collective-permute-start(bf16[64,384]{1,0:T(8,128)(2,1)S(1)} %get-tuple-element.28), channel_id=1, source_target_pairs={{0,28},{1,29},{2,30},{3,31},{4,24},{5,25},{6,26},{7,27},{8,20},{9,... | collective-permute-start | bytes 147464 | tf_op jit(solution)/shard_map/ppermute | solution.py:214
  31.3 5.6 %collective-permute-start.14 = (bf16[64,384]{1,0:T(8,128)(2,1)S(1)}, bf16[64,384]{1,0:T(8,128)(2,1)S(1)}, u32[]{:S(2)}, u32[]{:S(2)}) collective-permute-start(bf16[64,384]{1,0:T(8,128)(2,1)S(1)} %average.4.refs_4_), channel_id=1, source_target_pairs={{0,20},{1,21},{2,22},{3,23},{4,16},{5,17},{6,18},{7,19},{8,28},{9,... | collective-permute-start | bytes 147464 | tf_op jit(solution)/shard_map/ppermute | solution.py:214
  31.6 5.4 %collective-permute-start.13 = (bf16[64,384]{1,0:T(8,128)(2,1)S(1)}, bf16[64,384]{1,0:T(8,128)(2,1)S(1)}, u32[]{:S(2)}, u32[]{:S(2)}) collective-permute-start(bf16[64,384]{1,0:T(8,128)(2,1)S(1)} %average.3.refs_4_), channel_id=1, source_target_pairs={{0,16},{1,17},{2,18},{3,19},{4,20},{5,21},{6,22},{7,23},{8,24},{9,... | collective-permute-start | bytes 147464 | tf_op jit(solution)/shard_map/ppermute | solution.py:214
